TPU v7x, 32 devices: a whole 2x2x4 slice. The times are simulated.
32 devices in a mesh: dp: 4 (over y, core), seq: 8 (over z, x).
Axes of the slice: x: 2, y: 2, z: 4, core: 2. Of those that a mesh axis runs over, the one named last changes fastest.
Arguments:
- tokens: bfloat16 [8192, 1024], P(('dp', 'seq')), may hold values from -6 to 6
- lengths: int32 [4, 4], P('dp'), may hold values from 1 to 1024, 2048 in all within a row
- cotangent: bfloat16 [8192, 1024], P(('dp', 'seq')), may hold values from -6 to 6
- mixer_gain: bfloat16 [1024], P(('dp', 'seq')), may hold values from 0.5 to 1.5
- query_weight: bfloat16 [1024, 512], P(('dp', 'seq')), may hold values from -0.1875 to 0.1875
- keyval_weight: bfloat16 [1024, 256], P(('dp', 'seq')), may hold values from -0.1875 to 0.1875
- inner_weight: bfloat16 [1024, 3352], P(('dp', 'seq')), may hold values from -0.1875 to 0.1875
- conv_weight: bfloat16 [1792, 4], P(('dp', 'seq')), may hold values from -3 to 3
- conv_bias: bfloat16 [1792], P(('dp', 'seq')), may hold values from -1.5 to 1.5
- ssm_gain: bfloat16 [1536], P(('dp', 'seq')), may hold values from 0.5 to 1.5
- attn_out_weight: bfloat16 [512, 1024], P(('dp', 'seq')), may hold values from -2 to 2
- ssm_out_weight: bfloat16 [1536, 1024], P(('dp', 'seq')), may hold values from -0.15625 to 0.15625
- ffn_gain: bfloat16 [1024], P(('dp', 'seq')), may hold values from 0.5 to 1.5
- gate_up_weight: bfloat16 [1024, 4096], P(('dp', 'seq')), may hold values from -0.1875 to 0.1875
- down_weight: bfloat16 [2048, 1024], P(('dp', 'seq')), may hold values from -0.125 to 0.125
- decay_log: float32 [24], replicated, may hold values from -6 to 0
- step_bias: float32 [24], replicated, may hold values from -4 to -1
- skip_gain: float32 [24], replicated, may hold values from 0.5 to 1.5
Outputs:
- output: bfloat16 [8192, 1024], P(('dp', 'seq'))
- tokens_grad: float32 [8192, 1024], P(('dp', 'seq'))
- mixer_gain_grad: float32 [1024], P(('dp', 'seq'))
- query_weight_grad: float32 [1024, 512], P(('dp', 'seq'))
- keyval_weight_grad: float32 [1024, 256], P(('dp', 'seq'))
- inner_weight_grad: float32 [1024, 3352], P(('dp', 'seq'))
- conv_weight_grad: float32 [1792, 4], P(('dp', 'seq'))
- conv_bias_grad: float32 [1792], P(('dp', 'seq'))
- ssm_gain_grad: float32 [1536], P(('dp', 'seq'))
- attn_out_grad: float32 [512, 1024], P(('dp', 'seq'))
- ssm_out_grad: float32 [1536, 1024], P(('dp', 'seq'))
- ffn_gain_grad: float32 [1024], P(('dp', 'seq'))
- gate_up_grad: float32 [1024, 4096], P(('dp', 'seq'))
- down_grad: float32 [2048, 1024], P(('dp', 'seq'))
- decay_log_grad: float32 [24], replicated
- step_bias_grad: float32 [24], replicated
- skip_gain_grad: float32 [24], replicated
Inputs may be any that keep to these rules, and one draw needn't show every extreme that they name: Each row holds one data group's 4 sequence lengths in stream order; a row sums to 2048 and its largest entry is exactly 1024.
All inputs are finite; a program needn't handle non-finite values.
Results may differ from a plain program's by a relative error of at most 0.014.
Values may be sent and summed in bfloat16 or wider, within the bound.
No kernel may reach another device: no remote copies, remote signals or barrier semaphores. Data moves between devices by JAX's collectives and lax.ppermute only.
A program may use at most 256 MiB of HBM per device.

v0:
```python
import functools

import jax
import jax.numpy as jnp
from jax import lax
from jax.sharding import PartitionSpec as P

HEADS = 8
KV_HEADS = 2
HEAD_DIM = 64
SSM_HEADS = 24
SSM_DIM = 64
STATE = 128
CONV = 4
DS = 1536
CONV_CH = 1792
IN_COLS = 3352


eps_norm = 1e-06
rope_base = 10000.0


def passed_along(array, axis, by):
    length = lax.axis_size(axis)
    pairs = [(i, i + by) for i in range(length) if 0 <= i + by < length]
    return lax.ppermute(array, axis, pairs)


def entering_2(array, axis, join, neutral, backward):
    count = lax.axis_size(axis)
    place = lax.axis_index(axis)
    ahead = count - 1 - place if backward else place
    gathered = jax.tree.map(
        lambda a, kind: lax.all_gather(a.astype(kind), axis),
        array,
        jax.tree.map(lambda a: jnp.bfloat16 if a.dtype == jnp.float32 else a.dtype, array),
    )
    state = jax.tree.map(lambda a, e: jnp.zeros_like(a) + jnp.asarray(e, a.dtype), array, neutral)

    def one(step, state):
        source = count - 1 - step if backward else step
        return join(
            state,
            jax.tree.map(
                lambda a, own: lax.dynamic_index_in_dim(a, source, 0, False).astype(own.dtype),
                gathered,
                array,
            ),
        )

    return lax.fori_loop(0, ahead, one, state)


def for_sending(array):
    return jax.tree.map(lambda a: a.astype(jnp.bfloat16) if a.dtype == jnp.float32 else a, array)


def narrow_value(value):
    narrow = lax.optimization_barrier(value.astype(jnp.bfloat16))
    return narrow.astype(jnp.float32)


def narrow_keep(value):
    return (narrow_value(value), None)


def narrow_pass(kept, grad):
    return (grad,)


def round_value(value):
    rounder = jax.custom_vjp(narrow_value)
    rounder.defvjp(narrow_keep, narrow_pass)
    return rounder(value)


def plain_value(value):
    return value


def plain_keep(value):
    return (value, None)


def plain_round(kept, grad):
    return (narrow_value(grad),)


def round_grad(value):
    passer = jax.custom_vjp(plain_value)
    passer.defvjp(plain_keep, plain_round)
    return passer(value)


def narrow_product(left, right):
    return jnp.dot(
        left.astype(jnp.bfloat16), right.astype(jnp.bfloat16), preferred_element_type=jnp.float32
    )


def product_keep(left, right):
    return (narrow_product(left, right), (left, right))


def product_back(kept, grad):
    left, right = kept
    narrow = grad.astype(jnp.bfloat16)
    grad_left = jnp.dot(narrow, right.astype(jnp.bfloat16).T, preferred_element_type=jnp.float32)
    grad_right = jnp.dot(left.astype(jnp.bfloat16).T, narrow, preferred_element_type=jnp.float32)
    return (grad_left, grad_right)


def bfloat_dot(left, right):
    multiply = jax.custom_vjp(narrow_product)
    multiply.defvjp(product_keep, product_back)
    return multiply(left, right)


def seq_layout(places, seq_lengths):
    ends = jnp.cumsum(seq_lengths)
    before = (ends[None, :] <= places[:, None]).astype(jnp.int32)
    segments = jnp.sum(before, axis=1)
    offset = places - jnp.sum(before * seq_lengths[None, :], axis=1)
    return (segments, offset)


def rotate(values, offset):
    half = values.shape[-1] // 2
    freq = rope_base ** (-jnp.arange(half).astype(jnp.float32) / half)
    angle = offset.astype(jnp.float32)[:, None] * freq[None, :]
    cosine = jnp.cos(angle)[:, None, :]
    sine = jnp.sin(angle)[:, None, :]
    first_half = values[..., :half]
    second_half = values[..., half:]
    return jnp.concatenate(
        [first_half * cosine - second_half * sine, second_half * cosine + first_half * sine],
        axis=-1,
    )


def attend_block(product, query, query_place, query_seg, keys, values, key_place, key_seg):
    raw = round_grad(product(query, keys.T))
    scores = raw * query.shape[-1] ** (-0.5)
    allowed = (key_seg[None, :] == query_seg[:, None]) & (
        key_place[None, :] <= query_place[:, None]
    )
    scores = jnp.where(allowed, scores, -1e30)
    total = jax.nn.logsumexp(scores, axis=1, keepdims=True)
    weights = round_value(jnp.exp(scores - total))
    return product(weights, values)


def attention(product, queries, keyvals, query_place, query_seg, key_place, key_seg, block):
    rows = queries.shape[0]
    per_head = queries.reshape(rows // block, block, HEADS, HEAD_DIM).transpose(2, 0, 1, 3)
    pairs = keyvals.reshape(-1, 2, KV_HEADS, HEAD_DIM)
    keys_all = pairs[:, 0].transpose(1, 0, 2)
    values_all = pairs[:, 1].transpose(1, 0, 2)
    owner = jnp.arange(HEADS) // (HEADS // KV_HEADS)
    place_blocks = query_place.reshape(-1, block)
    seg_blocks = query_seg.reshape(-1, block)
    step_fn = jax.checkpoint(functools.partial(attend_block, product))

    def one_head(item):
        head_queries, which = item
        keys = keys_all[which]
        values = values_all[which]

        def one_block(part):
            return step_fn(part[0], part[1], part[2], keys, values, key_place, key_seg)

        return lax.map(one_block, (head_queries, place_blocks, seg_blocks))

    outputs = lax.map(one_head, (per_head, owner))
    merged = outputs.transpose(1, 2, 0, 3).reshape(rows, HEADS * HEAD_DIM)
    return round_value(round_grad(merged))


def front(product, stream, gain_one, w_query, w_keyval, w_inner, offset):
    rows = stream.shape[0]
    normed = round_value(
        stream
        * lax.rsqrt(jnp.mean(stream * stream, axis=1, keepdims=True) + eps_norm)
        * gain_one[None, :]
    )
    queries = round_grad(product(normed, w_query))
    keyvals = round_grad(product(normed, w_keyval))
    inner = round_value(round_grad(product(normed, w_inner)))
    queries = round_value(
        rotate(queries.reshape(rows, HEADS, HEAD_DIM), offset).reshape(rows, HEADS * HEAD_DIM)
    )
    pairs = keyvals.reshape(rows, 2, KV_HEADS, HEAD_DIM)
    keys = rotate(pairs[:, 0], offset)
    keyvals = round_value(
        jnp.stack([keys, pairs[:, 1]], axis=1).reshape(rows, 2 * KV_HEADS * HEAD_DIM)
    )
    return (queries, keyvals, inner)


def mixer_inputs(inner, rim, w_conv, b_conv, step_bias, decay_log, ext_seg, own_seg):
    rows = inner.shape[0]
    channels = inner[:, DS : DS + CONV_CH]
    extended = jnp.concatenate([rim, channels], axis=0)
    mixed = jnp.zeros_like(channels) + b_conv[None, :]
    for tap in range(CONV):
        same = (ext_seg[tap : tap + rows] == own_seg).astype(jnp.float32)
        mixed = mixed + extended[tap : tap + rows] * w_conv[:, tap][None, :] * same[:, None]
    active = jax.nn.silu(mixed)
    signal = active[:, :DS].reshape(rows, SSM_HEADS, SSM_DIM)
    inputs_b = active[:, DS : DS + STATE]
    inputs_c = active[:, DS + STATE :]
    step = jax.nn.softplus(inner[:, DS + CONV_CH :] + step_bias[None, :])
    log_decay = -step * jnp.exp(decay_log)[None, :]
    return (signal, inputs_b, inputs_c, step, log_decay)


def ssd_block(state, signal, inputs_b, inputs_c, step, log_decay, segments, seg_prev):
    size = signal.shape[0]
    cum = jnp.cumsum(log_decay, axis=0)
    diff = cum[:, None, :] - cum[None, :, :]
    order = jnp.arange(size)
    keep = (order[:, None] >= order[None, :]) & (segments[:, None] == segments[None, :])
    decay = jnp.exp(jnp.where(keep[:, :, None], diff, -1e30))
    scores = jnp.dot(inputs_c, inputs_b.T, precision=lax.Precision.HIGHEST)
    weighted = signal * step[:, :, None]
    result = jnp.einsum("tsh,ts,shp->thp", decay, scores, weighted, precision=lax.Precision.HIGHEST)
    carry = (segments == seg_prev).astype(jnp.float32)
    entering = jnp.einsum("tn,hpn->thp", inputs_c, state, precision=lax.Precision.HIGHEST)
    result = result + entering * (jnp.exp(cum) * carry[:, None])[:, :, None]
    tail = jnp.exp(cum[-1][None, :] - cum) * (segments == segments[-1]).astype(jnp.float32)[:, None]
    added = jnp.einsum("sh,shp,sn->hpn", tail, weighted, inputs_b, precision=lax.Precision.HIGHEST)
    new_state = state * (jnp.exp(cum[-1]) * carry[-1])[:, None, None] + added
    return (new_state, result)


def ssd_run(signal, inputs_b, inputs_c, step, log_decay, skip_gain, segments, seg_first, block):
    rows = signal.shape[0]
    count = rows // block
    before = jnp.concatenate([jnp.reshape(seg_first, (1,)), segments[:-1]])
    starts = before.reshape(count, block)[:, 0]

    def advance(state, item):
        return ssd_block(state, *item)

    initial = jnp.zeros((SSM_HEADS, SSM_DIM, STATE), jnp.float32)
    final, pieces = lax.scan(
        jax.checkpoint(advance),
        initial,
        (
            signal.reshape(count, block, SSM_HEADS, SSM_DIM),
            inputs_b.reshape(count, block, STATE),
            inputs_c.reshape(count, block, STATE),
            step.reshape(count, block, SSM_HEADS),
            log_decay.reshape(count, block, SSM_HEADS),
            segments.reshape(count, block),
            starts,
        ),
    )
    output = pieces.reshape(rows, SSM_HEADS, SSM_DIM) + skip_gain[None, :, None] * signal
    return (output.reshape(rows, DS), final)


def state_term(inputs_c, log_decay, entry, segments, seg_first):
    rows = inputs_c.shape[0]
    fading = (
        jnp.exp(jnp.cumsum(log_decay, axis=0))
        * (segments == seg_first).astype(jnp.float32)[:, None]
    )
    reading = jnp.einsum("tn,hpn->thp", inputs_c, entry, precision=lax.Precision.HIGHEST)
    return (reading * fading[:, :, None]).reshape(rows, DS)


def post(
    product,
    stream,
    attended,
    ssd_out,
    gate_in,
    w_attn_out,
    w_ssm_out,
    gain_ssm,
    gain_two,
    w_gate_up,
    w_down,
):
    gated = ssd_out * jax.nn.silu(gate_in)
    normed = (
        gated
        * lax.rsqrt(jnp.mean(gated * gated, axis=1, keepdims=True) + eps_norm)
        * gain_ssm[None, :]
    )
    mixed_out = round_value(normed)
    branch = round_grad(product(attended, w_attn_out) + product(mixed_out, w_ssm_out))
    middle = stream + branch
    normed_two = round_value(
        middle
        * lax.rsqrt(jnp.mean(middle * middle, axis=1, keepdims=True) + eps_norm)
        * gain_two[None, :]
    )
    gate_up = round_grad(product(normed_two, w_gate_up))
    width = w_down.shape[0]
    hidden = round_value(jax.nn.silu(gate_up[:, :width]) * gate_up[:, width:])
    return middle + round_grad(product(hidden, w_down))


def link(earlier, later):
    return (earlier[0] * later[0], later[0][:, None, None] * earlier[1] + later[1])


def local(
    tokens,
    lengths,
    cotangent,
    mixer_gain,
    query_weight,
    keyval_weight,
    inner_weight,
    conv_weight,
    conv_bias,
    ssm_gain,
    attn_out_weight,
    ssm_out_weight,
    ffn_gain,
    gate_up_weight,
    down_weight,
    decay_log,
    step_bias,
    skip_gain,
):
    gathered = (
        lax.all_gather(mixer_gain, ("dp", "seq"), axis=0, tiled=True),
        lax.all_gather(query_weight, ("dp", "seq"), axis=0, tiled=True),
        lax.all_gather(keyval_weight, ("dp", "seq"), axis=0, tiled=True),
        lax.all_gather(inner_weight, ("dp", "seq"), axis=0, tiled=True),
        lax.all_gather(conv_weight, ("dp", "seq"), axis=0, tiled=True),
        lax.all_gather(conv_bias, ("dp", "seq"), axis=0, tiled=True),
        lax.all_gather(ssm_gain, ("dp", "seq"), axis=0, tiled=True),
        lax.all_gather(attn_out_weight, ("dp", "seq"), axis=0, tiled=True),
        lax.all_gather(ssm_out_weight, ("dp", "seq"), axis=0, tiled=True),
        lax.all_gather(ffn_gain, ("dp", "seq"), axis=0, tiled=True),
        lax.all_gather(gate_up_weight, ("dp", "seq"), axis=0, tiled=True),
        lax.all_gather(down_weight, ("dp", "seq"), axis=0, tiled=True),
    )
    (
        gain_one,
        w_query,
        w_keyval,
        w_inner,
        w_conv,
        b_conv,
        gain_ssm,
        w_attn_out,
        w_ssm_out,
        gain_two,
        w_gate_up,
        w_down,
    ) = tuple((item.astype(jnp.float32) for item in gathered))
    rows = tokens.shape[0]
    seq_count = lax.axis_size("seq")
    seq_rank = lax.axis_index("seq")
    seq_lengths = lengths[0]
    group_rows = rows * seq_count
    longest = group_rows // 2
    window = min(group_rows, longest + rows)
    first_place = seq_rank * rows
    places = first_place + jnp.arange(rows)
    segments, offset = seq_layout(places, seq_lengths)
    rim_places = first_place - (CONV - 1) + jnp.arange(CONV - 1)
    rim_segs, unused_rim = seq_layout(rim_places, seq_lengths)
    seg_first = rim_segs[-1]
    window_start = jnp.clip(first_place + rows - window, 0, group_rows - window)
    window_places = window_start + jnp.arange(window)
    key_segs, unused_keys = seq_layout(window_places, seq_lengths)
    stream = tokens.astype(jnp.float32)

    def front_part(stream, gain_one, w_query, w_keyval, w_inner):
        return front(bfloat_dot, stream, gain_one, w_query, w_keyval, w_inner, offset)

    (queries, keyvals, inner), front_back = jax.vjp(
        front_part, stream, gain_one, w_query, w_keyval, w_inner
    )
    everyone = lax.all_gather(keyvals.astype(jnp.bfloat16), "seq", axis=0, tiled=True).astype(
        jnp.float32
    )

    def attend_part(queries, everyone):
        visible = lax.dynamic_slice_in_dim(everyone, window_start, window, 0)
        return attention(
            bfloat_dot, queries, visible, places, segments, window_places, key_segs, min(512, rows)
        )

    attended, attend_back = jax.vjp(attend_part, queries, everyone)
    channels = inner[:, DS : DS + CONV_CH]
    rim = passed_along(channels[rows - (CONV - 1) :].astype(jnp.bfloat16), "seq", 1).astype(
        jnp.float32
    )
    ext_seg = jnp.concatenate([rim_segs, segments])

    def mixer_part(inner, rim, w_conv, b_conv, step_bias, decay_log):
        return mixer_inputs(inner, rim, w_conv, b_conv, step_bias, decay_log, ext_seg, segments)

    (signal, inputs_b, inputs_c, step, log_decay), mixer_back = jax.vjp(
        mixer_part, inner, rim, w_conv, b_conv, step_bias, decay_log
    )

    def local_part(signal, inputs_b, inputs_c, step, log_decay, skip_gain):
        own_out, own_state = ssd_run(
            signal,
            inputs_b,
            inputs_c,
            step,
            log_decay,
            skip_gain,
            segments,
            seg_first,
            min(128, rows),
        )
        carry = jnp.exp(jnp.sum(log_decay, axis=0)) * (segments[-1] == seg_first).astype(
            jnp.float32
        )
        return (own_out, own_state, carry)

    (own_out, own_state, carry), local_back = jax.vjp(
        local_part, signal, inputs_b, inputs_c, step, log_decay, skip_gain
    )
    identity = (jnp.ones_like(carry), jnp.zeros_like(own_state))
    entry = entering_2((carry, own_state), "seq", link, identity, False)[1]

    def state_part(inputs_c, log_decay, entry):
        return state_term(inputs_c, log_decay, entry, segments, seg_first)

    entry_out, state_back = jax.vjp(state_part, inputs_c, log_decay, entry)
    ssd_total = own_out + entry_out

    def post_part(
        stream,
        attended,
        ssd_total,
        inner,
        w_attn_out,
        w_ssm_out,
        gain_ssm,
        gain_two,
        w_gate_up,
        w_down,
    ):
        return post(
            bfloat_dot,
            stream,
            attended,
            ssd_total,
            inner[:, :DS],
            w_attn_out,
            w_ssm_out,
            gain_ssm,
            gain_two,
            w_gate_up,
            w_down,
        )

    result, post_back = jax.vjp(
        post_part,
        stream,
        attended,
        ssd_total,
        inner,
        w_attn_out,
        w_ssm_out,
        gain_ssm,
        gain_two,
        w_gate_up,
        w_down,
    )
    (
        grad_stream_a,
        grad_attended,
        grad_ssd,
        grad_inner_a,
        g_attn_out,
        g_ssm_out,
        g_gain_ssm,
        g_gain_two,
        g_gate_up,
        g_down,
    ) = post_back(cotangent.astype(jnp.float32))
    grad_queries, grad_everyone = attend_back(grad_attended)
    grad_keyvals = jax.tree.map(
        lambda part: part.astype(jnp.float32),
        lax.psum_scatter(for_sending(grad_everyone), "seq", scatter_dimension=0, tiled=True),
    )
    grad_c_state, grad_decay_state, grad_entry = state_back(grad_ssd)
    downstream = entering_2((carry, grad_entry), "seq", link, identity, True)[1]
    grad_carry = jnp.sum(downstream * entry, axis=(1, 2))
    g_signal, g_inputs_b, g_inputs_c, g_step, g_log_decay, g_skip = local_back(
        (grad_ssd, downstream, grad_carry)
    )
    grad_inner_b, grad_rim, g_conv, g_conv_bias, g_step_bias, g_decay_log = mixer_back(
        (g_signal, g_inputs_b, g_inputs_c + grad_c_state, g_step, g_log_decay + grad_decay_state)
    )
    returned = passed_along(grad_rim, "seq", -1)
    tail_fix = jnp.pad(returned, ((rows - (CONV - 1), 0), (DS, IN_COLS - DS - CONV_CH)))
    grad_inner = grad_inner_a + grad_inner_b + tail_fix
    grad_stream_b, g_gain_one, g_query, g_keyval, g_inner = front_back(
        (grad_queries, grad_keyvals, grad_inner)
    )
    summed = (
        lax.psum_scatter(g_gain_one, ("dp", "seq"), scatter_dimension=0, tiled=True),
        lax.psum_scatter(g_query, ("dp", "seq"), scatter_dimension=0, tiled=True),
        lax.psum_scatter(g_keyval, ("dp", "seq"), scatter_dimension=0, tiled=True),
        lax.psum_scatter(g_inner, ("dp", "seq"), scatter_dimension=0, tiled=True),
        lax.psum_scatter(g_conv, ("dp", "seq"), scatter_dimension=0, tiled=True),
        lax.psum_scatter(g_conv_bias, ("dp", "seq"), scatter_dimension=0, tiled=True),
        lax.psum_scatter(g_gain_ssm, ("dp", "seq"), scatter_dimension=0, tiled=True),
        lax.psum_scatter(g_attn_out, ("dp", "seq"), scatter_dimension=0, tiled=True),
        lax.psum_scatter(g_ssm_out, ("dp", "seq"), scatter_dimension=0, tiled=True),
        lax.psum_scatter(g_gain_two, ("dp", "seq"), scatter_dimension=0, tiled=True),
        lax.psum_scatter(g_gate_up, ("dp", "seq"), scatter_dimension=0, tiled=True),
        lax.psum_scatter(g_down, ("dp", "seq"), scatter_dimension=0, tiled=True),
    )
    head_sums = lax.psum((g_decay_log, g_step_bias, g_skip), ("dp", "seq"))
    return (
        result.astype(jnp.bfloat16),
        grad_stream_a + grad_stream_b,
        summed[0],
        summed[1],
        summed[2],
        summed[3],
        summed[4],
        summed[5],
        summed[6],
        summed[7],
        summed[8],
        summed[9],
        summed[10],
        summed[11],
        head_sums[0],
        head_sums[1],
        head_sums[2],
    )


def solution(mesh):
    return jax.shard_map(
        local,
        mesh=mesh,
        in_specs=(
            P(("dp", "seq"), None),
            P("dp", None),
            P(("dp", "seq"), None),
            P(("dp", "seq")),
            P(("dp", "seq"), None),
            P(("dp", "seq"), None),
            P(("dp", "seq"), None),
            P(("dp", "seq"), None),
            P(("dp", "seq")),
            P(("dp", "seq")),
            P(("dp", "seq"), None),
            P(("dp", "seq"), None),
            P(("dp", "seq")),
            P(("dp", "seq"), None),
            P(("dp", "seq"), None),
            P(),
            P(),
            P(),
        ),
        out_specs=(
            P(("dp", "seq"), None),
            P(("dp", "seq"), None),
            P(("dp", "seq")),
            P(("dp", "seq"), None),
            P(("dp", "seq"), None),
            P(("dp", "seq"), None),
            P(("dp", "seq"), None),
            P(("dp", "seq")),
            P(("dp", "seq")),
            P(("dp", "seq"), None),
            P(("dp", "seq"), None),
            P(("dp", "seq")),
            P(("dp", "seq"), None),
            P(("dp", "seq"), None),
            P(),
            P(),
            P(),
        ),
        check_vma=False,
    )
```

profile of v0, /device:TPU:0, one launch (start us, length us, event | category | flops | bytes accessed | tf_op | source)
XLA Modules:
  0.0 2100.3 jit_solution(12108672980195716849)
XLA Ops:
  11.4 42.7 %all-reduce.38 = (bf16[1024]{0:T(1024)(128)(2,1)S(1)}, bf16[1792]{0:T(1024)(128)(2,1)S(1)}, bf16[1536]{0:T(1024)(128)(2,1)}, bf16[1024]{0:T(1024)(128)(2,1)}) all-reduce(bf16[1024]{0:T(1024)(128)(2,1)S(1)} %dynamic-update-slice.16, bf16[1792]{0:T(1024)(128)(2,1)S(1)} %dynamic-update-slice.17, ...), channel_id=1, replica_groups=mesh['dp'=4,'seq'=8] {'dp','seq'}, use_global_device_ids=true, to_apply=%add.27 | all-reduce | flops 5376 | bytes 21504
  57.8 71.4 %all_gather.59 = bf16[1024,256]{1,0:T(8,128)(2,1)S(1)} all-gather(bf16[32,256]{1,0:T(8,128)(2,1)S(1)} %copy-done.106), channel_id=1, replica_groups=mesh['dp'=4,'seq'=8] {'dp','seq'}, dimensions={0}, use_global_device_ids=true | all-gather | bytes 540672 | tf_op jit(solution)/shard_map/all_gather | solution.py:334
  135.2 63.6 %all-gather.3 = bf16[32,56,4]{1,2,0:T(4,128)(2,1)S(1)} all-gather(bf16[1,56,4]{1,2,0:T(4,128)(2,1)S(1)} %bitcast.724), channel_id=1, replica_groups=mesh['dp'=4,'seq'=8] {'dp','seq'}, dimensions={0}, use_global_device_ids=true | all-gather | bytes 14784 | tf_op jit(solution)/shard_map/all_gather | solution.py:336
  235.7 75.7 %while.133 = (s32[]{:T(128)}, f32[24,64,128]{2,1,0:T(8,128)S(1)}, f32[2,128,24,64]{1,0,3,2:T(2,128)}, f32[2,24,64,128]{3,2,1,0:T(8,128)}, f32[2,128,24]{2,1,0:T(...) while((s32[]{:T(128)}, f32[24,64,128]{2,1,0:T(8,128)S(1)}, ...), condition=%wide.region_12.13_spmd.clone.clone, body=%wide.region_10.12_spmd.clone.sunk.clone | while | flops 934730240 | bytes 10179904 | solution.py:247
  254.7 19.0 dynamic_update_slice.178
  292.5 19.0 dynamic_update_slice.178
  325.1 65.9 %while.131 = (s32[]{:T(128)}, bf16[8,1,256,64]{2,3,1,0:T(8,128)(2,1)}, s32[8]{0:T(128)S(1)}, bf16[8,1280,64]{2,1,0:T(8,128)(2,1)}, bf16[8,1280,64]{2,1,0:T(8,128...) while((s32[]{:T(128)}, ...), condition=%wide.region_8.9_spmd.clone.clone, body=%wide.region_5.8_spmd.clone.sunk.clone | while | flops 87163904 | bytes 9327855 | solution.py:175
  392.6 19.8 all-reduce.29
  437.3 51.6 %all-gather.18.cloned.1.call-done = bf16[512,1024]{1,0:T(8,128)(2,1)} async-done(((bf16[16,1024]{1,0:T(8,128)(2,1)}), bf16[512,1024]{1,0:T(8,128)(2,1)}) %all-gather.18.cloned.1.call-update) | async-done | bytes 1048592 | tf_op jit(solution)/shard_map/all_gather | solution.py:339
  492.3 76.0 %all-gather.24.cloned.1.call-done = bf16[1024,4096]{1,0:T(8,128)(2,1)} async-done(((bf16[32,4096]{1,0:T(8,128)(2,1)}), bf16[1024,4096]{1,0:T(8,128)(2,1)}) %all-gather.24.cloned.1.call-update) | async-done | bytes 8388624 | tf_op jit(solution)/shard_map/all_gather | solution.py:342
  576.1 55.9 %all-gather.26.cloned.1.call-done = bf16[2048,1024]{1,0:T(8,128)(2,1)} async-done(((bf16[64,1024]{1,0:T(8,128)(2,1)}), bf16[2048,1024]{1,0:T(8,128)(2,1)}) %all-gather.26.cloned.1.call-update) | async-done | bytes 4194320 | tf_op jit(solution)/shard_map/all_gather | solution.py:343
  647.1 67.8 %while.132 = (s32[]{:T(128)}, f32[2,1280,64]{1,2,0:T(8,128)S(1)}, f32[2,1280,64]{1,2,0:T(8,128)}, f32[8,1,256,64]{2,3,1,0:T(8,128)}, s32[8]{0:T(128)S(1)}, /*ind...) while((s32[]{:T(128)}, f32[2,1280,64]{1,2,0:T(8,128)S(1)}, ...), condition=%wide.region_42.43_spmd.clone.clone, body=%wide.region_38.42_spmd.clone.sunk.clone | while | flops 217092352 | bytes 19347700 | solution.py:175
  735.6 51.7 %reduce-scatter.10.cloned.1.call-done = bf16[256,256]{0,1:T(8,128)(2,1)} async-done(((bf16[2048,256]{0,1:T(8,128)(2,1)}), bf16[256,256]{0,1:T(8,128)(2,1)}) %reduce-scatter.10.cloned.1.call-update) | async-done | bytes 131088 | tf_op jit(solution)/shard_map/reduce_scatter | solution.py:490
  810.9 38.8 %all-gather.30.cloned.1.call-done = bf16[192,64,128]{2,1,0:T(8,128)(2,1)} async-done(((bf16[24,64,128]{2,1,0:T(8,128)(2,1)}), bf16[192,64,128]{2,1,0:T(8,128)(2,1)}) %all-gather.30.cloned.1.call-update) | async-done | bytes 3145744 | tf_op jit(solution)/shard_map/all_gather | solution.py:35
  867.8 105.4 %while.130 = (s32[]{:T(128)}, f32[24,64,128]{2,1,0:T(8,128)S(1)}, f32[2,128,24,64]{1,0,3,2:T(2,128)}, f32[2,128,128]{2,1,0:T(8,128)}, f32[2,128,128]{2,1,0:T(8,1...) while((s32[]{:T(128)}, f32[24,64,128]{2,1,0:T(8,128)S(1)}, ...), condition=%wide.region_33.34_spmd.clone, body=%wide.region_24.33_spmd.sunk.clone | while | flops 2198770176 | bytes 34682168 | solution.py:247
  897.1 19.0 dynamic_update_slice.169
  949.6 19.0 dynamic_update_slice.169
  1039.3 40.3 %all-reduce.37 = (f32[1024]{0:T(1024)S(1)}, f32[1792,4]{0,1:T(4,128)S(1)}, f32[1792]{0:T(1024)S(1)}, f32[1536]{0:T(1024)S(1)}, f32[1024]{0:T(1024)S(1)}, /*index=5*/f32[24]{0:T(128)}, f32[24]{0:T(128)}, f32[24]{0:T(128)}) all-reduce(f32[1024]{0:T(1024)S(1)} %get-tuple-element.1506, ...), channel_id=6, replica_groups=mesh['dp'=4,'seq'=8] {'dp','seq'}, use_global_device_ids=true, to_apply=%region_46.47.clone | all-reduce | flops 12616 | bytes 100928
  1085.4 37.9 %reduce-scatter.12.cloned.1.call-done = f32[32,512]{1,0:T(8,128)} async-done(((f32[1024,512]{1,0:T(8,128)}), f32[32,512]{1,0:T(8,128)}) %reduce-scatter.12.cloned.1.call-update) | async-done | bytes 65552 | tf_op jit(solution)/shard_map/reduce_scatter | solution.py:509
  1123.3 137.2 %reduce-scatter.18.cloned.1.call-done = f32[16,1024]{1,0:T(8,128)} async-done(((f32[512,1024]{1,0:T(8,128)}), f32[16,1024]{1,0:T(8,128)}) %reduce-scatter.18.cloned.1.call-update) | async-done | bytes 65552 | tf_op jit(solution)/shard_map/reduce_scatter | solution.py:515
  1260.5 117.3 %reduce-scatter.20.cloned.1.call-done = f32[48,1024]{1,0:T(8,128)} async-done(((f32[1536,1024]{1,0:T(8,128)}), f32[48,1024]{1,0:T(8,128)}) %reduce-scatter.20.cloned.1.call-update) | async-done | bytes 196624 | tf_op jit(solution)/shard_map/reduce_scatter | solution.py:516
  1377.8 186.7 %reduce-scatter.24.cloned.1.call-done = f32[64,1024]{1,0:T(8,128)} async-done(((f32[2048,1024]{1,0:T(8,128)}), f32[64,1024]{1,0:T(8,128)}) %reduce-scatter.24.cloned.1.call-update) | async-done | bytes 262160 | tf_op jit(solution)/shard_map/reduce_scatter | solution.py:519
  1564.4 169.5 %reduce-scatter.16.cloned.1.call-done = f32[32,3352]{1,0:T(8,128)} async-done(((f32[1024,3352]{1,0:T(8,128)}), f32[32,3352]{1,0:T(8,128)}) %reduce-scatter.16.cloned.1.call-update) | async-done | bytes 429072 | tf_op jit(solution)/shard_map/reduce_scatter | solution.py:511
  1733.9 359.6 %reduce-scatter.22.cloned.1.call-done = f32[32,4096]{1,0:T(8,128)} async-done(((f32[1024,4096]{1,0:T(8,128)}), f32[32,4096]{1,0:T(8,128)}) %reduce-scatter.22.cloned.1.call-update) | async-done | bytes 524304 | tf_op jit(solution)/shard_map/reduce_scatter | solution.py:518
  (969 shorter events, 482.2 us)
Async XLA Ops:
  7.2 193.1 %all-gather.20.cloned.1.call-start = ((), (), s32[]{:S(2)}) async-start(), calls=%async_computation.11 | async-start | bytes 7299072 | tf_op jit(solution)/shard_map/all_gather | solution.py:335
  7.9 311.9 %all-gather.16.cloned.1.call-start = ((), (), s32[]{:S(2)}) async-start(), calls=%async_computation.9 | async-start | bytes 1179648 | tf_op jit(solution)/shard_map/all_gather | solution.py:383
  57.7 148.5 %copy-start.13 = (bf16[256,1024]{1,0:T(8,128)(2,1)}, bf16[256,1024]{1,0:T(8,128)(2,1)S(1)}, u32[]{:S(2)}) copy-start(bf16[256,1024]{1,0:T(8,128)(2,1)S(1)} %fusion.143) | copy-start | bytes 1572868
  132.2 190.0 %all-gather.14.cloned.1.call-start = ((), (), s32[]{:S(2)}) async-start(), calls=%async_computation.8 | async-start | bytes 1081344 | tf_op jit(solution)/shard_map/all_gather | solution.py:333
  132.9 279.7 %all-gather.28.cloned.1.call-start = ((), (), s32[]{:S(2)}) async-start(), calls=%async_computation.23 | async-start | bytes 3538944 | tf_op jit(solution)/shard_map/all_gather | solution.py:35
  206.7 10.9 collective-permute-start
  312.3 121.1 %all-gather.22.cloned.1.call-start = ((), (), s32[]{:S(2)}) async-start(), calls=%async_computation.12 | async-start | bytes 3244032 | tf_op jit(solution)/shard_map/all_gather | solution.py:340
  312.9 175.9 %all-gather.18.cloned.1.call-start = ((), (), s32[]{:S(2)}) async-start(), calls=%async_computation.10 | async-start | bytes 1081344 | tf_op jit(solution)/shard_map/all_gather | solution.py:339
  313.5 254.8 %all-gather.24.cloned.1.call-start = ((), (), s32[]{:S(2)}) async-start(), calls=%async_computation.13 | async-start | bytes 8650752 | tf_op jit(solution)/shard_map/all_gather | solution.py:342
  314.3 317.7 %all-gather.26.cloned.1.call-start = ((), (), s32[]{:S(2)}) async-start(), calls=%async_computation.14 | async-start | bytes 4325376 | tf_op jit(solution)/shard_map/all_gather | solution.py:343
  315.0 472.3 %reduce-scatter.10.cloned.1.call-start = ((), (), s32[]{:S(2)}) async-start(), calls=%async_computation.15 | async-start | bytes 1179648 | tf_op jit(solution)/shard_map/reduce_scatter | solution.py:490
  412.6 320.8 %copy-start.71 = (f32[256,24]{0,1:T(8,128)}, f32[256,24]{0,1:T(8,128)S(1)}, u32[]{:S(2)}) copy-start(f32[256,24]{0,1:T(8,128)S(1)} %fusion.160) | copy-start | bytes 73732
  491.1 151.1 %copy-start.17 = (f32[256,1024]{1,0:T(8,128)}, f32[256,1024]{1,0:T(8,128)S(1)}, u32[]{:S(2)}) copy-start(f32[256,1024]{1,0:T(8,128)S(1)} %get-tuple-element.1720) | copy-start | bytes 3145732
  491.1 151.1 %copy-start.107 = (f32[256]{0:T(256)}, f32[256]{0:T(256)S(1)}, u32[]{:S(2)}) copy-start(f32[256]{0:T(256)S(1)} %fusion.166) | copy-start | bytes 3076
  492.3 139.7 %copy-start.40 = (bf16[256,1024]{1,0:T(8,128)(2,1)S(1)}, bf16[256,1024]{1,0:T(8,128)(2,1)}, u32[]{:S(2)}) copy-start(bf16[256,1024]{1,0:T(8,128)(2,1)} %param.32) | copy-start | bytes 1572868
  724.9 124.8 %all-gather.30.cloned.1.call-start = ((), (), s32[]{:S(2)}) async-start(), calls=%async_computation.24 | async-start | bytes 3538944 | tf_op jit(solution)/shard_map/all_gather | solution.py:35
  735.6 349.8 %reduce-scatter.14.cloned.1.call-start = ((), (), s32[]{:S(2)}) async-start(), calls=%async_computation.17 | async-start | bytes 1081344 | tf_op jit(solution)/shard_map/reduce_scatter | solution.py:510
  790.6 332.7 %reduce-scatter.12.cloned.1.call-start = ((), (), s32[]{:S(2)}) async-start(), calls=%async_computation.16 | async-start | bytes 2162688 | tf_op jit(solution)/shard_map/reduce_scatter | solution.py:509
  792.7 467.8 %reduce-scatter.18.cloned.1.call-start = ((), (), s32[]{:S(2)}) async-start(), calls=%async_computation.19 | async-start | bytes 2162688 | tf_op jit(solution)/shard_map/reduce_scatter | solution.py:515
  795.3 582.4 %reduce-scatter.20.cloned.1.call-start = ((), (), s32[]{:S(2)}) async-start(), calls=%async_computation.20 | async-start | bytes 6488064 | tf_op jit(solution)/shard_map/reduce_scatter | solution.py:516
  799.0 765.4 %reduce-scatter.24.cloned.1.call-start = ((), (), s32[]{:S(2)}) async-start(), calls=%async_computation.22 | async-start | bytes 8650752 | tf_op jit(solution)/shard_map/reduce_scatter | solution.py:519
  804.9 929.0 %reduce-scatter.16.cloned.1.call-start = ((), (), s32[]{:S(2)}) async-start(), calls=%async_computation.18 | async-start | bytes 14598144 | tf_op jit(solution)/shard_map/reduce_scatter | solution.py:511
  994.5 9.4 collective-permute-start.1
  1016.0 1077.6 %reduce-scatter.22.cloned.1.call-start = ((), (), s32[]{:S(2)}) async-start(), calls=%async_computation.21 | async-start | bytes 17301504 | tf_op jit(solution)/shard_map/reduce_scatter | solution.py:518
  (183 other events, 2197.4 us)
Sparse Core Ops, SparseCore 0:
  11.0 79.0 all-gather.19
  132.3 36.1 all-gather.15
  171.5 55.6 all-gather.13
  312.5 60.1 all-gather.27
  375.4 57.9 all-gather.21
  436.3 52.5 all-gather.17
  491.9 76.3 all-gather.23
  571.3 60.6 all-gather.25
  725.0 62.2 reduce-scatter.9
  790.2 59.4 all-gather.29
  852.6 133.7 reduce-scatter.13
  989.0 134.2 reduce-scatter.11
  1126.2 134.2 reduce-scatter.17
  1266.5 111.1 reduce-scatter.19
  1380.6 183.7 reduce-scatter.23
  1571.9 162.0 reduce-scatter.15
  1736.8 356.7 reduce-scatter.21
where the time goes:
time: 2120 us; the launch traced here: 2100 us
  waiting for transfers between devices  1300 us (61%)
  blocking collectives  238 us (11%)
  local copies, waits for them, and re-layouts  232 us (11%)
  matrix products  183 us (9%)
  other arithmetic  103 us (5%)
    reduce_scatter x1, waiting for transfers between devices, local(): lax.psum_scatter(g_gate_up, ('dp', 'seq'), scatter_dimension=0, tiled=True)  360 us
    reduce_scatter x1, waiting for transfers between devices, local(): lax.psum_scatter(g_down, ('dp', 'seq'), scatter_dimension=0, tiled=True)  187 us
    reduce_scatter x1, waiting for transfers between devices, local(): lax.psum_scatter(g_inner, ('dp', 'seq'), scatter_dimension=0, tiled=True)  170 us
    reduce_scatter x1, waiting for transfers between devices, local(): lax.psum_scatter(g_attn_out, ('dp', 'seq'), scatter_dimension=0, tiled=True)  137 us
    reduce_scatter x1, waiting for transfers between devices, local(): lax.psum_scatter(g_ssm_out, ('dp', 'seq'), scatter_dimension=0, tiled=True)  117 us
    unnamed x3, blocking collectives  103 us
    dot_general x70, matrix products, bfloat_dot(): return multiply(left, right)  99.5 us
    dynamic_update_slice x8, local copies, waits for them, and re-layouts, ssd_run(): lax.scan(jax.checkpoint(advance), initial, (signal.reshape(count, block,...  76 us
  transfers between devices with their start and end apart: 19, of which 13 were waited for; matrix products, arithmetic and copies ran while one was open for 19% of the time, Pallas kernels for 0%

commit v1 on v0

v1 whole, which is shorter than its diff:
```python
import functools

import jax
import jax.numpy as jnp
from jax import lax
from jax.experimental import pallas as pl
from jax.experimental.pallas import tpu as pltpu
from jax.sharding import PartitionSpec as P

HEADS = 8
KV_HEADS = 2
HEAD_DIM = 64
SSM_HEADS = 24
SSM_DIM = 64
STATE = 128
CONV = 4
DS = 1536
CONV_CH = 1792
RIM = 16
LANES = 128
A_COLS = 2 * KV_HEADS * HEAD_DIM + HEADS * HEAD_DIM + 2 * STATE + LANES
EPS = 1e-6
BASE = 10000.0
NEG = -1e30
AXES = ("dp", "seq")

f32 = jnp.float32
bf16 = jnp.bfloat16


def nn(a, b):
    return lax.dot_general(a, b, (((1,), (0,)), ((), ())), preferred_element_type=f32)


def tn(a, b):
    return lax.dot_general(a, b, (((0,), (0,)), ((), ())), preferred_element_type=f32)


def nt(a, b):
    return lax.dot_general(a, b, (((1,), (1,)), ((), ())), preferred_element_type=f32)


def nn_full(a, b):
    return lax.dot_general(
        a, b, (((1,), (0,)), ((), ())), precision=lax.Precision.HIGHEST, preferred_element_type=f32
    )


def iota(shape, dim):
    return lax.broadcasted_iota(jnp.int32, shape, dim)


def head_spread():
    row = iota((LANES, DS), 0)
    return (iota((LANES, DS), 1) // SSM_DIM == row).astype(f32)


def head_sum_matrix():
    col = iota((DS, LANES), 1)
    return (iota((DS, LANES), 0) // SSM_DIM == col).astype(f32)


def extents():
    across, along = lax.axis_size("dp"), lax.axis_size("seq")
    return {
        "x": (1, 2),
        "z": (2, along // 2),
        "core": (along, 2),
        "y": (2 * along, across // 2),
    }


def my_index():
    return lax.axis_index("dp") * lax.axis_size("seq") + lax.axis_index("seq")


def place_on(group):
    unit, size = extents()[group]
    return (my_index() // unit) % size


def swap(array, mask):
    count = lax.axis_size("dp") * lax.axis_size("seq")
    return lax.ppermute(array, AXES, [(i, i ^ mask) for i in range(count)])


def in_order(pieces, place):
    pieces = list(pieces)
    bit = 1
    while bit < len(pieces):
        flag = (place // bit) % 2 == 1
        pieces = [jnp.where(flag, pieces[j ^ bit], pieces[j]) for j in range(len(pieces))]
        bit *= 2
    return pieces


def collect(array, group, axis):
    unit, size = extents()[group]
    pieces = [array] + [swap(array, k * unit) for k in range(1, size)]
    return jnp.stack(in_order(pieces, place_on(group)), axis)


def gather_pair(shard, first):
    full = collect(shard, "z", 0)
    if first == "y":
        full = collect(collect(full, "y", 0), "x", 2)
    else:
        full = collect(collect(full, "x", 1), "y", 0)
    other = swap(full, extents()["core"][0])
    shape = (full.shape[0], full.shape[1] * full.shape[2] * full.shape[3], full.shape[4])
    return full.reshape(shape), other.reshape(shape)


def fold(total, group, axis):
    unit, size = extents()[group]
    place = place_on(group)
    result = lax.dynamic_index_in_dim(total, place, axis, False).astype(f32)
    for k in range(1, size):
        part = lax.dynamic_index_in_dim(total, place ^ k, axis, False).astype(bf16)
        result = result + swap(part, k * unit).astype(f32)
    return result


def reduce_pair(own, received, rows, first):
    table = extents()
    shape = (table["y"][1], table["z"][1], table["x"][1], rows, own.shape[-1])
    total = own.reshape(shape).astype(f32) + received.reshape(shape).astype(f32)
    if first == "x":
        total = fold(fold(total, "x", 2), "y", 0)
    else:
        total = fold(fold(total, "y", 0), "x", 1)
    return fold(total, "z", 0)


def gather_small(vector):
    full = collect(collect(collect(vector, "z", 0), "x", 1), "core", 0)
    return collect(full, "y", 0).reshape(-1, vector.shape[-1])


def sum_small(array):
    mask = 1
    while mask < lax.axis_size("dp") * lax.axis_size("seq"):
        array = array + swap(array, mask)
        mask *= 2
    return array


def shifted(array, by):
    count = lax.axis_size("seq")
    pairs = [(i, i + by) for i in range(count) if 0 <= i + by < count]
    return lax.ppermute(array, "seq", pairs)


def link(earlier, later):
    carry = later[1]
    wide = jnp.repeat(carry[0, :SSM_HEADS], SSM_DIM)[:, None]
    return (later[0] + wide * earlier[0], carry * earlier[1])


def carried(state, carry, back, sign):
    def moved(pair, by):
        packed = jnp.concatenate([pair[0], jnp.pad(pair[1], ((0, RIM - 1), (0, 0)))], 0)
        got = shifted(packed.astype(bf16), sign * by).astype(f32)
        return (got[:DS], got[DS : DS + 1])

    pair = (state, carry)
    by = 1
    while by < back:
        pair = link(moved(pair, by), pair)
        by *= 2
    return moved(pair, 1)[0]


def halves(block, core):
    width = block.shape[1] // 2
    low, high = block[:, :width], block[:, width:]
    return jnp.where(core == 0, low, high), jnp.where(core == 0, high, low)


def put(ref, y, own, other, core):
    width = own.shape[1]
    base = y * 2 * width
    ref[:, base : base + width] = jnp.where(core == 0, own, other).astype(ref.dtype)
    ref[:, base + width : base + 2 * width] = jnp.where(core == 0, other, own).astype(ref.dtype)


def sides(ref, core, count):
    width = ref.shape[-1] // count
    return [halves(ref[:, y * width : (y + 1) * width], core) for y in range(count)]


def cross_half(value):
    lane = iota(value.shape, 1) % HEAD_DIM
    up = pltpu.roll(value, LANES - HEAD_DIM // 2, 1)
    down = pltpu.roll(value, HEAD_DIM // 2, 1)
    return jnp.where(lane < HEAD_DIM // 2, up, down)


def turned(value, cos, sin):
    return value * cos + cross_half(value) * sin


def turned_back(value, cos, sin):
    return value * cos - cross_half(value) * sin


def split_heads(pair, which, lane):
    flipped = pltpu.roll(pair, HEAD_DIM, 1)
    if which == 0:
        return jnp.where(lane < HEAD_DIM, pair, 0.0), jnp.where(lane < HEAD_DIM, flipped, 0.0)
    return jnp.where(lane >= HEAD_DIM, flipped, 0.0), jnp.where(lane >= HEAD_DIM, pair, 0.0)


def join_heads(even, odd, which, lane):
    if which == 0:
        return jnp.where(lane < HEAD_DIM, even, pltpu.roll(odd, HEAD_DIM, 1))
    return jnp.where(lane < HEAD_DIM, pltpu.roll(even, HEAD_DIM, 1), odd)


def conv_taps(chan_ref, cols, off):
    ext = chan_ref[:, cols].astype(f32)
    taps = []
    for i in range(CONV):
        back = CONV - 1 - i
        rows = pltpu.roll(ext, back, 0)[RIM:] if back else ext[RIM:]
        taps.append(rows * (off >= back).astype(f32))
    return taps


def sigmoid(v):
    return 1.0 / (1.0 + jnp.exp(-v))


def softplus(v):
    return jnp.maximum(v, 0.0) + jnp.log1p(jnp.exp(-jnp.abs(v)))


def tail_of(cum, off):
    rows = cum.shape[0]
    last_off = off[rows - 1 :, :]
    keep = iota((rows, 1), 0) >= rows - 1 - last_off
    return jnp.exp(cum[rows - 1 :, :] - cum) * keep.astype(f32)


def fade_of(cum, off):
    keep = off > iota((cum.shape[0], 1), 0)
    return jnp.exp(cum) * keep.astype(f32)


def carry_of(cum, off):
    rows = cum.shape[0]
    return jnp.exp(cum[rows - 1 :, :]) * (off[rows - 1 :, :] >= rows).astype(f32)


def front_kernel(
    core_ref, tok_ref, gain_ref, wa_own, wa_oth, wb_own, wb_oth, cos_ref, sin_ref, off_ref,
    cw_ref, cb_ref, sb_ref, dec_ref,
    q8_ref, kv_ref, normed_ref, chan_ref, x_ref, bc_ref, step_ref, cum_ref, cumt_ref, z_ref,
    state_ref, carry_ref,
    n_ref, xt_ref,
):
    core = core_ref[0]
    rows = cos_ref.shape[0]
    tok = tok_ref[...].astype(f32)
    rms = lax.rsqrt(jnp.mean(tok * tok, axis=1, keepdims=True) + EPS)
    n_ref[...] = (tok * rms * gain_ref[...]).astype(bf16)
    normed_ref[...] = n_ref[RIM:, :]
    count = wa_own.shape[0]
    blocks = sides(n_ref, core, count)

    def project(own_ref, oth_ref, cols):
        total = 0.0
        for y, (own, oth) in enumerate(blocks):
            total = total + nn(own, own_ref[y, :, cols]) + nn(oth, oth_ref[y, :, cols])
        return total

    lane = iota((rows, LANES), 1)
    cos, sin, off = cos_ref[...], sin_ref[...], off_ref[...]
    kv = project(wa_own, wa_oth, pl.ds(0, 256))[RIM:]
    kv_ref[:, :LANES] = turned(kv[:, :LANES], cos, sin).astype(bf16)
    kv_ref[:, LANES:] = kv[:, LANES:].astype(bf16)
    queries = project(wa_own, wa_oth, pl.ds(256, 512))[RIM:]
    for j in range(HEADS // 2):
        pair = turned(queries[:, j * LANES : (j + 1) * LANES], cos, sin)
        even, odd = split_heads(pair, j // 2, lane)
        q8_ref[2 * j] = even.astype(bf16)
        q8_ref[2 * j + 1] = odd.astype(bf16)
    rest = project(wa_own, wa_oth, pl.ds(768, 384))
    chan_ref[:, DS:] = rest[:, : 2 * STATE].astype(bf16)
    z = rest[RIM:, 2 * STATE :].astype(bf16).astype(f32) + sb_ref[...]
    for j in range(DS // 512):
        cols = slice(j * 512, (j + 1) * 512)
        chan_ref[:, cols] = project(wb_own, wb_oth, pl.ds(j * 512, 512)).astype(bf16)
    z_ref[...] = z
    step = softplus(z)
    step_ref[...] = step
    tri = (iota((rows, rows), 0) >= iota((rows, rows), 1)).astype(f32)
    cum = nn_full(tri, -step * dec_ref[...])
    cum_ref[...] = cum
    cumt_ref[...] = cum.T
    carry_ref[...] = carry_of(cum, off)
    weight = nn_full(step * tail_of(cum, off), head_spread())
    for j in range(CONV_CH // 256):
        cols = slice(j * 256, (j + 1) * 256)
        mixed = cb_ref[:, cols]
        for i, tap in enumerate(conv_taps(chan_ref, cols, off)):
            mixed = mixed + tap * cw_ref[i : i + 1, cols]
        active = mixed * sigmoid(mixed)
        if j < DS // 256:
            x_ref[:, cols] = active
            xt_ref[:, cols] = (active * weight[:, cols]).astype(bf16)
        else:
            bc_ref[...] = active
    state_ref[...] = tn(xt_ref[...], bc_ref[:, :STATE].astype(bf16))


def scan_masks(off, rows):
    t, s = iota((rows, rows), 0), iota((rows, rows), 1)
    return (s <= t) & (s >= t - off)


def scan_kernel(x_ref, bc_ref, step_ref, cum_ref, cumt_ref, off_ref, y_ref, xw_ref, ce_ref):
    rows = x_ref.shape[0]
    spread = head_spread()
    xw_ref[...] = (x_ref[...] * nn_full(step_ref[...], spread)).astype(bf16)
    ce_ref[...] = nn_full(cum_ref[...], spread)
    keys, reads = bc_ref[:, :STATE].astype(bf16), bc_ref[:, STATE:].astype(bf16)
    scores = jnp.where(scan_masks(off_ref[...], rows), nt(reads, keys), 0.0)
    lane = iota((rows, LANES), 1)

    def pair(j, unused):
        cols = pl.ds(pl.multiple_of(j * LANES, LANES), LANES)
        wide = ce_ref[:, cols]
        xw = xw_ref[:, cols]
        outs = []
        for k in range(2):
            late = wide[:, k * SSM_DIM : k * SSM_DIM + 1]
            early = cumt_ref[pl.ds(2 * j + k, 1), :]
            decay = jnp.exp(jnp.minimum(late - early, 0.0))
            outs.append(nn((decay * scores).astype(bf16), xw))
        y_ref[:, cols] = jnp.where(lane < SSM_DIM, outs[0], outs[1])
        return unused

    lax.fori_loop(0, SSM_HEADS // 2, pair, 0)


def attend_bias(off, rows, window):
    query = iota((rows, window), 0) + (window - rows)
    key = iota((rows, window), 1)
    return jnp.where((key <= query) & (key >= query - off), 0.0, NEG)


def attend_kernel(count, q8_ref, *refs):
    pieces, (off_ref, att_ref, lse_ref, k_ref, v_ref, bias_ref, o_ref) = refs[:count], refs[count:]
    rows = off_ref.shape[0]
    window = count * rows
    for i, piece in enumerate(pieces):
        k_ref[i * rows : (i + 1) * rows, :] = piece[:, :LANES]
        v_ref[i * rows : (i + 1) * rows, :] = piece[:, LANES:]
    bias_ref[...] = attend_bias(off_ref[...], rows, window)
    lane = iota((rows, LANES), 1)

    def head(h, lses):
        scores = nt(q8_ref[h], k_ref[...]) * HEAD_DIM**-0.5 + bias_ref[...]
        top = jnp.max(scores, axis=1, keepdims=True)
        probs = jnp.exp(scores - top)
        total = jnp.sum(probs, axis=1, keepdims=True)
        o_ref[h] = nn((probs * (1.0 / total)).astype(bf16), v_ref[...])
        return jnp.where(lane == h, top + jnp.log(total), lses)

    lse_ref[...] = lax.fori_loop(0, HEADS, head, jnp.zeros((rows, LANES), f32))
    for j in range(HEADS // 2):
        pair = join_heads(o_ref[2 * j], o_ref[2 * j + 1], j // 2, lane)
        att_ref[:, j * LANES : (j + 1) * LANES] = pair.astype(bf16)


def attend_back_kernel(count, q8_ref, *refs):
    pieces, rest = refs[:count], refs[count:]
    off_ref, lse_ref, datt_ref, cos_ref, sin_ref, dq_ref, dkv_ref = rest[:7]
    k_ref, v_ref, bias_ref, do_ref, dq8_ref = rest[7:]
    rows = off_ref.shape[0]
    window = count * rows
    for i, piece in enumerate(pieces):
        k_ref[i * rows : (i + 1) * rows, :] = piece[:, :LANES]
        v_ref[i * rows : (i + 1) * rows, :] = piece[:, LANES:]
    bias_ref[...] = attend_bias(off_ref[...], rows, window)
    lane = iota((rows, LANES), 1)
    for j in range(HEADS // 2):
        pair = datt_ref[:, j * LANES : (j + 1) * LANES].astype(f32)
        even, odd = split_heads(pair, j // 2, lane)
        do_ref[2 * j] = even.astype(bf16)
        do_ref[2 * j + 1] = odd.astype(bf16)
    dkv_ref[...] = jnp.zeros(dkv_ref.shape, f32)

    def head(h, unused):
        query, grad = q8_ref[h], do_ref[h]
        total = jnp.sum(jnp.where(lane == h, lse_ref[...], 0.0), axis=1, keepdims=True)
        scores = nt(query, k_ref[...]) * HEAD_DIM**-0.5 + bias_ref[...]
        probs = jnp.exp(scores - total)
        dprobs = nt(grad, v_ref[...])
        mean = jnp.sum(probs * dprobs, axis=1, keepdims=True)
        draw = (probs * (dprobs - mean) * HEAD_DIM**-0.5).astype(bf16)
        dq8_ref[h] = nn(draw, k_ref[...])
        dkv_ref[:, :LANES] += tn(draw, query)
        dkv_ref[:, LANES:] += tn(probs.astype(bf16), grad)
        return unused

    lax.fori_loop(0, HEADS, head, 0)
    for j in range(HEADS // 2):
        pair = join_heads(dq8_ref[2 * j], dq8_ref[2 * j + 1], j // 2, lane)
        back = turned_back(pair, cos_ref[...], sin_ref[...])
        dq_ref[:, j * LANES : (j + 1) * LANES] = back.astype(bf16)


def post_kernel(
    core_ref, tok_ref, cot_ref, att_ref, yl_ref, x_ref, bc_ref, cum_ref, off_ref, entry_ref,
    skip_ref, normed_ref, gssm_ref, gffn_ref,
    gate_own, gate_oth, ao_own, ao_oth, so_own, so_oth, gu_own, gu_oth, down_own, down_oth,
    out_ref, dmid_ref, datt_ref, dssd_ref, ycore_ref, dentry_ref, n2_ref, hid_ref, mixed_ref,
    dbr_ref, dgu_ref, dgate_ref, dng_ref, dgssm_ref, dgffn_ref,
    gi_ref, gd_ref, mid_ref, gu_ref, dn_ref, dmx_ref, fd_ref,
):
    core = core_ref[0]
    rows, width = tok_ref.shape
    ff = hid_ref.shape[1]
    count = gate_own.shape[0]
    ys = range(count)
    reads = bc_ref[:, STATE:].astype(bf16)
    blocks = sides(normed_ref, core, count)
    spread = head_spread()
    fade = nn_full(fade_of(cum_ref[...], off_ref[...]), spread)
    entered = nt(reads, entry_ref[...].astype(bf16))
    square = 0.0
    for j in range(DS // 512):
        cols = slice(j * 512, (j + 1) * 512)
        gate = 0.0
        for y, (own, oth) in enumerate(blocks):
            gate = gate + nn(own, gate_own[y, :, cols]) + nn(oth, gate_oth[y, :, cols])
        gate = gate.astype(bf16).astype(f32)
        gi_ref[:, cols] = gate
        ycore = yl_ref[:, cols] + fade[:, cols] * entered[:, cols]
        ycore_ref[:, cols] = ycore
        ssd = ycore + skip_ref[:, cols] * x_ref[:, cols]
        gated = ssd * gate * sigmoid(gate)
        gd_ref[:, cols] = gated
        square = square + jnp.sum(gated * gated, axis=1, keepdims=True)
    rms_gate = lax.rsqrt(square / DS + EPS)
    mixed_ref[...] = (gd_ref[...] * rms_gate * gssm_ref[...]).astype(bf16)
    att_blocks = sides(att_ref, core, count)
    mix_blocks = sides(mixed_ref, core, count)
    square = 0.0
    for j in range(width // 512):
        cols = slice(j * 512, (j + 1) * 512)
        branch = 0.0
        for y in ys:
            branch = branch + nn(att_blocks[y][0], ao_own[y, :, cols])
            branch = branch + nn(att_blocks[y][1], ao_oth[y, :, cols])
            branch = branch + nn(mix_blocks[y][0], so_own[y, :, cols])
            branch = branch + nn(mix_blocks[y][1], so_oth[y, :, cols])
        middle = tok_ref[:, cols].astype(f32) + branch
        mid_ref[:, cols] = middle
        square = square + jnp.sum(middle * middle, axis=1, keepdims=True)
    rms = lax.rsqrt(square / width + EPS)
    n2_ref[...] = (mid_ref[...] * rms * gffn_ref[...]).astype(bf16)
    blocks = sides(n2_ref, core, count)

    def up(j, unused):
        cols = pl.ds(pl.multiple_of(j * 512, 512), 512)
        total = 0.0
        for y, (own, oth) in enumerate(blocks):
            total = total + nn(own, gu_own[y, :, cols]) + nn(oth, gu_oth[y, :, cols])
        gu_ref[:, cols] = total
        return unused

    lax.fori_loop(0, 2 * ff // 512, up, 0)
    for j in range(ff // 512):
        gate = gu_ref[:, j * 512 : (j + 1) * 512]
        lift = gu_ref[:, ff + j * 512 : ff + (j + 1) * 512]
        hid_ref[:, j * 512 : (j + 1) * 512] = (gate * sigmoid(gate) * lift).astype(bf16)
    blocks = sides(hid_ref, core, count)
    for j in range(width // 512):
        cols = slice(j * 512, (j + 1) * 512)
        total = mid_ref[:, cols]
        for y, (own, oth) in enumerate(blocks):
            total = total + nn(own, down_own[y, :, cols]) + nn(oth, down_oth[y, :, cols])
        out_ref[:, cols] = total.astype(bf16)
    cot = cot_ref[...]
    wide = ff // count // 2
    for y in ys:
        own, oth = nt(cot, down_own[y]), nt(cot, down_oth[y])
        for k in range(2):
            dhid = jnp.where(core == k, own, oth)
            base = (2 * y + k) * wide
            gate = gu_ref[:, base : base + wide]
            lift = gu_ref[:, ff + base : ff + base + wide]
            sg = sigmoid(gate)
            dgate = dhid * lift * (sg * (1.0 + gate * (1.0 - sg)))
            dgu_ref[:, base : base + wide] = dgate.astype(bf16)
            dgu_ref[:, ff + base : ff + base + wide] = (dhid * gate * sg).astype(bf16)
    for y in ys:
        put(dn_ref, y, nt(dgu_ref[...], gu_own[y]), nt(dgu_ref[...], gu_oth[y]), core)
    unit = mid_ref[...] * rms
    dn = dn_ref[...]
    dgffn_ref[...] = jnp.sum(dn * unit, axis=0, keepdims=True)
    dn = dn * gffn_ref[...]
    dmid = cot.astype(f32) + rms * (dn - unit * jnp.mean(dn * unit, axis=1, keepdims=True))
    dmid_ref[...] = dmid
    dbr_ref[...] = dmid.astype(bf16)
    for y in ys:
        put(datt_ref, y, nt(dbr_ref[...], ao_own[y]), nt(dbr_ref[...], ao_oth[y]), core)
        put(dmx_ref, y, nt(dbr_ref[...], so_own[y]), nt(dbr_ref[...], so_oth[y]), core)
    mean = 0.0
    for j in range(DS // 512):
        cols = slice(j * 512, (j + 1) * 512)
        unit = gd_ref[:, cols] * rms_gate
        dmx = dmx_ref[:, cols]
        dgssm_ref[:, cols] = jnp.sum(dmx * unit, axis=0, keepdims=True)
        mean = mean + jnp.sum(dmx * gssm_ref[:, cols] * unit, axis=1, keepdims=True)
    mean = mean / DS
    for j in range(DS // 512):
        cols = slice(j * 512, (j + 1) * 512)
        unit = gd_ref[:, cols] * rms_gate
        dgated = rms_gate * (dmx_ref[:, cols] * gssm_ref[:, cols] - unit * mean)
        gate = gi_ref[:, cols]
        sg = sigmoid(gate)
        ssd = ycore_ref[:, cols] + skip_ref[:, cols] * x_ref[:, cols]
        dssd = dgated * gate * sg
        dssd_ref[:, cols] = dssd
        dgate_ref[:, cols] = (dgated * ssd * (sg * (1.0 + gate * (1.0 - sg)))).astype(bf16)
        fd_ref[:, cols] = (dssd * fade[:, cols]).astype(bf16)
    dentry_ref[...] = tn(fd_ref[...], reads)
    for y in ys:
        put(dng_ref, y, nt(dgate_ref[...], gate_own[y]), nt(dgate_ref[...], gate_oth[y]), core)


def picked(ref, y, count, side):
    width = ref.shape[1] // count
    half = width // 2
    base = y * width
    low, high = ref[:, base : base + half], ref[:, base + half : base + width]
    return jnp.where(side == 0, low, high)


def products_kernel(pairs, side_ref, *refs):
    side = side_ref[0]
    names = max(max(p) for p in pairs) + 1
    ins, outs = refs[:names], refs[names:]
    for (a, g), out in zip(pairs, outs):
        count = out.shape[0]
        for y in range(count):
            left = picked(ins[a], y, count, side)
            for j in range(0, out.shape[2], 512):
                stop = min(j + 512, out.shape[2])
                out[y, :, j:stop] = tn(left, ins[g][:, j:stop]).astype(bf16)


def scan_back_kernel(
    dy_ref, ycore_ref, x_ref, bc_ref, step_ref, cum_ref, cumt_ref, z_ref, off_ref, entry_ref,
    down_ref, skip_ref, dec_ref, chan_ref, cw_ref, cb_ref,
    dext_ref, dz_ref, dcw_ref, dcb_ref, heads_ref,
    xw_ref, ce_ref, dyb_ref, dxw_ref, dg_ref, dact_ref,
):
    rows = x_ref.shape[0]
    spread, gather = head_spread(), head_sum_matrix()
    off, cum = off_ref[...], cum_ref[...]
    step_wide = nn_full(step_ref[...], spread)
    xw_ref[...] = (x_ref[...] * step_wide).astype(bf16)
    dyb_ref[...] = dy_ref[...].astype(bf16)
    ce_ref[...] = nn_full(cum, spread)
    keys, reads = bc_ref[:, :STATE].astype(bf16), bc_ref[:, STATE:].astype(bf16)
    keep = scan_masks(off, rows)
    scores = jnp.where(keep, nt(reads, keys), 0.0)
    lane = iota((rows, LANES), 1)
    dg_ref[...] = jnp.zeros((rows, rows), f32)

    def pair(j, unused):
        cols = pl.ds(pl.multiple_of(j * LANES, LANES), LANES)
        wide = ce_ref[:, cols]
        xw, dy = xw_ref[:, cols], dyb_ref[:, cols]
        outs = []
        for k in range(2):
            late = wide[:, k * SSM_DIM : k * SSM_DIM + 1]
            early = cumt_ref[pl.ds(2 * j + k, 1), :]
            decay = jnp.exp(jnp.minimum(late - early, 0.0))
            outs.append(tn((decay * scores).astype(bf16), dy))
            own = (lane < SSM_DIM) if k == 0 else (lane >= SSM_DIM)
            dm = nt(jnp.where(own, dy.astype(f32), 0.0).astype(bf16), xw)
            dg_ref[...] += dm * decay
        dxw_ref[:, cols] = jnp.where(lane < SSM_DIM, outs[0], outs[1])
        return unused

    lax.fori_loop(0, SSM_HEADS // 2, pair, 0)
    dscores = jnp.where(keep, dg_ref[...], 0.0).astype(bf16)
    down = down_ref[...].astype(bf16)
    tail = nn_full(tail_of(cum, off), spread)
    fade = nn_full(fade_of(cum, off), spread)
    bd = nt(keys, down) * tail
    xw = xw_ref[...].astype(f32)
    dxw = dxw_ref[...] + bd
    dact_ref[:, DS : DS + STATE] = tn(dscores, reads) + nn((tail * xw).astype(bf16), down)
    dact_ref[:, DS + STATE :] = nn(dscores, keys) + nn(
        (fade * dy_ref[...]).astype(bf16), entry_ref[...].astype(bf16)
    )
    through = jnp.sum(nn_full(xw * bd, gather), axis=0, keepdims=True)
    product = nt(jnp.ones((8, STATE), f32), down_ref[...] * entry_ref[...])
    kept = nn_full(product, gather)[:1] * carry_of(cum, off)
    last = (iota((rows, 1), 0) == rows - 1).astype(f32)
    dyb = dyb_ref[...].astype(f32)
    dcum = nn_full(dyb * ycore_ref[...] - xw * dxw, gather) + last * (through + kept)
    tri = (iota((rows, rows), 0) <= iota((rows, rows), 1)).astype(f32)
    dlog = nn_full(tri, dcum)
    x = x_ref[...]
    step, dec = step_ref[...], dec_ref[...]
    dstep = nn_full(dxw * x, gather) - dlog * dec
    dz = dstep * sigmoid(z_ref[...])
    dz_ref[...] = dz
    heads_ref[...] = jnp.zeros(heads_ref.shape, f32)
    heads_ref[0:1, :] = jnp.sum(dlog * (-step * dec), axis=0, keepdims=True)
    heads_ref[1:2, :] = jnp.sum(dz, axis=0, keepdims=True)
    heads_ref[2:3, :] = jnp.sum(nn_full(dy_ref[...] * x, gather), axis=0, keepdims=True)
    dact_ref[:, :DS] = dxw * step_wide + skip_ref[...] * dy_ref[...]
    dcw_ref[...] = jnp.zeros(dcw_ref.shape, f32)
    for j in range(CONV_CH // 256):
        cols = slice(j * 256, (j + 1) * 256)
        taps = conv_taps(chan_ref, cols, off)
        mixed = cb_ref[:, cols]
        for i, tap in enumerate(taps):
            mixed = mixed + tap * cw_ref[i : i + 1, cols]
        sg = sigmoid(mixed)
        dmix = dact_ref[:, cols] * (sg * (1.0 + mixed * (1.0 - sg)))
        dcb_ref[:, cols] = jnp.sum(dmix, axis=0, keepdims=True)
        total = 0.0
        for i, tap in enumerate(taps):
            back = CONV - 1 - i
            dcw_ref[i : i + 1, cols] = jnp.sum(dmix * tap, axis=0, keepdims=True)
            part = dmix * ((off >= back).astype(f32) * cw_ref[i : i + 1, cols])
            part = jnp.concatenate([jnp.zeros((RIM, 256), f32), part], axis=0)
            total = total + (pltpu.roll(part, rows + RIM - back, 0) if back else part)
        dext_ref[:, cols] = total


def back_grads_kernel(count, dq_ref, own_ref, *refs):
    parts, rest = refs[:count], refs[count:]
    dext_ref, ret_ref, dz_ref, cos_ref, sin_ref, ga_ref, gb_ref = rest
    rows = dq_ref.shape[0]
    dkv = own_ref[...]
    for part in parts:
        dkv = dkv + part[...].astype(f32)
    ga_ref[:, :LANES] = turned_back(dkv[:, :LANES], cos_ref[...], sin_ref[...]).astype(bf16)
    ga_ref[:, LANES:256] = dkv[:, LANES:].astype(bf16)
    ga_ref[:, 256:768] = dq_ref[...]
    ga_ref[: rows - RIM, 768:1024] = dext_ref[RIM:rows, DS:].astype(bf16)
    ga_ref[rows - RIM :, 768:1024] = (dext_ref[rows:, DS:] + ret_ref[:, DS:]).astype(bf16)
    ga_ref[:, 1024:] = dz_ref[...].astype(bf16)
    gb_ref[: rows - RIM, :] = dext_ref[RIM:rows, :DS].astype(bf16)
    gb_ref[rows - RIM :, :] = (dext_ref[rows:, :DS] + ret_ref[:, :DS]).astype(bf16)


def back_kernel(
    core_ref, ga_ref, gb_ref, wa_own, wa_oth, wb_own, wb_oth, tok_ref, dmid_ref, dng_ref, gain_ref,
    dtok_ref, dgain_ref, dn_ref,
):
    core = core_ref[0]
    for y in range(wa_own.shape[0]):
        own = nt(ga_ref[...], wa_own[y]) + nt(gb_ref[...], wb_own[y])
        oth = nt(ga_ref[...], wa_oth[y]) + nt(gb_ref[...], wb_oth[y])
        put(dn_ref, y, own, oth, core)
    dn = dn_ref[...] + dng_ref[...]
    tok = tok_ref[...].astype(f32)
    rms = lax.rsqrt(jnp.mean(tok * tok, axis=1, keepdims=True) + EPS)
    unit = tok * rms
    dgain_ref[...] = jnp.sum(dn * unit, axis=0, keepdims=True)
    dn = dn * gain_ref[...]
    dtok_ref[...] = dmid_ref[...] + rms * (dn - unit * jnp.mean(dn * unit, axis=1, keepdims=True))


def run(kernel, name, outs, args, scalars=0, scratch=(), flops=0):
    moved = sum(a.size * a.dtype.itemsize for a in args)
    shapes = [jax.ShapeDtypeStruct(shape, kind) for shape, kind in outs]
    moved += sum(s.size * s.dtype.itemsize for s in shapes)
    specs = [pl.BlockSpec(memory_space=pltpu.SMEM)] * scalars
    specs += [pl.BlockSpec(memory_space=pltpu.VMEM)] * (len(args) - scalars)
    return pl.pallas_call(
        kernel,
        name=name,
        out_shape=shapes,
        in_specs=specs,
        out_specs=[pl.BlockSpec(memory_space=pltpu.VMEM)] * len(shapes),
        scratch_shapes=[pltpu.VMEM(shape, kind) for shape, kind in scratch],
        compiler_params=pltpu.CompilerParams(vmem_limit_bytes=60 * 2**20),
        cost_estimate=pl.CostEstimate(flops=flops, bytes_accessed=moved, transcendentals=0),
    )(*args)


def padded(vector, width):
    return jnp.pad(vector.astype(f32), (0, width - vector.shape[0]))[None, :]


def local(
    tokens, lengths, cotangent, mixer_gain, query_weight, keyval_weight, inner_weight, conv_weight,
    conv_bias, ssm_gain, attn_out_weight, ssm_out_weight, ffn_gain, gate_up_weight, down_weight,
    decay_log, step_bias, skip_gain,
):
    rows, width = tokens.shape
    seq_count, seq_rank = lax.axis_size("seq"), lax.axis_index("seq")
    side = place_on("core").reshape(1)
    back = (rows * seq_count // 2) // rows
    part = query_weight.shape[0]
    heads_width, ff = HEADS * HEAD_DIM, gate_up_weight.shape[1] // 2
    a_rows, s_rows, f_rows = attn_out_weight.shape[0], ssm_out_weight.shape[0], down_weight.shape[0]
    ys = lax.axis_size("dp") // 2

    rim = shifted(tokens[rows - RIM :], 1)
    small = jnp.concatenate(
        [mixer_gain, conv_weight.reshape(-1), conv_bias, ssm_gain, ffn_gain]
    ).astype(f32)
    counts = [mixer_gain.size, conv_weight.size, conv_bias.size, ssm_gain.size, ffn_gain.size]
    slots = -(-small.size // LANES) * LANES
    small = gather_small(jnp.pad(small, (0, slots - small.size)))
    inner_tail = inner_weight[:, DS + CONV_CH :]
    front_a = jnp.concatenate(
        [
            keyval_weight,
            query_weight,
            inner_weight[:, 2 * DS : DS + CONV_CH],
            jnp.pad(inner_tail, ((0, 0), (0, LANES - SSM_HEADS))),
        ],
        1,
    )
    wa_own, wa_oth = gather_pair(front_a, "y")
    wb_own, wb_oth = gather_pair(inner_weight[:, DS : 2 * DS], "x")
    gate_own, gate_oth = gather_pair(inner_weight[:, :DS], "y")
    gu_own, gu_oth = gather_pair(gate_up_weight, "y")
    middle = jnp.concatenate([down_weight, attn_out_weight, ssm_out_weight], 0)
    mids = gather_pair(middle, "x")

    def unpacked(full, start, size):
        full = full.reshape(ys, -1, middle.shape[0], width)[:, :, start : start + size]
        return full.reshape(ys, -1, width)

    down_own, down_oth = (unpacked(m, 0, f_rows) for m in mids)
    ao_own, ao_oth = (unpacked(m, f_rows, a_rows) for m in mids)
    so_own, so_oth = (unpacked(m, f_rows + a_rows, s_rows) for m in mids)

    starts = [sum(counts[:i]) for i in range(len(counts))]
    gain_one, w_conv, b_conv, gain_ssm, gain_two = (
        small[:, s : s + c].reshape(-1) for s, c in zip(starts, counts)
    )
    w_conv = jnp.pad(w_conv.reshape(CONV_CH, CONV).T, ((0, 8 - CONV), (0, 0)))
    gain_one, b_conv, gain_ssm, gain_two = (
        v[None, :] for v in (gain_one, b_conv, gain_ssm, gain_two)
    )
    places = seq_rank * rows + jnp.arange(rows)
    begin = jnp.zeros_like(places)
    end = jnp.int32(0)
    for i in range(lengths.shape[1]):
        end = end + lengths[0, i]
        begin = jnp.where(end <= places, end, begin)
    offset = (places - begin).astype(jnp.int32)
    half = HEAD_DIM // 2
    freq = BASE ** (-jnp.arange(half).astype(f32) / half)
    angle = offset.astype(f32)[:, None] * freq[None, :]
    cos = jnp.tile(jnp.cos(angle), (1, 4))
    sin = jnp.sin(angle)
    sin = jnp.tile(jnp.concatenate([-sin, sin], 1), (1, 2))
    off = offset[:, None]
    step_bias_row, decay_row = padded(step_bias, LANES), padded(jnp.exp(decay_log), LANES)
    skip = jnp.repeat(skip_gain, SSM_DIM)[None, :]

    (q8, kv, normed, chan, x, bc, step, cum, cumt, z, state, carry) = run(
        front_kernel,
        "front",
        [
            ((HEADS, rows, LANES), bf16),
            ((rows, 256), bf16),
            ((rows, width), bf16),
            ((rows + RIM, CONV_CH), bf16),
            ((rows, DS), f32),
            ((rows, 2 * STATE), f32),
            ((rows, LANES), f32),
            ((rows, LANES), f32),
            ((LANES, rows), f32),
            ((rows, LANES), f32),
            ((DS, STATE), f32),
            ((1, LANES), f32),
        ],
        (
            side, jnp.concatenate([rim, tokens], 0), gain_one, wa_own, wa_oth, wb_own, wb_oth,
            cos, sin, off, w_conv, b_conv, step_bias_row, decay_row,
        ),
        scalars=1,
        scratch=[((rows + RIM, width), bf16), ((rows, DS), bf16)],
        flops=2 * rows * width * (A_COLS + DS),
    )
    pieces = [shifted(kv, back - i) for i in range(back)] + [kv]
    entry = carried(state, carry, back, 1)
    window = (back + 1) * rows
    y_local = run(
        scan_kernel, "scan", [((rows, DS), f32)], (x, bc, step, cum, cumt, off),
        scratch=[((rows, DS), bf16), ((rows, DS), f32)], flops=2 * SSM_HEADS * rows * rows * 128,
    )[0]
    attended, lse = run(
        functools.partial(attend_kernel, back + 1),
        "attend",
        [((rows, heads_width), bf16), ((rows, LANES), f32)],
        (q8, *pieces, off),
        scratch=[
            ((window, LANES), bf16),
            ((window, LANES), bf16),
            ((rows, window), f32),
            ((HEADS, rows, LANES), f32),
        ],
        flops=4 * HEADS * rows * window * LANES,
    )
    (
        output, dmid, datt, dssd, ycore, dentry, n2, hidden, mixed, dbr, dgu, dgate, dng,
        g_ssm, g_ffn,
    ) = run(
        post_kernel,
        "post",
        [
            ((rows, width), bf16),
            ((rows, width), f32),
            ((rows, heads_width), bf16),
            ((rows, DS), f32),
            ((rows, DS), f32),
            ((DS, STATE), f32),
            ((rows, width), bf16),
            ((rows, ff), bf16),
            ((rows, DS), bf16),
            ((rows, width), bf16),
            ((rows, 2 * ff), bf16),
            ((rows, DS), bf16),
            ((rows, width), f32),
            ((1, DS), f32),
            ((1, width), f32),
        ],
        (
            side, tokens, cotangent, attended, y_local, x, bc, cum, off, entry, skip, normed,
            gain_ssm, gain_two, gate_own, gate_oth, ao_own, ao_oth, so_own, so_oth, gu_own, gu_oth,
            down_own, down_oth,
        ),
        scalars=1,
        scratch=[
            ((rows, DS), f32),
            ((rows, DS), f32),
            ((rows, width), f32),
            ((rows, 2 * ff), f32),
            ((rows, width), f32),
            ((rows, DS), f32),
            ((rows, DS), bf16),
        ],
        flops=4 * rows * width * (3 * ff + DS + DS + heads_width),
    )

    def weight_grads(which):
        pairs = [(0, 1), (2, 3), (4, 5), (6, 5), (7, 8)]
        made = run(
            functools.partial(products_kernel, pairs),
            "weights",
            [
                ((ys, width // 2 // ys, 2 * ff), bf16),
                ((ys, ff // 2 // ys, width), bf16),
                ((ys, heads_width // 2 // ys, width), bf16),
                ((ys, DS // 2 // ys, width), bf16),
                ((ys, width // 2 // ys, DS), bf16),
            ],
            (which, n2, dgu, hidden, cotangent, attended, dbr, mixed, normed, dgate),
            scalars=1,
            flops=rows * width * (3 * ff + DS + DS + heads_width),
        )
        packed = jnp.concatenate(
            [
                m.reshape(ys, -1, r, width)
                for m, r in zip(made[1:4], (f_rows, a_rows, s_rows))
            ],
            2,
        )
        return made[0], packed, made[4]

    core_unit = extents()["core"][0]
    downstream = carried(dentry, carry, back, -1)
    others = weight_grads(1 - side)
    got = [swap(a, core_unit) for a in others]
    owns = weight_grads(side)
    r_gu = reduce_pair(owns[0], got[0], part, "x")
    r_mid = reduce_pair(owns[1], got[1], middle.shape[0], "y")
    r_gate = reduce_pair(owns[2], got[2], part, "x")
    dq, dkv = run(
        functools.partial(attend_back_kernel, back + 1),
        "attend_back",
        [((rows, heads_width), bf16), ((window, 256), f32)],
        (q8, *pieces, off, lse, datt, cos, sin),
        scratch=[
            ((window, LANES), bf16),
            ((window, LANES), bf16),
            ((rows, window), f32),
            ((HEADS, rows, LANES), bf16),
            ((HEADS, rows, LANES), f32),
        ],
        flops=10 * HEADS * rows * window * LANES,
    )
    dkv = dkv.reshape(back + 1, rows, 256)
    returned_kv = [shifted(dkv[i].astype(bf16), i - back) for i in range(back)]
    dext, dz, g_conv, g_conv_bias, heads = run(
        scan_back_kernel,
        "scan_back",
        [
            ((rows + RIM, CONV_CH), f32),
            ((rows, LANES), f32),
            ((8, CONV_CH), f32),
            ((1, CONV_CH), f32),
            ((8, LANES), f32),
        ],
        (
            dssd, ycore, x, bc, step, cum, cumt, z, off, entry, downstream, skip, decay_row, chan,
            w_conv, b_conv,
        ),
        scratch=[
            ((rows, DS), bf16),
            ((rows, DS), f32),
            ((rows, DS), bf16),
            ((rows, DS), f32),
            ((rows, rows), f32),
            ((rows, CONV_CH), f32),
        ],
        flops=4 * SSM_HEADS * rows * rows * 128,
    )
    ret = shifted(dext[:RIM], -1)
    ga, gb = run(
        functools.partial(back_grads_kernel, back),
        "back_grads",
        [((rows, A_COLS), bf16), ((rows, DS), bf16)],
        (dq, dkv[back], *returned_kv, dext, ret, dz, cos, sin),
    )

    def front_grads(which):
        return run(
            functools.partial(products_kernel, [(0, 1), (0, 2)]),
            "front_weights",
            [((ys, width // 2 // ys, A_COLS), bf16), ((ys, width // 2 // ys, DS), bf16)],
            (which, normed, ga, gb),
            scalars=1,
            flops=rows * width * (A_COLS + DS),
        )

    others = front_grads(1 - side)
    got = [swap(a, core_unit) for a in others]
    owns = front_grads(side)
    r_a = reduce_pair(owns[0], got[0], part, "x")
    r_b = reduce_pair(owns[1], got[1], part, "y")
    grad_tokens, g_mixer = run(
        back_kernel,
        "back",
        [((rows, width), f32), ((1, width), f32)],
        (side, ga, gb, wa_own, wa_oth, wb_own, wb_oth, tokens, dmid, dng, gain_one),
        scalars=1,
        scratch=[((rows, width), f32)],
        flops=2 * rows * width * (A_COLS + DS),
    )
    vector = jnp.concatenate(
        [
            g_mixer.reshape(-1), g_conv[:CONV].T.reshape(-1), g_conv_bias.reshape(-1),
            g_ssm.reshape(-1), g_ffn.reshape(-1), heads[:3].reshape(-1),
        ]
    )
    vector = sum_small(vector.reshape(-1, LANES)).reshape(-1)
    me = my_index()
    small_out = []
    start = 0
    count = lax.axis_size("dp") * lax.axis_size("seq")
    for size in counts:
        small_out.append(lax.dynamic_slice_in_dim(vector, start + me * size, size, 0))
        start += count * size
    heads = vector[start:].reshape(3, LANES)[:, :SSM_HEADS]
    g_inner = jnp.concatenate([r_gate, r_b, r_a[:, 768 : 1024 + SSM_HEADS]], 1)
    return (
        output,
        grad_tokens,
        small_out[0],
        r_a[:, 256:768],
        r_a[:, :256],
        g_inner,
        small_out[1].reshape(-1, CONV),
        small_out[2],
        small_out[3],
        r_mid[f_rows : f_rows + a_rows],
        r_mid[f_rows + a_rows :],
        small_out[4],
        r_gu,
        r_mid[:f_rows],
        heads[0],
        heads[1],
        heads[2],
    )


def solution(mesh):
    lead, flat, rep = P(AXES, None), P(AXES), P()
    return jax.shard_map(
        local,
        mesh=mesh,
        in_specs=(
            lead, P("dp", None), lead, flat, lead, lead, lead, lead, flat, flat, lead, lead, flat,
            lead, lead, rep, rep, rep,
        ),
        out_specs=(
            lead, lead, flat, lead, lead, lead, lead, flat, flat, lead, lead, flat, lead, lead,
            rep, rep, rep,
        ),
        check_vma=False,
    )
```

time: 2120 us -> 668 us (0.32)
  waiting for transfers between devices: 1300 us -> 245 us
  blocking collectives: 238 us -> 0 us
  matrix products: 183 us -> 0 us
  local copies, waits for them, and re-layouts: 232 us -> 66.5 us
  starting transfers between devices: 6.51 us -> 149 us
  Pallas kernels: 0 us -> 135 us
  other arithmetic: 103 us -> 56 us
    reduce_scatter x8 -> x0, waiting for transfers between devices: 1060 us -> none  [the longest x1 360 us: local(): lax.psum_scatter(g_gate_up, ('dp', 'seq'), scatter_dimension=0, tiled=True)]
    ppermute x2 -> x87, waiting for transfers between devices: 3.13 us -> 245 us  [the longest x71 223 us: swap(): return lax.ppermute(array, AXES, [(i, i ^ mask) for i in range(count)])]
    all_gather x9 -> x0, waiting for transfers between devices: 235 us -> none  [the longest x1 76 us: local(): lax.all_gather(gate_up_weight, ('dp', 'seq'), axis=0, tiled=True)]
    dot_general x108 -> x0, matrix products: 183 us -> none  [the longest x70 99.5 us: bfloat_dot(): return multiply(left, right)]
    ppermute x2 -> x87, starting transfers between devices: 5.62 us -> 149 us  [the longest x71 107 us: swap(): return lax.ppermute(array, AXES, [(i, i ^ mask) for i in range(count)])]
    all_gather x2 -> x0, blocking collectives: 135 us -> none  [the longest x1 71.4 us: local(): lax.all_gather(keyval_weight, ('dp', 'seq'), axis=0, tiled=True)]
    pallas_call x0 -> x12, Pallas kernels: none -> 135 us  [run(): pl.pallas_call(kernel, name=name, out_shape=shapes, in_specs=specs, out_s...]
    unnamed x3 -> x0, blocking collectives: 103 us -> none
  transfers between devices with their start and end apart: 19 -> 87, of which waited for: 13 -> 27; matrix products, arithmetic and copies ran while one was open for 19% -> 16% of each run, Pallas kernels for 0% -> 16%
where the time goes in v1:
time: 668 us; the launch traced here: 657 us
  waiting for transfers between devices  245 us (37%)
  starting transfers between devices  149 us (22%)
  Pallas kernels  135 us (20%)
  local copies, waits for them, and re-layouts  66.5 us (10%)
  other arithmetic  56 us (8%)
    ppermute x71, waiting for transfers between devices, swap(): return lax.ppermute(array, AXES, [(i, i ^ mask) for i in range(count)])  223 us
    pallas_call x12, Pallas kernels, run(): pl.pallas_call(kernel, name=name, out_shape=shapes, in_specs=specs, out_s...  135 us
    ppermute x71, starting transfers between devices, swap(): return lax.ppermute(array, AXES, [(i, i ^ mask) for i in range(count)])  107 us
    ppermute x16, starting transfers between devices, shifted(): return lax.ppermute(array, 'seq', pairs)  42.7 us
    ppermute x16, waiting for transfers between devices, shifted(): return lax.ppermute(array, 'seq', pairs)  21.5 us
  transfers between devices with their start and end apart: 87, of which 27 were waited for; matrix products, arithmetic and copies ran while one was open for 16% of the time, Pallas kernels for 16%

profile of v1, /device:TPU:0, one launch (start us, length us, event | category | flops | bytes accessed | tf_op | source)
XLA Modules:
  0.0 656.6 jit_solution(123755903029995368)
XLA Ops:
  58.2 9.7 %collective-permute-done.13 = bf16[32,1536]{1,0:T(8,128)(2,1)S(1)} collective-permute-done((bf16[32,1536]{1,0:T(8,128)(2,1)S(1)}, bf16[32,1536]{1,0:T(8,128)(2,1)S(1)}, u32[]{:S(2)}, u32[]{:S(2)}) %collective-permute-start.13) | collective-permute-done | bytes 98336 | tf_op jit(solution)/shard_map/ppermute | solution.py:84
  67.8 13.1 %collective-permute-start.34 = (bf16[128,1024]{1,0:T(8,128)(2,1)S(1)}, bf16[128,1024]{1,0:T(8,128)(2,1)S(1)}, u32[]{:S(2)}, u32[]{:S(2)}) collective-permute-start(bf16[128,1024]{1,0:T(8,128)(2,1)S(1)} %constant_dynamic-update-slice_fusion), channel_id=1, source_target_pairs={{0,2},{1,3},{2,0},{3,1},{4,6},{5,7},{6,4},{7,5},{8,10},{9,11},{10,... | collective-permute-start | bytes 786440 | tf_op jit(solution)/shard_map/ppermute | solution.py:84
  88.1 6.8 %collective-permute-done.34 = bf16[128,1024]{1,0:T(8,128)(2,1)S(1)} collective-permute-done((bf16[128,1024]{1,0:T(8,128)(2,1)S(1)}, bf16[128,1024]{1,0:T(8,128)(2,1)S(1)}, u32[]{:S(2)}, u32[]{:S(2)}) %collective-permute-start.34) | collective-permute-done | bytes 262176 | tf_op jit(solution)/shard_map/ppermute | solution.py:84
  97.0 7.0 %collective-permute-done.39 = bf16[32,4096]{1,0:T(8,128)(2,1)S(1)} collective-permute-done((bf16[32,4096]{1,0:T(8,128)(2,1)S(1)}, bf16[32,4096]{1,0:T(8,128)(2,1)S(1)}, u32[]{:S(2)}, u32[]{:S(2)}) %collective-permute-start.39) | collective-permute-done | bytes 262176 | tf_op jit(solution)/shard_map/ppermute | solution.py:84
  110.2 32.5 %collective-permute-done.11 = bf16[2,4,32,1152]{3,2,1,0:T(8,128)(2,1)S(1)} collective-permute-done((bf16[2,4,32,1152]{3,2,1,0:T(8,128)(2,1)S(1)}, bf16[2,4,32,1152]{3,2,1,0:T(8,128)(2,1)S(1)}, u32[]{:S(2)}, u32[]{:S(2)}) %collective-permute-start.11) | collective-permute-done | bytes 589856 | tf_op jit(solution)/shard_map/ppermute | solution.py:84
  147.8 11.7 %collective-permute-done.30 = bf16[2,4,32,1536]{3,2,1,0:T(8,128)(2,1)S(1)} collective-permute-done((bf16[2,4,32,1536]{3,2,1,0:T(8,128)(2,1)S(1)}, bf16[2,4,32,1536]{3,2,1,0:T(8,128)(2,1)S(1)}, u32[]{:S(2)}, u32[]{:S(2)}) %collective-permute-start.30) | collective-permute-done | bytes 786464 | tf_op jit(solution)/shard_map/ppermute | solution.py:84
  161.9 30.7 %collective-permute-done.36 = bf16[4,2,128,1024]{3,2,1,0:T(8,128)(2,1)S(1)} collective-permute-done((bf16[4,2,128,1024]{3,2,1,0:T(8,128)(2,1)S(1)}, bf16[4,2,128,1024]{3,2,1,0:T(8,128)(2,1)S(1)}, u32[]{:S(2)}, u32[]{:S(2)}) %collective-permute-start.36) | collective-permute-done | bytes 2097184 | tf_op jit(solution)/shard_map/ppermute | solution.py:84
  208.0 8.0 %front.1 = (bf16[8,256,128]{2,1,0:T(8,128)(2,1)}, bf16[256,256]{1,0:T(8,128)(2,1)}, bf16[256,1024]{1,0:T(8,128)(2,1)}, bf16[272,1792]{1,0:T(8,128)(2,1)}, f32[25...) custom-call(s32[1]{0:T(128)} %bitcast.core_ref.side_ref, ...), custom_call_target="tpu_custom_call" | custom-call | flops 1409286144 | bytes 11695620 | tf_op jit(solution)/shard_map/front/pallas_call | solution.py:683
  231.1 6.8 %collective-permute-start.20 = (bf16[256,256]{1,0:T(8,128)(2,1)}, bf16[256,256]{1,0:T(8,128)(2,1)S(1)}, u32[]{:S(2)}, u32[]{:S(2)}) collective-permute-start(bf16[256,256]{1,0:T(8,128)(2,1)} %get-tuple-element.72.refs_4_), channel_id=1, source_target_pairs={{0,3},{1,4},{2,5},{3,6},{4,7},{8,11},{9,12},{10,13},{11,14},{12,15... | collective-permute-start | bytes 393224 | tf_op jit(solution)/shard_map/ppermute | solution.py:151
  256.1 9.1 %scan.1.yl_ref = f32[256,1536]{1,0:T(8,128)} custom-call(f32[256,1536]{1,0:T(8,128)} %get-tuple-element.74.x_ref, f32[256,256]{1,0:T(8,128)} %get-tuple-element.75.bc_ref, f32[256,128]{1,0:T(8,128)} %get-tuple-element.76.step_ref, f32[256,128]{1,0:T(8,128)} %get-tuple-element.77.cum_ref, f32[128,256]{1,0:T(8,128)} %get-tuple-element.78.cumt_ref, ...), custom_call_target="tpu_custom_call" | custom-call | flops 402653184 | bytes 3802112 | tf_op jit(solution)/shard_map/scan/pallas_call | solution.py:683
  265.2 10.2 %attend.1 = (bf16[256,512]{1,0:T(8,128)(2,1)}, f32[256,128]{1,0:T(8,128)}) custom-call(bf16[8,256,128]{2,1,0:T(8,128)(2,1)} %get-tuple-element.71.q8_ref, bf16[256,256]{1,0:T(8,128)(2,1)} %collective-permute-done.19.refs_0_, bf16[256,256]{1,0:T(8,128)(2,1)} %copy-done.33, bf16[256,256]{1,0:T(8,128)(2,1)} %collective-permute-done.21.refs_2_, ...), custom_call_target="tpu_custom_call" | custom-call | flops 1342177280 | bytes 1573888 | tf_op jit(solution)/shard_map/attend/pallas_call | solution.py:683
  306.0 29.8 %post.1 = (bf16[256,1024]{1,0:T(8,128)(2,1)}, f32[256,1024]{1,0:T(8,128)}, bf16[256,512]{1,0:T(8,128)(2,1)}, f32[256,1536]{1,0:T(8,128)}, f32[256,1536]{1,0:T(8,...) custom-call(s32[1]{0:T(128)} %bitcast.core_ref.side_ref, ...), custom_call_target="tpu_custom_call" | custom-call | flops 10200547328 | bytes 38693892 | tf_op jit(solution)/shard_map/post/pallas_call | solution.py:683
  338.5 10.0 %collective-permute-done.48 = bf16[1552,128]{1,0:T(8,128)(2,1)S(1)} collective-permute-done((bf16[1552,128]{1,0:T(8,128)(2,1)S(1)}, bf16[1552,128]{1,0:T(8,128)(2,1)S(1)}, u32[]{:S(2)}, u32[]{:S(2)}) %collective-permute-start.48) | collective-permute-done | bytes 397344 | tf_op jit(solution)/shard_map/ppermute | solution.py:151
  350.2 14.6 %attend_back.1 = (bf16[256,512]{1,0:T(8,128)(2,1)}, f32[1280,256]{1,0:T(8,128)}) custom-call(bf16[8,256,128]{2,1,0:T(8,128)(2,1)} %get-tuple-element.71.q8_ref, bf16[256,256]{1,0:T(8,128)(2,1)} %collective-permute-done.19.refs_0_, bf16[256,256]{1,0:T(8,128)(2,1)} %copy-done.33, bf16[256,256]{1,0:T(8,128)(2,1)} %collective-permute-done.21.refs_2_, ...), custom_call_target="tpu_custom_call" | custom-call | flops 3355443200 | bytes 3408896 | tf_op jit(solution)/shard_map/attend_back/pallas_call | solution.py:683
  376.4 8.1 %weights.3 = (bf16[2,256,4096]{2,1,0:T(8,128)(2,1)}, bf16[2,512,1024]{2,1,0:T(8,128)(2,1)}, bf16[2,128,1024]{2,1,0:T(8,128)(2,1)}, bf16[2,384,1024]{2,1,0:T(8,128)(2,1)}, bf16[2,256,1536]{2,1,0:T(8,128)(2,1)}) custom-call(s32[1]{0:T(128)S(6)} %sub.94.side_ref, bf16[256,1024]{1,0:T(8,128)(2,1)} %get-tuple-element.107.refs_0_, ...), custom_call_target="tpu_custom_call" | custom-call | flops 2550136832 | bytes 17039364 | tf_op jit(solution)/shard_map/weights/pallas_call | solution.py:683
  385.5 29.8 %scan_back.1 = (f32[272,1792]{1,0:T(8,128)}, f32[256,128]{1,0:T(8,128)}, f32[8,1792]{1,0:T(8,128)}, f32[1,1792]{1,0:T(1,128)}, f32[8,128]{1,0:T(8,128)}) custom-call(f32[256,1536]{1,0:T(8,128)} %get-tuple-element.87.dy_ref, f32[256,1536]{1,0:T(8,128)} %get-tuple-element.88.ycore_ref, f32[256,1536]{1,0:T(8,128)} %get-tuple-element.74.x_ref, ...), custom_call_target="tpu_custom_call" | custom-call | flops 805306368 | bytes 10274304 | tf_op jit(solution)/shard_map/scan_back/pallas_call | solution.py:683
  440.8 8.0 %weights.2 = (bf16[2,256,4096]{2,1,0:T(8,128)(2,1)}, bf16[2,512,1024]{2,1,0:T(8,128)(2,1)}, bf16[2,128,1024]{2,1,0:T(8,128)(2,1)}, bf16[2,384,1024]{2,1,0:T(8,128)(2,1)}, bf16[2,256,1536]{2,1,0:T(8,128)(2,1)}) custom-call(s32[1]{0:T(128)} %bitcast.core_ref.side_ref, bf16[256,1024]{1,0:T(8,128)(2,1)} %get-tuple-element.107.refs_0_, ...), custom_call_target="tpu_custom_call" | custom-call | flops 2550136832 | bytes 17039364 | tf_op jit(solution)/shard_map/weights/pallas_call | solution.py:683
  482.5 8.6 %collective-permute-done.65 = bf16[4,32,1536]{2,1,0:T(8,128)(2,1)S(1)} collective-permute-done((bf16[4,32,1536]{2,1,0:T(8,128)(2,1)S(1)}, bf16[4,32,1536]{2,1,0:T(8,128)(2,1)S(1)}, u32[]{:S(2)}, u32[]{:S(2)}) %collective-permute-start.65) | collective-permute-done | bytes 393248 | tf_op jit(solution)/shard_map/ppermute | solution.py:84
  506.4 16.2 %collective-permute-done.70 = bf16[4,2,32,1536]{3,2,0,1:T(8,128)(2,1)S(1)} collective-permute-done((bf16[4,2,32,1536]{3,2,0,1:T(8,128)(2,1)S(1)}, bf16[4,2,32,1536]{3,2,0,1:T(8,128)(2,1)S(1)}, u32[]{:S(2)}, u32[]{:S(2)}) %collective-permute-start.70) | collective-permute-done | bytes 786464 | tf_op jit(solution)/shard_map/ppermute | solution.py:84
  538.3 48.4 %collective-permute-done.71 = bf16[4,32,1536]{2,1,0:T(8,128)(2,1)S(1)} collective-permute-done((bf16[4,32,1536]{2,1,0:T(8,128)(2,1)S(1)}, bf16[4,32,1536]{2,1,0:T(8,128)(2,1)S(1)}, u32[]{:S(2)}, u32[]{:S(2)}) %collective-permute-start.71) | collective-permute-done | bytes 393248 | tf_op jit(solution)/shard_map/ppermute | solution.py:84
  600.7 11.1 %collective-permute-done.77 = bf16[4,128,1024]{2,1,0:T(8,128)(2,1)S(1)} collective-permute-done((bf16[4,128,1024]{2,1,0:T(8,128)(2,1)S(1)}, bf16[4,128,1024]{2,1,0:T(8,128)(2,1)S(1)}, u32[]{:S(2)}, u32[]{:S(2)}) %collective-permute-start.77) | collective-permute-done | bytes 1048608 | tf_op jit(solution)/shard_map/ppermute | solution.py:84
  623.4 11.6 %collective-permute-start.84 = (bf16[32,4096]{1,0:T(8,128)(2,1)S(1)}, bf16[32,4096]{1,0:T(8,128)(2,1)S(1)}, u32[]{:S(2)}, u32[]{:S(2)}) collective-permute-start(bf16[32,4096]{1,0:T(8,128)(2,1)S(1)} %get-tuple-element.150), channel_id=1, source_target_pairs={{0,2},{1,3},{2,0},{3,1},{4,6},{5,7},{6,4},{7,5},{8,10},{9,11},{10,... | collective-permute-start | bytes 786440 | tf_op jit(solution)/shard_map/ppermute | solution.py:84
  635.8 9.9 %collective-permute-done.79 = bf16[128,1024]{1,0:T(8,128)(2,1)S(1)} collective-permute-done((bf16[128,1024]{1,0:T(8,128)(2,1)S(1)}, bf16[128,1024]{1,0:T(8,128)(2,1)S(1)}, u32[]{:S(2)}, u32[]{:S(2)}) %collective-permute-start.79) | collective-permute-done | bytes 262176 | tf_op jit(solution)/shard_map/ppermute | solution.py:84
  647.9 7.4 %collective-permute-done.85 = bf16[32,4096]{1,0:T(8,128)(2,1)S(1)} collective-permute-done((bf16[32,4096]{1,0:T(8,128)(2,1)S(1)}, bf16[32,4096]{1,0:T(8,128)(2,1)S(1)}, u32[]{:S(2)}, u32[]{:S(2)}) %collective-permute-start.85) | collective-permute-done | bytes 262176 | tf_op jit(solution)/shard_map/ppermute | solution.py:84
  (429 shorter events, 292.3 us)
Async XLA Ops:
  50.8 35.8 %collective-permute-start.33 = (bf16[128,1024]{1,0:T(8,128)(2,1)S(1)}, bf16[128,1024]{1,0:T(8,128)(2,1)S(1)}, u32[]{:S(2)}, u32[]{:S(2)}) collective-permute-start(bf16[128,1024]{1,0:T(8,128)(2,1)S(1)} %constant_dynamic-update-slice_fusion), channel_id=1, source_target_pairs={{0,4},{1,5},{2,6},{3,7},{4,0},{5,1},{6,2},{7,3},{8,12},{9,13},{10,... | collective-permute-start | bytes 786440 | tf_op jit(solution)/shard_map/ppermute | solution.py:84
  103.9 40.2 %collective-permute-start.35 = (bf16[4,128,1024]{2,1,0:T(8,128)(2,1)S(1)}, bf16[4,128,1024]{2,1,0:T(8,128)(2,1)S(1)}, u32[]{:S(2)}, u32[]{:S(2)}) collective-permute-start(bf16[4,128,1024]{2,1,0:T(8,128)(2,1)S(1)} %pad_maximum_fusion.11), channel_id=1, source_target_pairs={{0,1},{1,0},{2,3},{3,2},{4,5},{5,4},{6,7},{7,6},{8,9},{9,8},{10,11... | collective-permute-start | bytes 3145736 | tf_op jit(solution)/shard_map/ppermute | solution.py:84
  105.4 40.7 %collective-permute-start.41 = (bf16[4,32,4096]{2,1,0:T(8,128)(2,1)S(1)}, bf16[4,32,4096]{2,1,0:T(8,128)(2,1)S(1)}, u32[]{:S(2)}, u32[]{:S(2)}) collective-permute-start(bf16[4,32,4096]{2,1,0:T(8,128)(2,1)S(1)} %pad_maximum_fusion.12), channel_id=1, source_target_pairs={{0,16},{1,17},{2,18},{3,19},{4,20},{5,21},{6,22},{7,23},{8,24},{9,... | collective-permute-start | bytes 3145736 | tf_op jit(solution)/shard_map/ppermute | solution.py:84
  108.2 51.3 %collective-permute-start.30 = (bf16[2,4,32,1536]{3,2,1,0:T(8,128)(2,1)S(1)}, bf16[2,4,32,1536]{3,2,1,0:T(8,128)(2,1)S(1)}, u32[]{:S(2)}, u32[]{:S(2)}) collective-permute-start(bf16[2,4,32,1536]{3,2,1,0:T(8,128)(2,1)S(1)} %pad_maximum_fusion.14), channel_id=1, source_target_pairs={{0,1},{1,0},{2,3},{3,2},{4,5},{5,4},{6,7},{7,6},{8,9},{9,8},{10,11... | collective-permute-start | bytes 2359304 | tf_op jit(solution)/shard_map/ppermute | solution.py:84
  109.6 51.3 %collective-permute-start.17 = (bf16[4,2,32,1536]{3,2,0,1:T(8,128)(2,1)S(1)}, bf16[4,2,32,1536]{3,2,0,1:T(8,128)(2,1)S(1)}, u32[]{:S(2)}, u32[]{:S(2)}) collective-permute-start(bf16[4,2,32,1536]{3,2,0,1:T(8,128)(2,1)S(1)} %pad_maximum_fusion.13), channel_id=1, source_target_pairs={{0,16},{1,17},{2,18},{3,19},{4,20},{5,21},{6,22},{7,23},{8,24},{9,... | collective-permute-start | bytes 2359304 | tf_op jit(solution)/shard_map/ppermute | solution.py:84
  144.1 61.4 %collective-permute-start.12 = (bf16[2,4,2,32,1152]{4,3,1,0,2:T(8,128)(2,1)S(1)}, bf16[2,4,2,32,1152]{4,3,1,0,2:T(8,128)(2,1)S(1)}, u32[]{:S(2)}, u32[]{:S(2)}) collective-permute-start(bf16[2,4,2,32,1152]{4,3,1,0,2:T(8,128)(2,1)S(1)} %pad_maximum_fusion.10), channel_id=1, source_target_pairs={{0,8},{1,9},{2,10},{3,11},{4,12},{5,13},{6,14},{7,15},{8,0},{9,1},... | collective-permute-start | bytes 3538952 | tf_op jit(solution)/shard_map/ppermute | solution.py:84
  144.5 48.1 %collective-permute-start.36 = (bf16[4,2,128,1024]{3,2,1,0:T(8,128)(2,1)S(1)}, bf16[4,2,128,1024]{3,2,1,0:T(8,128)(2,1)S(1)}, u32[]{:S(2)}, u32[]{:S(2)}) collective-permute-start(bf16[4,2,128,1024]{3,2,1,0:T(8,128)(2,1)S(1)} %pad_maximum_fusion.4), channel_id=1, source_target_pairs={{0,16},{1,17},{2,18},{3,19},{4,20},{5,21},{6,22},{7,23},{8,24},{9,... | collective-permute-start | bytes 6291464 | tf_op jit(solution)/shard_map/ppermute | solution.py:84
  146.5 54.9 %collective-permute-start.42 = (bf16[2,4,32,4096]{3,2,1,0:T(8,128)(2,1)S(1)}, bf16[2,4,32,4096]{3,2,1,0:T(8,128)(2,1)S(1)}, u32[]{:S(2)}, u32[]{:S(2)}) collective-permute-start(bf16[2,4,32,4096]{3,2,1,0:T(8,128)(2,1)S(1)} %pad_maximum_fusion.5), channel_id=1, source_target_pairs={{0,1},{1,0},{2,3},{3,2},{4,5},{5,4},{6,7},{7,6},{8,9},{9,8},{10,11... | collective-permute-start | bytes 6291464 | tf_op jit(solution)/shard_map/ppermute | solution.py:84
  161.0 77.9 %collective-permute-start.31 = (bf16[2,4,2,32,1536]{4,3,1,0,2:T(8,128)(2,1)}, bf16[2,4,2,32,1536]{4,3,1,0,2:T(8,128)(2,1)}, u32[]{:S(2)}, u32[]{:S(2)}) collective-permute-start(bf16[2,4,2,32,1536]{4,3,1,0,2:T(8,128)(2,1)} %pad_maximum_fusion.9), channel_id=1, source_target_pairs={{0,8},{1,9},{2,10},{3,11},{4,12},{5,13},{6,14},{7,15},{8,0},{9,1},... | collective-permute-start | bytes 4718600 | tf_op jit(solution)/shard_map/ppermute | solution.py:84
  161.4 45.4 %collective-permute-start.18 = (bf16[2,4,2,32,1536]{4,3,1,2,0:T(8,128)(2,1)S(1)}, bf16[2,4,2,32,1536]{4,3,1,2,0:T(8,128)(2,1)S(1)}, u32[]{:S(2)}, u32[]{:S(2)}) collective-permute-start(bf16[2,4,2,32,1536]{4,3,1,2,0:T(8,128)(2,1)S(1)} %pad_maximum_fusion.8), channel_id=1, source_target_pairs={{0,8},{1,9},{2,10},{3,11},{4,12},{5,13},{6,14},{7,15},{8,0},{9,1},... | collective-permute-start | bytes 4718600 | tf_op jit(solution)/shard_map/ppermute | solution.py:84
  195.6 98.0 %collective-permute-start.37 = (bf16[2,4,2,128,1024]{4,3,2,1,0:T(8,128)(2,1)}, bf16[2,4,2,128,1024]{4,3,2,1,0:T(8,128)(2,1)}, u32[]{:S(2)}, u32[]{:S(2)}) collective-permute-start(bf16[2,4,2,128,1024]{4,3,2,1,0:T(8,128)(2,1)} %pad_maximum_fusion), channel_id=1, source_target_pairs={{0,8},{1,9},{2,10},{3,11},{4,12},{5,13},{6,14},{7,15},{8,0},{9,1},... | collective-permute-start | bytes 12582920 | tf_op jit(solution)/shard_map/ppermute | solution.py:84
  204.1 97.2 %collective-permute-start.43 = (bf16[2,4,2,32,4096]{4,3,1,0,2:T(8,128)(2,1)}, bf16[2,4,2,32,4096]{4,3,1,0,2:T(8,128)(2,1)}, u32[]{:S(2)}, u32[]{:S(2)}) collective-permute-start(bf16[2,4,2,32,4096]{4,3,1,0,2:T(8,128)(2,1)} %pad_maximum_fusion.1), channel_id=1, source_target_pairs={{0,8},{1,9},{2,10},{3,11},{4,12},{5,13},{6,14},{7,15},{8,0},{9,1},... | collective-permute-start | bytes 12582920 | tf_op jit(solution)/shard_map/ppermute | solution.py:84
  369.9 46.3 %collective-permute-start.44 = (bf16[256,256]{1,0:T(8,128)(2,1)S(1)}, bf16[256,256]{1,0:T(8,128)(2,1)S(1)}, u32[]{:S(2)}, u32[]{:S(2)}) collective-permute-start(bf16[256,256]{1,0:T(8,128)(2,1)S(1)} %get-tuple-element.187), channel_id=1, source_target_pairs={{4,0},{5,1},{6,2},{7,3},{12,8},{13,9},{14,10},{15,11},{20,16},{21,... | collective-permute-start | bytes 393224 | tf_op jit(solution)/shard_map/ppermute | solution.py:151
  371.2 48.7 %collective-permute-start.45 = (bf16[256,256]{1,0:T(8,128)(2,1)S(1)}, bf16[256,256]{1,0:T(8,128)(2,1)S(1)}, u32[]{:S(2)}, u32[]{:S(2)}) collective-permute-start(bf16[256,256]{1,0:T(8,128)(2,1)S(1)} %get-tuple-element.186), channel_id=1, source_target_pairs={{3,0},{4,1},{5,2},{6,3},{7,4},{11,8},{12,9},{13,10},{14,11},{15,12... | collective-permute-start | bytes 393224 | tf_op jit(solution)/shard_map/ppermute | solution.py:151
  372.5 47.5 %collective-permute-start.46 = (bf16[256,256]{1,0:T(8,128)(2,1)S(1)}, bf16[256,256]{1,0:T(8,128)(2,1)S(1)}, u32[]{:S(2)}, u32[]{:S(2)}) collective-permute-start(bf16[256,256]{1,0:T(8,128)(2,1)S(1)} %get-tuple-element.185), channel_id=1, source_target_pairs={{2,0},{3,1},{4,2},{5,3},{6,4},{7,5},{10,8},{11,9},{12,10},{13,11},... | collective-permute-start | bytes 393224 | tf_op jit(solution)/shard_map/ppermute | solution.py:151
  373.8 46.2 %collective-permute-start.47 = (bf16[256,256]{1,0:T(8,128)(2,1)S(1)}, bf16[256,256]{1,0:T(8,128)(2,1)}, u32[]{:S(2)}, u32[]{:S(2)}) collective-permute-start(bf16[256,256]{1,0:T(8,128)(2,1)S(1)} %get-tuple-element.184), channel_id=1, source_target_pairs={{1,0},{2,1},{3,2},{4,3},{5,4},{6,5},{7,6},{9,8},{10,9},{11,10},{12... | collective-permute-start | bytes 393224 | tf_op jit(solution)/shard_map/ppermute | solution.py:151
  384.5 68.2 %collective-permute-start.63 = (bf16[2,256,1536]{2,1,0:T(8,128)(2,1)}, bf16[2,256,1536]{2,1,0:T(8,128)(2,1)S(1)}, u32[]{:S(2)}, u32[]{:S(2)}) collective-permute-start(bf16[2,256,1536]{2,1,0:T(8,128)(2,1)} %get-tuple-element.114), channel_id=1, source_target_pairs={{0,8},{1,9},{2,10},{3,11},{4,12},{5,13},{6,14},{7,15},{8,0},{9,1},... | collective-permute-start | bytes 4718600 | tf_op jit(solution)/shard_map/ppermute | solution.py:84
  469.2 53.6 %collective-permute-start.75 = (bf16[2,8,128,1024]{3,2,1,0:T(8,128)(2,1)}, bf16[2,8,128,1024]{3,2,1,0:T(8,128)(2,1)}, u32[]{:S(2)}, u32[]{:S(2)}) collective-permute-start(bf16[2,8,128,1024]{3,2,1,0:T(8,128)(2,1)} %pad_maximum_fusion.2), channel_id=1, source_target_pairs={{0,8},{1,9},{2,10},{3,11},{4,12},{5,13},{6,14},{7,15},{8,0},{9,1},... | collective-permute-start | bytes 12582920 | tf_op jit(solution)/shard_map/ppermute | solution.py:84
  469.2 59.3 %collective-permute-start.81 = (bf16[2,256,4096]{2,1,0:T(8,128)(2,1)}, bf16[2,256,4096]{2,1,0:T(8,128)(2,1)}, u32[]{:S(2)}, u32[]{:S(2)}) collective-permute-start(bf16[2,256,4096]{2,1,0:T(8,128)(2,1)} %get-tuple-element.124), channel_id=1, source_target_pairs={{0,8},{1,9},{2,10},{3,11},{4,12},{5,13},{6,14},{7,15},{8,0},{9,1},... | collective-permute-start | bytes 12582920 | tf_op jit(solution)/shard_map/ppermute | solution.py:84
  528.0 58.9 %collective-permute-start.76 = (bf16[4,2,128,1024]{3,2,1,0:T(8,128)(2,1)}, bf16[4,2,128,1024]{3,2,1,0:T(8,128)(2,1)}, u32[]{:S(2)}, u32[]{:S(2)}) collective-permute-start(bf16[4,2,128,1024]{3,2,1,0:T(8,128)(2,1)} %fusion), channel_id=1, source_target_pairs={{0,16},{1,17},{2,18},{3,19},{4,20},{5,21},{6,22},{7,23},{8,24},{9,... | collective-permute-start | bytes 6291464 | tf_op jit(solution)/shard_map/ppermute | solution.py:84
  533.2 57.4 %collective-permute-start.82 = (bf16[2,4,32,4096]{3,2,1,0:T(8,128)(2,1)S(1)}, bf16[2,4,32,4096]{3,2,1,0:T(8,128)(2,1)S(1)}, u32[]{:S(2)}, u32[]{:S(2)}) collective-permute-start(bf16[2,4,32,4096]{3,2,1,0:T(8,128)(2,1)S(1)} %fusion.1), channel_id=1, source_target_pairs={{0,1},{1,0},{2,3},{3,2},{4,5},{5,4},{6,7},{7,6},{8,9},{9,8},{10,11... | collective-permute-start | bytes 6291464 | tf_op jit(solution)/shard_map/ppermute | solution.py:84
  535.4 51.3 %collective-permute-start.71 = (bf16[4,32,1536]{2,1,0:T(8,128)(2,1)S(1)}, bf16[4,32,1536]{2,1,0:T(8,128)(2,1)S(1)}, u32[]{:S(2)}, u32[]{:S(2)}) collective-permute-start(bf16[4,32,1536]{2,1,0:T(8,128)(2,1)S(1)} %fusion.26), channel_id=1, source_target_pairs={{0,1},{1,0},{2,3},{3,2},{4,5},{5,4},{6,7},{7,6},{8,9},{9,8},{10,11... | collective-permute-start | bytes 1179656 | tf_op jit(solution)/shard_map/ppermute | solution.py:84
  536.6 56.4 %collective-permute-start.62 = (bf16[32,1152]{1,0:T(8,128)(2,1)S(1)}, bf16[32,1152]{1,0:T(8,128)(2,1)S(1)}, u32[]{:S(2)}, u32[]{:S(2)}) collective-permute-start(bf16[32,1152]{1,0:T(8,128)(2,1)S(1)} %get-tuple-element.189), channel_id=1, source_target_pairs={{0,6},{1,7},{2,4},{3,5},{4,2},{5,3},{6,0},{7,1},{8,14},{9,15},{10,... | collective-permute-start | bytes 221192 | tf_op jit(solution)/shard_map/ppermute | solution.py:84
  538.3 57.1 %collective-permute-start.61 = (bf16[32,1152]{1,0:T(8,128)(2,1)S(1)}, bf16[32,1152]{1,0:T(8,128)(2,1)S(1)}, u32[]{:S(2)}, u32[]{:S(2)}) collective-permute-start(bf16[32,1152]{1,0:T(8,128)(2,1)S(1)} %get-tuple-element.190), channel_id=1, source_target_pairs={{0,4},{1,5},{2,6},{3,7},{4,0},{5,1},{6,2},{7,3},{8,12},{9,13},{10,... | collective-permute-start | bytes 221192 | tf_op jit(solution)/shard_map/ppermute | solution.py:84
  (98 other events, 1541.5 us)

commit v2 on v1

v2 whole, which is shorter than its diff:
```python
import functools

import jax
import jax.numpy as jnp
from jax import lax
from jax.experimental import pallas as pl
from jax.experimental.pallas import tpu as pltpu
from jax.sharding import PartitionSpec as P

HEADS = 8
KV_HEADS = 2
HEAD_DIM = 64
SSM_HEADS = 24
SSM_DIM = 64
STATE = 128
CONV = 4
DS = 1536
CONV_CH = 1792
RIM = 16
LANES = 128
A_COLS = 2 * KV_HEADS * HEAD_DIM + HEADS * HEAD_DIM + 2 * STATE + LANES
EPS = 1e-6
BASE = 10000.0
NEG = -1e30
AXES = ("y", "core", "z", "x")
SEQ = AXES[2:]

f32 = jnp.float32
bf16 = jnp.bfloat16


def nn(a, b):
    return lax.dot_general(a, b, (((1,), (0,)), ((), ())), preferred_element_type=f32)


def tn(a, b):
    return lax.dot_general(a, b, (((0,), (0,)), ((), ())), preferred_element_type=f32)


def nt(a, b):
    return lax.dot_general(a, b, (((1,), (1,)), ((), ())), preferred_element_type=f32)


def terms(value, count):
    parts = []
    for unused in range(count):
        parts.append(value.astype(bf16))
        value = value - parts[-1].astype(f32)
    return parts


def nn_left(value, ones, count):
    return sum(nn(part, ones) for part in terms(value, count))


def nn_right(ones, value, count):
    return sum(nn(ones, part) for part in terms(value, count))


def iota(shape, dim):
    return lax.broadcasted_iota(jnp.int32, shape, dim)


def head_spread():
    row = iota((LANES, DS), 0)
    return (iota((LANES, DS), 1) // SSM_DIM == row).astype(f32).astype(bf16)


def head_sum_matrix():
    col = iota((DS, LANES), 1)
    return (iota((DS, LANES), 0) // SSM_DIM == col).astype(f32).astype(bf16)


def extents():
    along = lax.axis_size(SEQ)
    return {
        "x": (1, 2),
        "z": (2, along // 2),
        "core": (along, 2),
        "y": (2 * along, lax.axis_size("y")),
    }


def my_index():
    return lax.axis_index(AXES)


def place_on(group):
    unit, size = extents()[group]
    return (my_index() // unit) % size


def swap(array, mask):
    count = lax.axis_size(AXES)
    return lax.ppermute(array, AXES, [(i, i ^ mask) for i in range(count)])


def in_order(pieces, place):
    pieces = list(pieces)
    bit = 1
    while bit < len(pieces):
        flag = (place // bit) % 2 == 1
        pieces = [jnp.where(flag, pieces[j ^ bit], pieces[j]) for j in range(len(pieces))]
        bit *= 2
    return pieces


def collect(array, group, axis):
    unit, size = extents()[group]
    pieces = [array] + [swap(array, k * unit) for k in range(1, size)]
    return jnp.stack(in_order(pieces, place_on(group)), axis)


def gather_pair(full, first):
    if first == "y":
        full = collect(collect(full, "y", 0), "x", 2)
    else:
        full = collect(collect(full, "x", 1), "y", 0)
    other = swap(full, extents()["core"][0])
    shape = (full.shape[0], full.shape[1] * full.shape[2] * full.shape[3], full.shape[4])
    return full.reshape(shape), other.reshape(shape)


def cut(total, group, axis):
    size = extents()[group][1]
    place = place_on(group)
    keep = lax.dynamic_index_in_dim(total, place, axis, False)
    parts = [lax.dynamic_index_in_dim(total, place ^ k, axis, False) for k in range(1, size)]
    return keep, [p.astype(bf16) for p in parts]


def crossed(parts, group):
    unit = extents()[group][0]
    return [swap(part, (k + 1) * unit) for k, part in enumerate(parts)]


def joined(keep, received):
    total = keep.astype(f32)
    for part in received:
        total = total + part.astype(f32)
    return total


class Reduction:
    def __init__(self, total, rows, first):
        table = extents()
        self.total = total.reshape(
            table["y"][1], table["z"][1], table["x"][1], rows, total.shape[-1]
        )
        order = [("x", 2), ("y", 0)] if first == "x" else [("y", 0), ("x", 1)]
        self.stages = order + [("z", 0)]

    def send(self):
        (group, axis), self.stages = self.stages[0], self.stages[1:]
        self.keep, self.parts = cut(self.total, group, axis)
        self.received = crossed(self.parts, group)
        return self.parts

    def receive(self, *others):
        self.received = after(self.received, *others)
        self.total = joined(self.keep, self.received)
        return self.total


def after(value, *others):
    return lax.optimization_barrier((value, others))[0]


def gather_small(vector):
    full = collect(collect(collect(vector, "z", 0), "x", 1), "core", 0)
    return collect(full, "y", 0).reshape(-1, vector.shape[-1])


def dealt(array, axes):
    return lax.all_to_all(array, axes, 0, 0, tiled=True)


def shared(array, axes):
    return dealt(jnp.broadcast_to(array[None], (lax.axis_size(axes), *array.shape)), axes)


def shifted(array, by):
    count = lax.axis_size(SEQ)
    pairs = [(i, i + by) for i in range(count) if 0 <= i + by < count]
    return lax.ppermute(array, SEQ, pairs)


def link(earlier, later):
    carry = later[1]
    wide = jnp.repeat(carry[0, :SSM_HEADS], SSM_DIM)[:, None]
    return (later[0] + wide * earlier[0], carry * earlier[1])


class Carrying:
    def __init__(self, state, carry, back, sign):
        self.pair, self.back, self.sign, self.by = (state, carry), back, sign, 0

    def send(self):
        packed = jnp.concatenate(
            [self.pair[0], jnp.pad(self.pair[1], ((0, RIM - 1), (0, 0)))], 0
        ).astype(bf16)
        steps = [self.by] if self.by else [1] + [2] * (self.back > 1)
        self.got = [shifted(packed, self.sign * by) for by in steps]
        return packed

    def receive(self, *others):
        pairs = []
        for got in after(self.got, *others):
            got = got.astype(f32)
            pairs.append((got[:DS], got[DS : DS + 1]))
        self.by = 2 * self.by if self.by else min(self.back, 2)
        if len(pairs) == 2:
            self.pair = link(pairs[1], pairs[0])
        else:
            self.pair = link(pairs[0], self.pair) if self.by > 2 else pairs[0]
        return self.pair[0] if self.by >= self.back else None


def halves(block, core):
    width = block.shape[1] // 2
    low, high = block[:, :width], block[:, width:]
    return jnp.where(core == 0, low, high), jnp.where(core == 0, high, low)


def put(ref, y, own, other, core):
    width = own.shape[1]
    base = y * 2 * width
    ref[:, base : base + width] = jnp.where(core == 0, own, other).astype(ref.dtype)
    ref[:, base + width : base + 2 * width] = jnp.where(core == 0, other, own).astype(ref.dtype)


def sides(ref, core, count):
    width = ref.shape[-1] // count
    return [halves(ref[:, y * width : (y + 1) * width], core) for y in range(count)]


def cross_half(value):
    lane = iota(value.shape, 1) % HEAD_DIM
    up = pltpu.roll(value, LANES - HEAD_DIM // 2, 1)
    down = pltpu.roll(value, HEAD_DIM // 2, 1)
    return jnp.where(lane < HEAD_DIM // 2, up, down)


def turned(value, cos, sin):
    return value * cos + cross_half(value) * sin


def turned_back(value, cos, sin):
    return value * cos - cross_half(value) * sin


def split_heads(pair, which, lane):
    flipped = pltpu.roll(pair, HEAD_DIM, 1)
    if which == 0:
        return jnp.where(lane < HEAD_DIM, pair, 0.0), jnp.where(lane < HEAD_DIM, flipped, 0.0)
    return jnp.where(lane >= HEAD_DIM, flipped, 0.0), jnp.where(lane >= HEAD_DIM, pair, 0.0)


def join_heads(even, odd, which, lane):
    if which == 0:
        return jnp.where(lane < HEAD_DIM, even, pltpu.roll(odd, HEAD_DIM, 1))
    return jnp.where(lane < HEAD_DIM, pltpu.roll(even, HEAD_DIM, 1), odd)


def conv_taps(chan_ref, cols, off):
    ext = chan_ref[:, cols].astype(f32)
    taps = []
    for i in range(CONV):
        back = CONV - 1 - i
        rows = pltpu.roll(ext, back, 0)[RIM:] if back else ext[RIM:]
        taps.append(rows * (off >= back).astype(f32))
    return taps


def sigmoid(v):
    return 1.0 / (1.0 + jnp.exp(-v))


def softplus(v):
    return jnp.maximum(v, 0.0) + jnp.log1p(jnp.exp(-jnp.abs(v)))


def tail_of(cum, off):
    rows = cum.shape[0]
    last_off = off[rows - 1 :, :]
    keep = iota((rows, 1), 0) >= rows - 1 - last_off
    return jnp.exp(cum[rows - 1 :, :] - cum) * keep.astype(f32)


def fade_of(cum, off):
    keep = off > iota((cum.shape[0], 1), 0)
    return jnp.exp(cum) * keep.astype(f32)


def carry_of(cum, off):
    rows = cum.shape[0]
    return jnp.exp(cum[rows - 1 :, :]) * (off[rows - 1 :, :] >= rows).astype(f32)


def front_kernel(
    core_ref, tok_ref, gain_ref, wa_own, wa_oth, wb_own, wb_oth, cos_ref, sin_ref, off_ref,
    cw_ref, cb_ref, sb_ref, dec_ref,
    q8_ref, kv_ref, normed_ref, nrim_ref, chan_ref, x_ref, bc_ref, step_ref, cum_ref, cumt_ref, z_ref,
    state_ref, carry_ref,
    n_ref, xt_ref,
):
    core = core_ref[0]
    rows = cos_ref.shape[0]
    tok = tok_ref[...].astype(f32)
    rms = lax.rsqrt(jnp.mean(tok * tok, axis=1, keepdims=True) + EPS)
    n_ref[...] = (tok * rms * gain_ref[...]).astype(bf16)
    normed_ref[...] = n_ref[RIM:, :]
    nrim_ref[...] = n_ref[:RIM, :]
    count = wa_own.shape[0]
    blocks = sides(n_ref, core, count)

    def project(own_ref, oth_ref, cols):
        total = 0.0
        for y, (own, oth) in enumerate(blocks):
            total = total + nn(own, own_ref[y, :, cols]) + nn(oth, oth_ref[y, :, cols])
        return total

    lane = iota((rows, LANES), 1)
    cos, sin, off = cos_ref[...], sin_ref[...], off_ref[...]
    kv = project(wa_own, wa_oth, pl.ds(0, 256))[RIM:]
    kv_ref[:, :LANES] = turned(kv[:, :LANES], cos, sin).astype(bf16)
    kv_ref[:, LANES:] = kv[:, LANES:].astype(bf16)
    queries = project(wa_own, wa_oth, pl.ds(256, 512))[RIM:]
    for j in range(HEADS // 2):
        pair = turned(queries[:, j * LANES : (j + 1) * LANES], cos, sin)
        even, odd = split_heads(pair, j // 2, lane)
        q8_ref[2 * j] = even.astype(bf16)
        q8_ref[2 * j + 1] = odd.astype(bf16)
    rest = project(wa_own, wa_oth, pl.ds(768, 384))
    chan_ref[:, DS:] = rest[:, : 2 * STATE].astype(bf16)
    z = rest[RIM:, 2 * STATE :].astype(bf16).astype(f32) + sb_ref[...]
    for j in range(DS // 512):
        cols = slice(j * 512, (j + 1) * 512)
        chan_ref[:, cols] = project(wb_own, wb_oth, pl.ds(j * 512, 512)).astype(bf16)
    z_ref[...] = z
    step = softplus(z)
    step_ref[...] = step
    tri = (iota((rows, rows), 0) >= iota((rows, rows), 1)).astype(f32).astype(bf16)
    cum = nn_right(tri, -step * dec_ref[...], 3)
    cum_ref[...] = cum
    cumt_ref[...] = cum.T
    carry_ref[...] = carry_of(cum, off)
    weight = nn_left(step * tail_of(cum, off), head_spread(), 2)
    for j in range(CONV_CH // 256):
        cols = slice(j * 256, (j + 1) * 256)
        mixed = cb_ref[:, cols]
        for i, tap in enumerate(conv_taps(chan_ref, cols, off)):
            mixed = mixed + tap * cw_ref[i : i + 1, cols]
        active = mixed * sigmoid(mixed)
        if j < DS // 256:
            x_ref[:, cols] = active
            xt_ref[:, cols] = (active * weight[:, cols]).astype(bf16)
        else:
            bc_ref[...] = active
    state_ref[...] = tn(xt_ref[...], bc_ref[:, :STATE].astype(bf16))


def scan_masks(off, rows):
    t, s = iota((rows, rows), 0), iota((rows, rows), 1)
    return (s <= t) & (s >= t - off)


def scan_kernel(x_ref, bc_ref, step_ref, cum_ref, cumt_ref, off_ref, y_ref, xw_ref, ce_ref):
    rows = x_ref.shape[0]
    spread = head_spread()
    xw_ref[...] = (x_ref[...] * nn_left(step_ref[...], spread, 2)).astype(bf16)
    ce_ref[...] = nn_left(cum_ref[...], spread, 3)
    keys, reads = bc_ref[:, :STATE].astype(bf16), bc_ref[:, STATE:].astype(bf16)
    scores = jnp.where(scan_masks(off_ref[...], rows), nt(reads, keys), 0.0)
    lane = iota((rows, LANES), 1)

    def pair(j, unused):
        cols = pl.ds(pl.multiple_of(j * LANES, LANES), LANES)
        wide = ce_ref[:, cols]
        xw = xw_ref[:, cols]
        outs = []
        for k in range(2):
            late = wide[:, k * SSM_DIM : k * SSM_DIM + 1]
            early = cumt_ref[pl.ds(2 * j + k, 1), :]
            decay = jnp.exp(jnp.minimum(late - early, 0.0))
            outs.append(nn((decay * scores).astype(bf16), xw))
        y_ref[:, cols] = jnp.where(lane < SSM_DIM, outs[0], outs[1])
        return unused

    lax.fori_loop(0, SSM_HEADS // 2, pair, 0)


def attend_bias(off, rows, window):
    query = iota((rows, window), 0) + (window - rows)
    key = iota((rows, window), 1)
    return jnp.where((key <= query) & (key >= query - off), 0.0, NEG)


def window_of(count, rank, kv_ref, k_ref, v_ref):
    rows = kv_ref.shape[1]
    for i in range(count):
        piece = jnp.maximum(rank - (count - 1 - i), 0)
        k_ref[i * rows : (i + 1) * rows, :] = kv_ref[piece, :, :LANES]
        v_ref[i * rows : (i + 1) * rows, :] = kv_ref[piece, :, LANES:]


def attend_kernel(
    count, rank_ref, q8_ref, kv_ref, off_ref, att_ref, lse_ref, k_ref, v_ref, bias_ref, o_ref
):
    rows = off_ref.shape[0]
    window = count * rows
    window_of(count, rank_ref[0], kv_ref, k_ref, v_ref)
    bias_ref[...] = attend_bias(off_ref[...], rows, window)
    lane = iota((rows, LANES), 1)

    def head(h, lses):
        scores = nt(q8_ref[h], k_ref[...]) * HEAD_DIM**-0.5 + bias_ref[...]
        top = jnp.max(scores, axis=1, keepdims=True)
        probs = jnp.exp(scores - top)
        total = jnp.sum(probs, axis=1, keepdims=True)
        o_ref[h] = nn((probs * (1.0 / total)).astype(bf16), v_ref[...])
        return jnp.where(lane == h, top + jnp.log(total), lses)

    lse_ref[...] = lax.fori_loop(0, HEADS, head, jnp.zeros((rows, LANES), f32)).T
    for j in range(HEADS // 2):
        pair = join_heads(o_ref[2 * j], o_ref[2 * j + 1], j // 2, lane)
        att_ref[:, j * LANES : (j + 1) * LANES] = pair.astype(bf16)


def attend_back_kernel(
    count, rank_ref, q8_ref, kv_ref, off_ref, lse_ref, datt_ref, cos_ref, sin_ref,
    dq_ref, out_ref, k_ref, v_ref, bias_ref, do_ref, dq8_ref, dkv_ref,
):
    rows = off_ref.shape[1]
    window = count * rows
    rank = rank_ref[0]
    window_of(count, rank, kv_ref, k_ref, v_ref)
    query = iota((window, rows), 1) + (window - rows)
    key = iota((window, rows), 0)
    bias_ref[...] = jnp.where((key <= query) & (key >= query - off_ref[...]), 0.0, NEG)
    lane = iota((rows, LANES), 1)
    for j in range(HEADS // 2):
        pair = datt_ref[:, j * LANES : (j + 1) * LANES].astype(f32)
        even, odd = split_heads(pair, j // 2, lane)
        do_ref[2 * j] = even.astype(bf16)
        do_ref[2 * j + 1] = odd.astype(bf16)
    dkv_ref[...] = jnp.zeros(dkv_ref.shape, f32)

    def head(h, unused):
        query, grad = q8_ref[h], do_ref[h]
        scores = nt(k_ref[...], query) * HEAD_DIM**-0.5 + bias_ref[...]
        probs = jnp.exp(scores - lse_ref[pl.ds(h, 1), :])
        dprobs = nt(v_ref[...], grad)
        mean = jnp.sum(probs * dprobs, axis=0, keepdims=True)
        draw = (probs * (dprobs - mean) * HEAD_DIM**-0.5).astype(bf16)
        dkv_ref[:, :LANES] += nn(draw, query)
        dkv_ref[:, LANES:] += nn(probs.astype(bf16), grad)
        dq8_ref[h] = tn(draw, k_ref[...])
        return unused

    lax.fori_loop(0, HEADS, head, 0)
    out_ref[...] = jnp.zeros(out_ref.shape, bf16)
    for i in range(count):
        piece = rank - (count - 1 - i)

        @pl.when(piece >= 0)
        def unused():
            out_ref[piece] = dkv_ref[i * rows : (i + 1) * rows, :].astype(bf16)

    for j in range(HEADS // 2):
        pair = join_heads(dq8_ref[2 * j], dq8_ref[2 * j + 1], j // 2, lane)
        back = turned_back(pair, cos_ref[...], sin_ref[...])
        dq_ref[:, j * LANES : (j + 1) * LANES] = back.astype(bf16)


class PackedWeights:
    def __init__(self, sources, held, sems, parts):
        self.held = held
        part, a_part, s_part, f_part = self.parts = parts
        self.so_at = 2 * part
        self.gu_at = self.so_at + s_part
        self.down_at = self.gu_at + 4 * part
        ends = [0, self.so_at, self.gu_at, self.down_at + f_part]
        self.copies = []
        for k in range(3):
            rows = pl.ds(ends[k], ends[k + 1] - ends[k])
            self.copies.append(
                [
                    pltpu.make_async_copy(
                        sources[i].at[:, :, rows], held.at[i, :, :, rows], sems.at[k, i]
                    )
                    for i in range(2)
                ]
            )
        for pair in self.copies:
            for copy in pair:
                copy.start()

    def wait(self, k):
        for copy in self.copies[k]:
            copy.wait()

    def block(self, i, y, start, size, cols):
        got = self.held[i, y, :, start : start + size, cols]
        return got.reshape(got.shape[0] * size, got.shape[2])

    def gate(self, i, y, j):
        part = self.parts[0]
        return self.block(i, y, j // 2 * part, part, slice(j % 2 * 512, j % 2 * 512 + 512))

    def ao(self, i, y, j):
        part, a_part = self.parts[:2]
        return self.block(i, y, part + j * a_part, a_part, slice(512, 1024))

    def so(self, i, y, j):
        return self.block(i, y, self.so_at, self.parts[2], slice(j * 512, j * 512 + 512))

    def down(self, i, y, j):
        return self.block(i, y, self.down_at, self.parts[3], slice(j * 512, j * 512 + 512))

    def gu(self, i, y, j):
        part = self.parts[0]
        start = pl.multiple_of(self.gu_at + j // 2 * part, 16)
        cols = pl.multiple_of(j % 2 * 512, 512)
        got = self.held[i, y, :, pl.ds(start, part), pl.ds(cols, 512)]
        return got.reshape(got.shape[0] * part, 512)


class PlainWeights:
    def __init__(self, refs):
        self.refs = refs

    def wait(self, k):
        pass

    def block(self, name, i, y, j):
        return self.refs[2 * name + i][y, :, j * 512 : j * 512 + 512]

    def gate(self, i, y, j):
        return self.block(0, i, y, j)

    def ao(self, i, y, j):
        return self.block(1, i, y, j)

    def so(self, i, y, j):
        return self.block(2, i, y, j)

    def down(self, i, y, j):
        return self.block(3, i, y, j)

    def gu(self, i, y, j):
        return self.refs[8 + i][y, :, pl.ds(pl.multiple_of(j * 512, 512), 512)]


def post_kernel(
    parts, ys, core_ref, tok_ref, cot_ref, att_ref, yl_ref, x_ref, bc_ref, cum_ref, off_ref,
    entry_ref, skip_ref, normed_ref, gssm_ref, gffn_ref, *refs,
):
    if parts:
        weights = PackedWeights(refs[:2], refs[-2], refs[-1], parts)
        refs = refs[2:-2]
    else:
        weights, refs = PlainWeights(refs[:10]), refs[10:]
    pairs = [(i, y) for y in range(ys) for i in range(2)]

    def through(ref, weight, j):
        blocks = sides(ref, core, ys)
        return sum(nn(blocks[y][i], weight(i, y, j)) for i, y in pairs)

    def back_through(ref, grad, weight, count):
        for y in range(ys):
            both = []
            for i in range(2):
                both.append(
                    sum(nt(grad[:, j * 512 : j * 512 + 512], weight(i, y, j)) for j in range(count))
                )
            put(ref, y, both[0], both[1], core)

    (
        out_ref, dmid_ref, datt_ref, dssd_ref, ycore_ref, dentry_ref, send_ref, keep_ref, dng_ref,
        gi_ref, gd_ref, mid_ref, gu_ref, dn_ref, dmx_ref, fd_ref, n2_ref, hid_ref, mixed_ref, dh_ref,
    ) = refs
    core = core_ref[0]
    rows, width = tok_ref.shape
    heads_width = att_ref.shape[1]
    ff = hid_ref.shape[1]
    half = keep_ref.shape[1]
    cot_at, dbr_at, dgate_at, sel_at = 2 * ff, 2 * ff + width, 2 * ff + 2 * width, 2 * ff + 2 * width + DS
    reads = bc_ref[:, STATE:].astype(bf16)
    spread = head_spread()
    fade = nn_left(fade_of(cum_ref[...], off_ref[...]), spread, 2)
    entered = nt(reads, entry_ref[...].astype(bf16))
    square = 0.0
    weights.wait(0)
    for j in range(DS // 512):
        cols = slice(j * 512, (j + 1) * 512)
        gate = through(normed_ref, weights.gate, j).astype(bf16).astype(f32)
        gi_ref[:, cols] = gate
        ycore = yl_ref[:, cols] + fade[:, cols] * entered[:, cols]
        ycore_ref[:, cols] = ycore
        ssd = ycore + skip_ref[:, cols] * x_ref[:, cols]
        gated = ssd * gate * sigmoid(gate)
        gd_ref[:, cols] = gated
        square = square + jnp.sum(gated * gated, axis=1, keepdims=True)
    rms_gate = lax.rsqrt(square / DS + EPS)
    mixed_ref[...] = (gd_ref[...] * rms_gate * gssm_ref[...]).astype(bf16)
    square = 0.0
    weights.wait(1)
    for j in range(width // 512):
        cols = slice(j * 512, (j + 1) * 512)
        branch = through(att_ref, weights.ao, j) + through(mixed_ref, weights.so, j)
        middle = tok_ref[:, cols].astype(f32) + branch
        mid_ref[:, cols] = middle
        square = square + jnp.sum(middle * middle, axis=1, keepdims=True)
    rms = lax.rsqrt(square / width + EPS)
    n2_ref[...] = (mid_ref[...] * rms * gffn_ref[...]).astype(bf16)
    weights.wait(2)
    blocks = sides(n2_ref, core, ys)

    def up(j, unused):
        cols = pl.ds(pl.multiple_of(j * 512, 512), 512)
        gu_ref[:, cols] = sum(nn(blocks[y][i], weights.gu(i, y, j)) for i, y in pairs)
        return unused

    lax.fori_loop(0, 2 * ff // 512, up, 0)
    for j in range(ff // 512):
        gate = gu_ref[:, j * 512 : (j + 1) * 512]
        lift = gu_ref[:, ff + j * 512 : ff + (j + 1) * 512]
        hid_ref[:, j * 512 : (j + 1) * 512] = (gate * sigmoid(gate) * lift).astype(bf16)
    for j in range(width // 512):
        cols = slice(j * 512, (j + 1) * 512)
        out_ref[:, cols] = (mid_ref[:, cols] + through(hid_ref, weights.down, j)).astype(bf16)
    cot = cot_ref[...]
    back_through(dh_ref, cot, weights.down, 2)
    for j in range(ff // 512):
        cols = slice(j * 512, (j + 1) * 512)
        gate = gu_ref[:, cols]
        lift = gu_ref[:, ff + j * 512 : ff + (j + 1) * 512]
        sg = sigmoid(gate)
        dhid = dh_ref[:, cols]
        dgate = dhid * lift * (sg * (1.0 + gate * (1.0 - sg)))
        send_ref[:, cols] = dgate.astype(bf16)
        send_ref[:, ff + j * 512 : ff + (j + 1) * 512] = (dhid * gate * sg).astype(bf16)
    send_ref[:, cot_at:dbr_at] = cot
    wide = width // ys // 2

    def down(j, totals):
        grad = send_ref[:, pl.ds(pl.multiple_of(j * 512, 512), 512)]
        return [t + nt(grad, weights.gu(i, y, j)) for t, (i, y) in zip(totals, pairs)]

    zero = [jnp.zeros((rows, wide), f32)] * len(pairs)
    totals = lax.fori_loop(0, 2 * ff // 512, down, zero)
    for y in range(ys):
        put(dn_ref, y, totals[2 * y], totals[2 * y + 1], core)
    unit = mid_ref[...] * rms
    dn = dn_ref[...]
    dn = dn * gffn_ref[...]
    dmid = cot.astype(f32) + rms * (dn - unit * jnp.mean(dn * unit, axis=1, keepdims=True))
    dmid_ref[...] = dmid
    dbr = dmid.astype(bf16)
    send_ref[:, dbr_at:dgate_at] = dbr
    back_through(datt_ref, dbr, weights.ao, 2)
    back_through(dmx_ref, dbr, weights.so, 2)
    mean = 0.0
    for j in range(DS // 512):
        cols = slice(j * 512, (j + 1) * 512)
        unit = gd_ref[:, cols] * rms_gate
        dmx = dmx_ref[:, cols]
        mean = mean + jnp.sum(dmx * gssm_ref[:, cols] * unit, axis=1, keepdims=True)
    mean = mean / DS
    for j in range(DS // 512):
        cols = slice(j * 512, (j + 1) * 512)
        unit = gd_ref[:, cols] * rms_gate
        dgated = rms_gate * (dmx_ref[:, cols] * gssm_ref[:, cols] - unit * mean)
        gate = gi_ref[:, cols]
        sg = sigmoid(gate)
        ssd = ycore_ref[:, cols] + skip_ref[:, cols] * x_ref[:, cols]
        dssd = dgated * gate * sg
        dssd_ref[:, cols] = dssd
        dgate = (dgated * ssd * (sg * (1.0 + gate * (1.0 - sg)))).astype(bf16)
        send_ref[:, dgate_at + j * 512 : dgate_at + (j + 1) * 512] = dgate
        fd_ref[:, cols] = (dssd * fade[:, cols]).astype(bf16)
    back_through(dng_ref, send_ref[:, dgate_at:sel_at], weights.gate, 3)
    dentry_ref[...] = tn(fd_ref[...], reads)
    at = 0
    for ref in (n2_ref, hid_ref, att_ref, mixed_ref, normed_ref):
        count = ys
        wide = ref.shape[1] // count
        for y in range(count):
            own, oth = halves(ref[:, y * wide : (y + 1) * wide], core)
            keep_ref[:, at : at + wide // 2] = own
            send_ref[:, sel_at + at : sel_at + at + wide // 2] = oth
            at += wide // 2


def products_kernel(plan, extra, keep_ref, own_ref, act_ref, *refs):
    got_ref, outs = act_ref, refs
    if extra:
        (extra_ref, *outs) = refs
    for which, a_at, act_at, size, g_at in plan:
        out = outs[which]
        for y in range(out.shape[0]):
            left = keep_ref[:, a_at + y * size : a_at + (y + 1) * size]
            right = act_ref[:, act_at + y * size : act_at + (y + 1) * size]
            for j in range(0, out.shape[-1], 512):
                stop = min(j + 512, out.shape[-1])
                total = tn(left, own_ref[:, g_at + j : g_at + stop])
                total = total + tn(right, got_ref[:, g_at + j : g_at + stop])
                if extra and which == 0 and stop == out.shape[-1]:
                    total = total + extra_ref[y]
                out[y, :, j:stop] = total.astype(bf16)


def split_products_kernel(plan, extra, y_ref, x_ref, keep_ref, own_ref, act_ref, *refs):
    got_ref, outs = act_ref, refs
    if extra:
        (extra_ref, *outs) = refs
    xkeep_ref, xsend_ref, ykeep_ref, ysend_ref = outs
    my_y, my_x = y_ref[0], x_ref[0]
    for kind, place, a_at, act_at, size, g_at, wide in plan:
        for k in range(2):
            y = k if kind == "x" else lax.rem(my_y + k, 2)
            left = keep_ref[:, pl.ds(pl.multiple_of(a_at + y * size, LANES), size)]
            right = act_ref[:, pl.ds(pl.multiple_of(act_at + y * size, LANES), size)]
            keep, send = (xkeep_ref, xsend_ref) if kind == "x" else (ykeep_ref, ysend_ref)
            for j in range(0, wide, 512):
                stop = min(j + 512, wide)
                total = tn(left, own_ref[:, g_at + j : g_at + stop])
                total = total + tn(right, got_ref[:, g_at + j : g_at + stop])
                if kind == "x":
                    zs, each = keep.shape[1], keep.shape[2]
                    if extra and stop == wide:
                        total = total + extra_ref[k]
                    cols = slice(place + j, place + stop)
                    total = total.reshape(zs, 2, each, stop - j)
                    low, high = total[:, 0], total[:, 1]
                    keep[k, :, :, cols] = jnp.where(my_x == 0, low, high).astype(bf16)
                    send[k, :, :, cols] = jnp.where(my_x == 0, high, low).astype(bf16)
                else:
                    count = keep.shape[0]
                    each = size // count
                    total = total.reshape(count, each, stop - j).astype(bf16)
                    (send if k else keep)[:, place : place + each, j:stop] = total


def fold_one_kernel(
    y_ref, x_ref, xkeep_ref, xgot_ref, ykeep_ref, ygot_ref,
    xkeep_out, xsend_out, ykeep_out, ysend_out,
):
    my_y, my_x = y_ref[0], x_ref[0]
    xkeep_out[...] = xkeep_ref[my_y].astype(f32) + xgot_ref[my_y].astype(f32)
    other = 1 - my_y
    xsend_out[...] = (xkeep_ref[other].astype(f32) + xgot_ref[other].astype(f32)).astype(bf16)
    for z in range(ykeep_out.shape[0]):
        at = 2 * z + my_x
        ykeep_out[z] = ykeep_ref[at].astype(f32) + ygot_ref[at].astype(f32)
        at = 2 * z + 1 - my_x
        ysend_out[z] = (ykeep_ref[at].astype(f32) + ygot_ref[at].astype(f32)).astype(bf16)


def laid(refs, width):
    at = 0
    for ref in refs:
        each = ref.shape[-2]
        for j in range(ref.shape[-1] // width):
            yield ref, at, j * width
            at += each


def fold_two_kernel(xkeep_ref, xgot_ref, ykeep_ref, ygot_ref, out_ref):
    width = out_ref.shape[2]
    keeps = laid((xkeep_ref, ykeep_ref), width)
    gots = laid((xgot_ref, ygot_ref), width)
    for (keep, at, col), (got, *unused) in zip(keeps, gots):
        each = keep.shape[-2]
        value = keep[:, :, col : col + width] + got[:, :, col : col + width].astype(f32)
        out_ref[:, at : at + each, :] = value.astype(bf16)


def fold_three_kernel(got_ref, *outs):
    width = got_ref.shape[2]
    for out, at, col in laid(outs, width):
        rows = slice(at, at + out.shape[0])
        total = got_ref[0, rows, :].astype(f32)
        for z in range(1, got_ref.shape[0]):
            total = total + got_ref[z, rows, :].astype(f32)
        out[:, col : col + width] = total


class PairReduction:
    def __init__(self, pieces, width):
        self.places = tuple(place_on(g).reshape(1).astype(jnp.int32) for g in ("y", "x"))
        self.xkeep, xsend, self.ykeep, ysend = pieces
        self.width = width
        self.send(xsend, ysend, "x", "y")

    def send(self, xsend, ysend, first, second):
        self.sent = (xsend, ysend)
        self.gots = (
            swap(xsend, extents()[first][0]), swap(ysend, extents()[second][0])
        )

    def fold_one(self, *others):
        gots = after(self.gots, *others)
        x, y = self.xkeep.shape, self.ykeep.shape
        x, y = x[1:], (y[0] // 2, *y[1:])
        self.xkeep, xsend, self.ykeep, ysend = run(
            fold_one_kernel, "fold_one", [(x, f32), (x, bf16), (y, f32), (y, bf16)],
            (*self.places, self.xkeep, gots[0], self.ykeep, gots[1]),
            scalars=2,
        )
        self.send(xsend, ysend, "y", "x")

    def fold_two(self, *others):
        gots = after(self.gots, *others)
        self.shapes = [self.xkeep.shape[1:], self.ykeep.shape[1:]]
        rows = sum(r * c // self.width for r, c in self.shapes)
        zs = self.xkeep.shape[0]
        self.sent = run(
            fold_two_kernel, "fold_two", [((zs, rows, self.width), bf16)],
            (self.xkeep, gots[0], self.ykeep, gots[1]),
        )[0]
        self.gots = dealt(self.sent, "z")

    def fold_three(self, *others):
        gots = after(self.gots, *others)
        self.sent = run(
            fold_three_kernel, "fold_three", [(shape, f32) for shape in self.shapes], (gots,),
        )
        return self.sent


class PlainReduction:
    def __init__(self, pieces, rows):
        self.parts = [Reduction(pieces[0], rows[0], "x"), Reduction(pieces[1], rows[1], "y")]
        self.sent = [part.send() for part in self.parts]

    def fold_one(self, *others):
        for part in self.parts:
            part.receive(*others)
        self.sent = [part.send() for part in self.parts]

    fold_two = fold_one

    def fold_three(self, *others):
        self.sent = [part.receive(*others) for part in self.parts]
        return self.sent


def scan_back_kernel(
    dy_ref, x_ref, bc_ref, step_ref, cum_ref, cumt_ref, off_ref, dxw_ref, ds_ref,
    xw_ref, ce_ref, dyb_ref, dg_ref,
):
    rows = x_ref.shape[0]
    spread = head_spread()
    xw_ref[...] = (x_ref[...] * nn_left(step_ref[...], spread, 2)).astype(bf16)
    dyb_ref[...] = dy_ref[...].astype(bf16)
    ce_ref[...] = nn_left(cum_ref[...], spread, 3)
    keys, reads = bc_ref[:, :STATE].astype(bf16), bc_ref[:, STATE:].astype(bf16)
    early, late = iota((rows, rows), 0), iota((rows, rows), 1)
    keep = (early <= late) & (early >= late - off_ref[...])
    scores = jnp.where(keep, nt(keys, reads), 0.0)
    lane = iota((rows, LANES), 1)
    dg_ref[...] = jnp.zeros((rows, rows), f32)

    def pair(j, unused):
        cols = pl.ds(pl.multiple_of(j * LANES, LANES), LANES)
        wide = ce_ref[:, cols]
        xw, dy = xw_ref[:, cols], dyb_ref[:, cols]
        outs = []
        change = 0.0
        for k in range(2):
            first = wide[:, k * SSM_DIM : k * SSM_DIM + 1]
            second = cumt_ref[pl.ds(2 * j + k, 1), :]
            decay = jnp.exp(jnp.minimum(second - first, 0.0))
            outs.append(nn((decay * scores).astype(bf16), dy))
            mine = (lane < SSM_DIM) if k == 0 else (lane >= SSM_DIM)
            change = change + nt(xw * mine.astype(bf16), dy) * decay
        dg_ref[...] += change
        dxw_ref[:, cols] = jnp.where(lane < SSM_DIM, outs[0], outs[1])
        return unused

    lax.fori_loop(0, SSM_HEADS // 2, pair, 0)
    ds_ref[...] = jnp.where(keep, dg_ref[...], 0.0).astype(bf16)


def mixer_back_kernel(
    dy_ref, ycore_ref, x_ref, bc_ref, step_ref, cum_ref, z_ref, off_ref, entry_ref,
    down_ref, skip_ref, dec_ref, chan_ref, cw_ref, cb_ref, dxwl_ref, ds_ref,
    dext_ref, dz_ref, small_ref,
    dact_ref,
):
    rows = x_ref.shape[0]
    spread, gather = head_spread(), head_sum_matrix()
    off, cum = off_ref[...], cum_ref[...]
    step_wide = nn_left(step_ref[...], spread, 2)
    keys, reads = bc_ref[:, :STATE].astype(bf16), bc_ref[:, STATE:].astype(bf16)
    dscores = ds_ref[...]
    down = down_ref[...].astype(bf16)
    tail = nn_left(tail_of(cum, off), spread, 2)
    fade = nn_left(fade_of(cum, off), spread, 2)
    bd = nt(keys, down) * tail
    xw = (x_ref[...] * step_wide).astype(bf16).astype(f32)
    dxw = dxwl_ref[...] + bd
    dact_ref[:, DS : DS + STATE] = nn(dscores, reads) + nn((tail * xw).astype(bf16), down)
    dact_ref[:, DS + STATE :] = tn(dscores, keys) + nn(
        (fade * dy_ref[...]).astype(bf16), entry_ref[...].astype(bf16)
    )
    ones = jnp.ones((8, STATE), bf16)
    product = sum(nt(ones, part) for part in terms(down_ref[...] * entry_ref[...], 3))
    through = jnp.sum(xw * bd, axis=0, keepdims=True)
    direct = jnp.sum(dy_ref[...] * x_ref[...], axis=0, keepdims=True)
    row = iota((8, DS), 0)
    sums = jnp.where(row == 0, product, jnp.where(row == 1, through, direct))
    sums = nn_left(sums, gather, 3)
    through, kept = sums[1:2], sums[0:1] * carry_of(cum, off)
    last = (iota((rows, 1), 0) == rows - 1).astype(f32)
    dyb = dy_ref[...].astype(bf16).astype(f32)
    dcum = nn_left(dyb * ycore_ref[...] - xw * dxw, gather, 2) + last * (through + kept)
    tri = (iota((rows, rows), 0) <= iota((rows, rows), 1)).astype(f32).astype(bf16)
    dlog = nn_right(tri, dcum, 3)
    x = x_ref[...]
    step, dec = step_ref[...], dec_ref[...]
    dstep = nn_left(dxw * x, gather, 2) - dlog * dec
    dz = dstep * sigmoid(z_ref[...])
    dz_ref[...] = dz
    small_ref[...] = jnp.zeros(small_ref.shape, f32)
    small_ref[CONV + 1 : CONV + 2, :LANES] = jnp.sum(dlog * (-step * dec), axis=0, keepdims=True)
    small_ref[CONV + 1 : CONV + 2, LANES : 2 * LANES] = jnp.sum(dz, axis=0, keepdims=True)
    small_ref[CONV + 1 : CONV + 2, 2 * LANES : 3 * LANES] = sums[2:3]
    dact_ref[:, :DS] = dxw * step_wide + skip_ref[...] * dy_ref[...]
    for j in range(CONV_CH // 256):
        cols = slice(j * 256, (j + 1) * 256)
        taps = conv_taps(chan_ref, cols, off)
        mixed = cb_ref[:, cols]
        for i, tap in enumerate(taps):
            mixed = mixed + tap * cw_ref[i : i + 1, cols]
        sg = sigmoid(mixed)
        dmix = dact_ref[:, cols] * (sg * (1.0 + mixed * (1.0 - sg)))
        small_ref[CONV : CONV + 1, cols] = jnp.sum(dmix, axis=0, keepdims=True)
        total = 0.0
        for i, tap in enumerate(taps):
            back = CONV - 1 - i
            small_ref[i : i + 1, cols] = jnp.sum(dmix * tap, axis=0, keepdims=True)
            part = dmix * ((off >= back).astype(f32) * cw_ref[i : i + 1, cols])
            part = jnp.concatenate([jnp.zeros((RIM, 256), f32), part], axis=0)
            total = total + (pltpu.roll(part, rows + RIM - back, 0) if back else part)
        dext_ref[:, cols] = total


def back_grads_kernel(
    ys, core_ref, dq_ref, dkv_ref, dext_ref, dz_ref, cos_ref, sin_ref, normed_ref, nrim_ref,
    ga_ref, keep_ref,
):
    core = core_ref[0]
    dkv = dkv_ref[0].astype(f32)
    for i in range(1, dkv_ref.shape[0]):
        dkv = dkv + dkv_ref[i].astype(f32)
    ga_ref[:RIM, :768] = jnp.zeros((RIM, 768), bf16)
    ga_ref[:RIM, 1024:A_COLS] = jnp.zeros((RIM, LANES), bf16)
    ga_ref[RIM:, :LANES] = turned_back(dkv[:, :LANES], cos_ref[...], sin_ref[...]).astype(bf16)
    ga_ref[RIM:, LANES:256] = dkv[:, LANES:].astype(bf16)
    ga_ref[RIM:, 256:768] = dq_ref[...]
    ga_ref[:, 768:1024] = dext_ref[:, DS:].astype(bf16)
    ga_ref[RIM:, 1024:A_COLS] = dz_ref[...].astype(bf16)
    ga_ref[:, A_COLS : A_COLS + DS] = dext_ref[:, :DS].astype(bf16)
    wide = normed_ref.shape[1] // ys
    at, to = 0, A_COLS + DS
    for y in range(ys):
        cols = slice(y * wide, (y + 1) * wide)
        for ref, rows in ((nrim_ref, slice(0, RIM)), (normed_ref, slice(RIM, None))):
            own, oth = halves(ref[:, cols], core)
            keep_ref[rows, at : at + wide // 2] = own
            ga_ref[rows, to + at : to + at + wide // 2] = oth
        at += wide // 2


def back_kernel(
    core_ref, gab_ref, wa_own, wa_oth, wb_own, wb_oth, tok_ref, dmid_ref, dng_ref, gain_ref,
    dtok_ref, drim_ref, dn_ref,
):
    core = core_ref[0]
    for y in range(wa_own.shape[0]):
        ga, gb = gab_ref[:, :A_COLS], gab_ref[:, A_COLS : A_COLS + DS]
        own = nt(ga, wa_own[y]) + nt(gb, wb_own[y])
        oth = nt(ga, wa_oth[y]) + nt(gb, wb_oth[y])
        put(dn_ref, y, own, oth, core)

    def through_norm(dn, tok):
        tok = tok.astype(f32)
        rms = lax.rsqrt(jnp.mean(tok * tok, axis=1, keepdims=True) + EPS)
        unit = tok * rms
        dn = dn * gain_ref[...]
        return rms * (dn - unit * jnp.mean(dn * unit, axis=1, keepdims=True))

    drim_ref[...] = through_norm(dn_ref[:RIM, :], tok_ref[:RIM, :])
    dtok_ref[...] = dmid_ref[...] + through_norm(dn_ref[RIM:, :] + dng_ref[...], tok_ref[RIM:, :])


def gain_kernel(pairs, count, *refs):
    gains, refs = refs[:count], refs[count:]
    outs = refs[-count:]
    for k, out in enumerate(outs):
        total = 0.0
        for group, w, g in pairs:
            if group == k:
                total = total + jnp.sum(
                    refs[w][...].astype(f32) * refs[g][...], axis=1, keepdims=True
                )
        out[...] = total / gains[k][...].astype(f32)


def run(kernel, name, outs, args, scalars=0, scratch=(), flops=0, left=0, sems=()):
    moved = sum(a.size * a.dtype.itemsize for a in args)
    shapes = [jax.ShapeDtypeStruct(shape, kind) for shape, kind in outs]
    moved += sum(s.size * s.dtype.itemsize for s in shapes)
    specs = [pl.BlockSpec(memory_space=pltpu.SMEM)] * scalars
    specs += [pl.BlockSpec(memory_space=pltpu.VMEM)] * (len(args) - scalars - left)
    specs += [pl.BlockSpec(memory_space=pl.ANY)] * left
    return pl.pallas_call(
        kernel,
        name=name,
        out_shape=shapes,
        in_specs=specs,
        out_specs=[pl.BlockSpec(memory_space=pltpu.VMEM)] * len(shapes),
        scratch_shapes=[pltpu.VMEM(shape, kind) for shape, kind in scratch]
        + [pltpu.SemaphoreType.DMA(shape) for shape in sems],
        compiler_params=pltpu.CompilerParams(vmem_limit_bytes=62 * 2**20),
        cost_estimate=pl.CostEstimate(
            flops=flops, bytes_accessed=moved, transcendentals=0
        ),
    )(*args)


def padded(vector, width):
    return jnp.pad(vector.astype(f32), (0, width - vector.shape[0]))[None, :]


def local(
    tokens, lengths, cotangent, mixer_gain, query_weight, keyval_weight, inner_weight, conv_weight,
    conv_bias, ssm_gain, attn_out_weight, ssm_out_weight, ffn_gain, gate_up_weight, down_weight,
    decay_log, step_bias, skip_gain,
):
    rows, width = tokens.shape
    seq_count, seq_rank = lax.axis_size(SEQ), lax.axis_index(SEQ)
    side = place_on("core").reshape(1)
    back = (rows * seq_count // 2) // rows
    part = query_weight.shape[0]
    heads_width, ff = HEADS * HEAD_DIM, gate_up_weight.shape[1] // 2
    a_rows, s_rows, f_rows = attn_out_weight.shape[0], ssm_out_weight.shape[0], down_weight.shape[0]
    ys = lax.axis_size("y")

    rim = shifted(tokens[rows - RIM :], 1)
    small = jnp.concatenate(
        [mixer_gain, conv_weight.reshape(-1), conv_bias, ssm_gain, ffn_gain]
    ).astype(f32)
    counts = [mixer_gain.size, conv_weight.size, conv_bias.size, ssm_gain.size, ffn_gain.size]
    slots = -(-small.size // LANES) * LANES
    small = gather_small(jnp.pad(small, (0, slots - small.size)))
    inner_tail = inner_weight[:, DS + CONV_CH :]
    front_a = jnp.concatenate(
        [
            keyval_weight,
            query_weight,
            inner_weight[:, 2 * DS : DS + CONV_CH],
            jnp.pad(inner_tail, ((0, 0), (0, LANES - SSM_HEADS))),
        ],
        1,
    )
    front = shared(jnp.concatenate([front_a, inner_weight[:, DS : 2 * DS]], 1), "z")
    wa_own, wa_oth = gather_pair(front[:, :, :A_COLS], "y")
    wb_own, wb_oth = gather_pair(front[:, :, A_COLS:], "x")
    others = lax.axis_size(SEQ)
    aligned = ys == 2 and others == 8 and all(r % 16 == 0 for r in (part, a_rows, s_rows, f_rows))
    core_unit = extents()["core"][0]
    packed = jnp.concatenate(
        [
            inner_weight[:, :width],
            jnp.concatenate(
                [
                    inner_weight[:, width:DS],
                    jnp.concatenate([attn_out_weight[:, :512], attn_out_weight[:, 512:]], 0),
                ],
                1,
            ),
            ssm_out_weight,
        ]
        + [gate_up_weight[:, k * width : (k + 1) * width] for k in range(2 * ff // width)]
        + [down_weight],
        0,
    )
    packed = lax.all_gather(packed, ("y", "z", "x"), axis=0)
    packed = packed.reshape(ys, others, *packed.shape[1:])
    starts = [sum(counts[:i]) for i in range(len(counts))]
    gain_one, w_conv, b_conv, gain_ssm, gain_two = (
        small[:, s : s + c].reshape(-1) for s, c in zip(starts, counts)
    )
    w_conv = jnp.pad(w_conv.reshape(CONV_CH, CONV).T, ((0, 8 - CONV), (0, 0)))
    gain_one, b_conv, gain_ssm, gain_two = (
        v[None, :] for v in (gain_one, b_conv, gain_ssm, gain_two)
    )
    tokens_rim = jnp.concatenate([rim, tokens], 0)
    places = seq_rank * rows + jnp.arange(rows)
    begin = jnp.zeros_like(places)
    end = jnp.int32(0)
    for i in range(lengths.shape[1]):
        end = end + lengths[0, i]
        begin = jnp.where(end <= places, end, begin)
    offset = (places - begin).astype(jnp.int32)
    half = HEAD_DIM // 2
    freq = BASE ** (-jnp.arange(half).astype(f32) / half)
    angle = offset.astype(f32)[:, None] * freq[None, :]
    cos = jnp.tile(jnp.cos(angle), (1, 4))
    sin = jnp.sin(angle)
    sin = jnp.tile(jnp.concatenate([-sin, sin], 1), (1, 2))
    off = offset[:, None]
    step_bias_row, decay_row = padded(step_bias, LANES), padded(jnp.exp(decay_log), LANES)
    skip = jnp.repeat(skip_gain, SSM_DIM)[None, :]

    (q8, kv, normed, nrim, chan, x, bc, step, cum, cumt, z, state, carry) = run(
        front_kernel,
        "front",
        [
            ((HEADS, rows, LANES), bf16),
            ((rows, 256), bf16),
            ((rows, width), bf16),
            ((RIM, width), bf16),
            ((rows + RIM, CONV_CH), bf16),
            ((rows, DS), f32),
            ((rows, 2 * STATE), f32),
            ((rows, LANES), f32),
            ((rows, LANES), f32),
            ((LANES, rows), f32),
            ((rows, LANES), f32),
            ((DS, STATE), f32),
            ((1, LANES), f32),
        ],
        (
            side, tokens_rim, gain_one, wa_own, wa_oth, wb_own, wb_oth,
            cos, sin, off, w_conv, b_conv, step_bias_row, decay_row,
        ),
        scalars=1,
        scratch=[((rows + RIM, width), bf16), ((rows, DS), bf16)],
        flops=2 * rows * width * (A_COLS + DS),
    )
    carrying = Carrying(state, carry, back, 1)
    sent_state = carrying.send()
    rank = seq_rank.reshape(1).astype(jnp.int32)
    kv_all = shared(kv, SEQ)
    window = (back + 1) * rows
    y_local = run(
        scan_kernel, "scan", [((rows, DS), f32)],
        after((x, bc, step, cum, cumt, off), sent_state),
        scratch=[((rows, DS), bf16), ((rows, DS), f32)], flops=2 * SSM_HEADS * rows * rows * 128,
    )[0]
    order = y_local
    entry = None
    while entry is None:
        entry = carrying.receive(order)
        if entry is None:
            sent_state = carrying.send()
    packed = after(packed, order, sent_state)
    packed = (packed, swap(packed, core_unit))
    post_scratch, post_sems = [], []
    if aligned:
        parts, post_weights = (part, a_rows, s_rows, f_rows), packed
        post_scratch, post_sems = [((2, *packed[0].shape), bf16)], [(3, 2)]
    else:
        parts = ()
        gu_at = 2 * part + s_rows

        def taken(full, start, size, low, high):
            return full[:, :, start : start + size, low:high].reshape(ys, -1, high - low)

        def joined_columns(blocks):
            return [jnp.concatenate([taken(f, *block) for block in blocks], 2) for f in packed]

        post_weights = (
            *joined_columns([(0, part, 0, width), (part, part, 0, DS - width)]),
            *joined_columns([(part + k * a_rows, a_rows, 512, 1024) for k in range(2)]),
            *joined_columns([(2 * part, s_rows, 0, width)]),
            *joined_columns([(gu_at + 4 * part, f_rows, 0, width)]),
            *joined_columns([(gu_at + k * part, part, 0, width) for k in range(2 * ff // width)]),
        )

    attended, lse = run(
        functools.partial(attend_kernel, back + 1),
        "attend",
        [((rows, heads_width), bf16), ((LANES, rows), f32)],
        after((rank, q8, kv_all, off), packed[0]),
        scalars=1,
        scratch=[
            ((window, LANES), bf16),
            ((window, LANES), bf16),
            ((rows, window), f32),
            ((HEADS, rows, LANES), f32),
        ],
        flops=4 * HEADS * rows * window * LANES,
    )
    half = (2 * width + ff + heads_width + DS) // 2
    sent = 2 * ff + 2 * width + DS
    output, dmid, datt, dssd, ycore, dentry, send, keep, dng = run(
        functools.partial(post_kernel, parts, ys),
        "post",
        [
            ((rows, width), bf16),
            ((rows, width), f32),
            ((rows, heads_width), bf16),
            ((rows, DS), f32),
            ((rows, DS), f32),
            ((DS, STATE), f32),
            ((rows, sent + half), bf16),
            ((rows, half), bf16),
            ((rows, width), f32),
        ],
        (
            side, tokens, cotangent, attended, y_local, x, bc, cum, off, entry, skip, normed,
            gain_ssm, gain_two, *post_weights,
        ),
        scalars=1,
        left=2 if aligned else 0,
        sems=post_sems,
        scratch=[
            ((rows, DS), f32),
            ((rows, DS), f32),
            ((rows, width), f32),
            ((rows, 2 * ff), f32),
            ((rows, width), f32),
            ((rows, DS), f32),
            ((rows, DS), bf16),
            ((rows, width), bf16),
            ((rows, ff), bf16),
            ((rows, DS), bf16),
            ((rows, ff), f32),
        ]
        + post_scratch,
        flops=4 * rows * width * (3 * ff + DS + DS + heads_width),
    )
    got = swap(send, core_unit)
    carrying = Carrying(dentry, carry, back, -1)
    sent_state = carrying.send()
    off_row = offset[None, :]
    sizes = [width // 2, ff // 2, heads_width // 2, DS // 2, width // 2]
    ats = [sum(sizes[:i]) for i in range(5)]
    sizes = [size // ys for size in sizes]
    n2_at, hid_at, att_at, mix_at, norm_at = ats
    cot_at, dbr_at, dgate_at = 2 * ff, 2 * ff + width, 2 * ff + 2 * width
    places = tuple(place_on(g).reshape(1).astype(jnp.int32) for g in ("y", "x"))

    def weight_sums(name, x_parts, y_parts, keep, own, got, extra=()):
        flops = sum(4 * rows * p[2] * p[4] * ys for p in x_parts + y_parts)
        plan, at, tall = [], 0, y_parts[0][4]
        for p in x_parts:
            plan.append(("x", at, *p))
            at += p[4]
        wide, at = at, 0
        for p in y_parts:
            plan.append(("y", at, *p))
            at += p[2] // others
        if aligned:
            xs = (ys, others // 2, x_parts[0][2] // others, wide)
            made = run(
                functools.partial(split_products_kernel, plan, len(extra)),
                name,
                [(xs, bf16), (xs, bf16), ((others, at, tall), bf16), ((others, at, tall), bf16)],
                (*places, keep, own, got, *extra),
                scalars=2,
                flops=flops,
            )
            return PairReduction(made, 512 if wide % 512 == 0 else 384)
        parts = x_parts + y_parts
        made = run(
            functools.partial(
                products_kernel, [(i, *p[:4]) for i, p in enumerate(parts)], len(extra)
            ),
            name,
            [((ys, p[2], p[4]), bf16) for p in parts],
            (keep, own, got, *extra),
            flops=flops,
        )
        heads = made[: len(x_parts)]
        tails = [m.reshape(ys, others, -1, tall) for m in made[len(x_parts) :]]
        rows_of = (x_parts[0][2] // others, at)
        return PlainReduction((jnp.concatenate(heads, 2), jnp.concatenate(tails, 2)), rows_of)

    dq, dkv = run(
        functools.partial(attend_back_kernel, back + 1),
        "attend_back",
        [((rows, heads_width), bf16), ((seq_count, rows, 256), bf16)],
        after((rank, q8, kv_all, off_row, lse, datt, cos, sin), sent_state),
        scalars=1,
        scratch=[
            ((window, LANES), bf16),
            ((window, LANES), bf16),
            ((window, rows), f32),
            ((HEADS, rows, LANES), bf16),
            ((HEADS, rows, LANES), f32),
            ((window, 256), f32),
        ],
        flops=10 * HEADS * rows * window * LANES,
    )
    dkv_got = dealt(dkv, SEQ)
    downstream = carrying.receive(dq)
    if downstream is None:
        sent_state = carrying.send()
    keep, send, got = after((keep, send, got), dq, sent_state)
    red_one = weight_sums(
        "weights_one",
        [(n2_at, sent + n2_at, sizes[0], 0, ff)],
        [(hid_at, sent + hid_at, sizes[1], cot_at, width)],
        keep,
        send,
        got,
    )
    while downstream is None:
        downstream = carrying.receive(red_one.sent)
        if downstream is None:
            carrying.send()
    keep, send, got = after((keep, send, got), red_one.sent, downstream)
    red_two = weight_sums(
        "weights_two",
        [
            (n2_at, sent + n2_at, sizes[0], ff, ff),
            (norm_at, sent + norm_at, sizes[4], dgate_at, DS),
        ],
        [
            (att_at, sent + att_at, sizes[2], dbr_at, width),
            (mix_at, sent + mix_at, sizes[3], dbr_at, width),
        ],
        keep,
        send,
        got,
    )
    dxw, dscores = run(
        scan_back_kernel,
        "scan_back",
        [((rows, DS), f32), ((rows, rows), bf16)],
        after((dssd, x, bc, step, cum, cumt, off_row), red_two.sent),
        scratch=[
            ((rows, DS), bf16),
            ((rows, DS), f32),
            ((rows, DS), bf16),
            ((rows, rows), f32),
        ],
        flops=4 * SSM_HEADS * rows * rows * 128,
    )

    red_one.fold_one(dxw)
    dext, dz, small = run(
        mixer_back_kernel,
        "mixer_back",
        [
            ((rows + RIM, CONV_CH), f32),
            ((rows, LANES), f32),
            ((8, CONV_CH), f32),
        ],
        after(
            (
                dssd, ycore, x, bc, step, cum, z, off, entry, downstream, skip, decay_row, chan,
                w_conv, b_conv, dxw, dscores,
            ),
            red_one.sent,
        ),
        scratch=[((rows, CONV_CH), f32)],
        flops=8 * rows * DS * 128,
    )
    count = lax.axis_size(AXES)
    small_got = swap(small, core_unit)
    gab, norm_keep = run(
        functools.partial(back_grads_kernel, ys),
        "back_grads",
        [((rows + RIM, A_COLS + DS + width // 2), bf16), ((rows + RIM, width // 2), bf16)],
        (side, dq, dkv_got, dext, dz, cos, sin, normed, nrim),
        scalars=1,
    )
    gab_got = swap(gab, core_unit)
    red_two.fold_one(gab)
    small = small + after(small_got, gab)
    per_device = jnp.concatenate(
        [
            small[: CONV + 1].reshape(CONV + 1, count, -1).transpose(1, 0, 2).reshape(count, -1),
            jnp.broadcast_to(
                small[CONV + 1, : 3 * LANES].reshape(3, LANES)[:, :SSM_HEADS].reshape(1, -1),
                (count, 3 * SSM_HEADS),
            ),
        ],
        1,
    )
    slots = per_device.shape[1]
    free = LANES - SSM_HEADS
    per_device = lax.dynamic_index_in_dim(
        per_device.reshape(ys, 2, others, slots), place_on("core"), 1, False
    )
    extra = jnp.pad(per_device, ((0, 0), (0, 0), (0, part * free - slots)))
    extra = extra.reshape(ys, others * part, free)
    aside = 512 if A_COLS % 512 == 0 else A_COLS % 512
    extra = jnp.pad(extra, ((0, 0), (0, 0), (aside - free, 0)))
    grad_tokens, grad_rim = run(
        back_kernel,
        "back",
        [((rows, width), f32), ((RIM, width), f32)],
        (
            side, after(gab, red_two.sent), wa_own, wa_oth, wb_own, wb_oth, tokens_rim, dmid, dng,
            gain_one,
        ),
        scalars=1,
        scratch=[((rows + RIM, width), f32)],
        flops=2 * rows * width * (A_COLS + DS),
    )
    rim_got = shifted(grad_rim, -1)
    norm_keep, gab, gab_got, extra = after((norm_keep, gab, gab_got, extra), grad_tokens)
    red_three = weight_sums(
        "front_weights",
        [(0, A_COLS + DS, sizes[4], 0, A_COLS)],
        [(0, A_COLS + DS, sizes[4], A_COLS, DS)],
        norm_keep,
        gab,
        gab_got,
        (extra,),
    )
    red_one.fold_two(red_three.sent)
    red_two.fold_two(red_one.sent)
    red_three.fold_one(red_two.sent)
    r_one, r_down = red_one.fold_three(red_three.sent)
    red_three.fold_two(r_one)
    r_two, r_out = red_two.fold_three(red_three.sent)
    rim_got = after(rim_got, r_two)
    grad_tokens = grad_tokens.at[rows - RIM :].add(rim_got)
    r_e, r_f = red_three.fold_three(grad_tokens)
    r_gu = jnp.concatenate([r_one, r_two[:, :ff]], 1)
    small = r_e[:, A_COLS - free :].reshape(-1)[:slots]
    conv = small[: (CONV + 1) * conv_bias.size].reshape(CONV + 1, -1)
    heads = small[(CONV + 1) * conv_bias.size :].reshape(3, SSM_HEADS)
    g_inner = jnp.concatenate([r_two[:, ff:], r_f, r_e[:, 768 : 1024 + SSM_HEADS]], 1)
    g_mixer, g_ssm, g_ffn = run(
        functools.partial(
            gain_kernel, [(0, 0, 1), (0, 2, 3), (0, 4, 5), (1, 6, 7), (2, 8, 9)], 3
        ),
        "gains",
        [((part, 1), f32), ((s_rows, 1), f32), ((part, 1), f32)],
        (
            mixer_gain[:, None], ssm_gain[:, None], ffn_gain[:, None],
            keyval_weight, r_e[:, :256], query_weight, r_e[:, 256:768], inner_weight, g_inner,
            ssm_out_weight, r_out[a_rows:], gate_up_weight, r_gu,
        ),
    )
    return (
        output,
        grad_tokens,
        g_mixer[:, 0],
        r_e[:, 256:768],
        r_e[:, :256],
        g_inner,
        conv[:CONV].T,
        conv[CONV],
        g_ssm[:, 0],
        r_out[:a_rows],
        r_out[a_rows:],
        g_ffn[:, 0],
        r_gu,
        r_down,
        heads[0],
        heads[1],
        heads[2],
    )


def solution(mesh):
    across, along = mesh.shape["dp"], mesh.shape["seq"]
    mesh = jax.sharding.Mesh(mesh.devices.reshape(across // 2, 2, along // 2, 2), AXES)
    lead, flat, rep = P(AXES, None), P(AXES), P()
    return jax.shard_map(
        local,
        mesh=mesh,
        in_specs=(
            lead, P(AXES[:2], None), lead, flat, lead, lead, lead, lead, flat, flat, lead, lead, flat,
            lead, lead, rep, rep, rep,
        ),
        out_specs=(
            lead, lead, flat, lead, lead, lead, lead, flat, flat, lead, lead, flat, lead, lead,
            rep, rep, rep,
        ),
        check_vma=False,
    )
```

time: 668 us -> 541 us (0.81)
  waiting for transfers between devices: 245 us -> 185 us
  starting transfers between devices: 149 us -> 93.6 us
  other arithmetic: 56 us -> 24.9 us
  Pallas kernels: 135 us -> 156 us
  local copies, waits for them, and re-layouts: 66.5 us -> 53.2 us
  between operations: 5.06 us -> 17.9 us
    ppermute x71 -> x28, waiting for transfers between devices: 223 us -> 92.7 us  [swap(): return lax.ppermute(array, AXES, [(i, i ^ mask) for i in range(count)])]
    ppermute x71 -> x28, starting transfers between devices: 107 us -> 28.6 us  [swap(): return lax.ppermute(array, AXES, [(i, i ^ mask) for i in range(count)])]
    all_to_all x0 -> x6, starting transfers between devices: none -> 47.1 us  [dealt(): return lax.all_to_all(array, axes, 0, 0, tiled=True)]
    all_gather x0 -> x1, waiting for transfers between devices: none -> 26.1 us  [local(): packed = lax.all_gather(packed, ('y', 'z', 'x'), axis=0)]
    ppermute x16 -> x8, starting transfers between devices: 42.7 us -> 17.9 us  [shifted(): return lax.ppermute(array, SEQ, pairs)]
    all_to_all x0 -> x6, waiting for transfers between devices: none -> 24.3 us  [dealt(): return lax.all_to_all(array, axes, 0, 0, tiled=True)]
    pallas_call x12 -> x22, Pallas kernels: 135 us -> 156 us  [run(): pl.pallas_call(kernel, name=name, out_shape=shapes, in_specs=specs, out_s...]
    ppermute x16 -> x8, waiting for transfers between devices: 21.5 us -> 42.1 us  [shifted(): return lax.ppermute(array, SEQ, pairs)]
  transfers between devices with their start and end apart: 87 -> 43, of which waited for: 27 -> 20; matrix products, arithmetic and copies ran while one was open for 16% -> 9% of each run, Pallas kernels for 16% -> 22%
where the time goes in v2:
time: 541 us; the launch traced here: 531 us
  waiting for transfers between devices  185 us (34%)
  Pallas kernels  156 us (29%)
  starting transfers between devices  93.6 us (17%)
  local copies, waits for them, and re-layouts  53.2 us (10%)
  other arithmetic  24.9 us (5%)
  between operations  17.9 us (3%)
    pallas_call x22, Pallas kernels, run(): pl.pallas_call(kernel, name=name, out_shape=shapes, in_specs=specs, out_s...  156 us
    ppermute x28, waiting for transfers between devices, swap(): return lax.ppermute(array, AXES, [(i, i ^ mask) for i in range(count)])  92.7 us
    all_to_all x6, starting transfers between devices, dealt(): return lax.all_to_all(array, axes, 0, 0, tiled=True)  47.1 us
    ppermute x8, waiting for transfers between devices, shifted(): return lax.ppermute(array, SEQ, pairs)  42.1 us
    ppermute x28, starting transfers between devices, swap(): return lax.ppermute(array, AXES, [(i, i ^ mask) for i in range(count)])  28.6 us
    all_gather x1, waiting for transfers between devices, local(): packed = lax.all_gather(packed, ('y', 'z', 'x'), axis=0)  26.1 us
    all_to_all x6, waiting for transfers between devices, dealt(): return lax.all_to_all(array, axes, 0, 0, tiled=True)  24.3 us
    ppermute x8, starting transfers between devices, shifted(): return lax.ppermute(array, SEQ, pairs)  17.9 us
  transfers between devices with their start and end apart: 43, of which 20 were waited for; matrix products, arithmetic and copies ran while one was open for 9% of the time, Pallas kernels for 22%

profile of v2, /device:TPU:0, one launch (start us, length us, event | category | flops | bytes accessed | tf_op | source)
XLA Modules:
  0.0 531.1 jit_solution(5352586362342116711)
XLA Ops:
  39.8 18.7 %all-to-all-done = bf16[4,32,2688]{2,1,0:T(8,128)(2,1)S(1)} async-done(((bf16[4,32,2688]{2,1,0:T(8,128)(2,1)}), bf16[4,32,2688]{2,1,0:T(8,128)(2,1)S(1)}, u32[]{:S(2)}, u32[]{:S(2)}) %all-to-all-start) | async-done | bytes 688160 | tf_op jit(solution)/shard_map/all_to_all | solution.py:175
  64.0 9.1 %collective-permute-done.10 = bf16[4,32,1536]{2,1,0:T(8,128)(2,1)S(1)} collective-permute-done((bf16[4,32,1536]{2,1,0:T(8,128)(2,1)S(1)}, bf16[4,32,1536]{2,1,0:T(8,128)(2,1)S(1)}, u32[]{:S(2)}, u32[]{:S(2)}) %collective-permute-start.10) | collective-permute-done | bytes 393248 | tf_op jit(solution)/shard_map/ppermute | solution.py:95
  78.9 18.5 %collective-permute-done.11 = bf16[4,2,32,1536]{3,2,1,0:T(8,128)(2,1)S(1)} collective-permute-done((bf16[4,2,32,1536]{3,2,1,0:T(8,128)(2,1)S(1)}, bf16[4,2,32,1536]{3,2,1,0:T(8,128)(2,1)S(1)}, u32[]{:S(2)}, u32[]{:S(2)}) %collective-permute-start.11) | collective-permute-done | bytes 786464 | tf_op jit(solution)/shard_map/ppermute | solution.py:95
  117.1 8.3 %front.1 = (bf16[8,256,128]{2,1,0:T(8,128)(2,1)}, bf16[256,256]{1,0:T(8,128)(2,1)}, bf16[256,1024]{1,0:T(8,128)(2,1)}, bf16[16,1024]{1,0:T(8,128)(2,1)}, bf16[27...) custom-call(s32[1]{0:T(128)} %bitcast.core_ref, ...), custom_call_target="tpu_custom_call" | custom-call | flops 1409286144 | bytes 11728388 | tf_op jit(solution)/shard_map/front/pallas_call | solution.py:1020
  131.4 7.7 %scan.1.yl_ref = f32[256,1536]{1,0:T(8,128)} custom-call(f32[256,1536]{1,0:T(8,128)} %get-tuple-element.249.x_ref, f32[256,256]{1,0:T(8,128)} %get-tuple-element.250.bc_ref, f32[256,128]{1,0:T(8,128)} %get-tuple-element.251.step_ref, f32[256,128]{1,0:T(8,128)} %get-tuple-element.252.cum_ref, f32[128,256]{1,0:T(8,128)} %get-tuple-element.237.cumt_ref, ...), custom_call_target="tpu_custom_call" | custom-call | flops 402653184 | bytes 3802112 | tf_op jit(solution)/shard_map/scan/pallas_call | solution.py:1020
  139.1 8.4 %collective-permute-done.13 = bf16[1552,128]{1,0:T(8,128)(2,1)S(1)} collective-permute-done((bf16[1552,128]{1,0:T(8,128)(2,1)S(1)}, bf16[1552,128]{1,0:T(8,128)(2,1)S(1)}, u32[]{:S(2)}, u32[]{:S(2)}) %collective-permute-start.13) | collective-permute-done | bytes 397344 | tf_op jit(solution)/shard_map/ppermute | solution.py:185
  149.4 26.1 %all-gather.3.cloned.1.call-done = bf16[4864,1024]{1,0:T(8,128)(2,1)} async-done(((bf16[304,1024]{1,0:T(8,128)(2,1)}), bf16[4864,1024]{1,0:T(8,128)(2,1)}) %all-gather.3.cloned.1.call-update) | async-done | bytes 9961488 | tf_op jit(solution)/shard_map/all_gather | solution.py:1092
  176.6 9.8 %all-to-all-start.1 = ((bf16[8,256,256]{2,1,0:T(8,128)(2,1)}), bf16[8,256,256]{2,1,0:T(8,128)(2,1)S(1)}, u32[]{:S(2)}, u32[]{:S(2)}) async-start(bf16[8,256,256]{2,1,0:T(8,128)(2,1)} %broadcast_in_dim.70), calls=%async_computation.1 | async-start | bytes 2097152 | tf_op jit(solution)/shard_map/all_to_all | solution.py:175
  193.8 19.9 %collective-permute-done.15 = bf16[1552,128]{1,0:T(8,128)(2,1)} collective-permute-done((bf16[1552,128]{1,0:T(8,128)(2,1)S(1)}, bf16[1552,128]{1,0:T(8,128)(2,1)}, u32[]{:S(2)}, u32[]{:S(2)}) %collective-permute-start.15) | collective-permute-done | bytes 397344 | tf_op jit(solution)/shard_map/ppermute | solution.py:185
  217.0 10.3 %attend.1 = (bf16[256,512]{1,0:T(8,128)(2,1)}, f32[128,256]{1,0:T(8,128)}) custom-call(s32[1]{0:T(128)} %bitcast.1.rank_ref, bf16[8,256,128]{2,1,0:T(8,128)(2,1)} %get-tuple-element.204.q8_ref, bf16[8,256,256]{2,1,0:T(8,128)(2,1)} %copy-done.4, s32[256,1]{1,0:T(8,128)} %select_subtract_fusion.off_ref), custom_call_target="tpu_custom_call" | custom-call | flops 1342177280 | bytes 1967108 | tf_op jit(solution)/shard_map/attend/pallas_call | solution.py:1020
  227.3 29.8 %post.1 = (bf16[256,1024]{1,0:T(8,128)(2,1)}, f32[256,1024]{1,0:T(8,128)}, bf16[256,512]{1,0:T(8,128)(2,1)}, f32[256,1536]{1,0:T(8,128)}, f32[256,1536]{1,0:T(8,...) custom-call(s32[1]{0:T(128)} %bitcast.core_ref, ...), custom_call_target="tpu_custom_call" | custom-call | flops 10200547328 | bytes 39994372 | tf_op jit(solution)/shard_map/post/pallas_call | solution.py:1020
  263.7 14.3 %attend_back.1 = (bf16[256,512]{1,0:T(8,128)(2,1)}, bf16[8,256,256]{2,1,0:T(8,128)(2,1)}) custom-call(s32[1]{0:T(128)} %bitcast.1.rank_ref, bf16[8,256,128]{2,1,0:T(8,128)(2,1)} %get-tuple-element.204.q8_ref, bf16[8,256,256]{2,1,0:T(8,128)(2,1)} %copy-done.4, s32[1,256]{1,0:T(1,128)} %fusion.18.off_ref, f32[128,256]{1,0:T(8,128)} %get-tuple-element.207.lse_ref, ...), custom_call_target="tpu_custom_call" | custom-call | flops 3355443200 | bytes 3539972 | tf_op jit(solution)/shard_map/attend_back/pallas_call | solution.py:1020
  278.0 14.6 %all-to-all-start.2 = ((bf16[8,256,256]{2,1,0:T(8,128)(2,1)}), bf16[8,256,256]{2,1,0:T(8,128)(2,1)}, u32[]{:S(2)}, u32[]{:S(2)}) async-start(bf16[8,256,256]{2,1,0:T(8,128)(2,1)} %get-tuple-element.212), calls=%async_computation.2 | async-start | bytes 2097152 | tf_op jit(solution)/shard_map/all_to_all | solution.py:175
  296.3 8.0 %weights_one.1 = (bf16[2,4,32,2048]{3,2,1,0:T(8,128)(2,1)}, bf16[2,4,32,2048]{3,2,1,0:T(8,128)(2,1)}, bf16[8,64,1024]{2,1,0:T(8,128)(2,1)}, bf16[8,64,1024]{2,1,0:T(8,128)(2,1)}) custom-call(s32[1]{0:T(128)} %bitcast.39.y_ref, s32[1]{0:T(128)} %bitcast.40.x_ref, bf16[256,3072]{1,0:T(8,128)(2,1)} %get-tuple-element.227.keep_ref, ...), custom_call_target="tpu_custom_call" | custom-call | flops 2147483648 | bytes 16777224 | tf_op jit(solution)/shard_map/weights_one/pallas_call | solution.py:1020
  308.0 12.6 %collective-permute-done.19 = bf16[1552,128]{1,0:T(8,128)(2,1)} collective-permute-done((bf16[1552,128]{1,0:T(8,128)(2,1)S(1)}, bf16[1552,128]{1,0:T(8,128)(2,1)}, u32[]{:S(2)}, u32[]{:S(2)}) %collective-permute-start.19) | collective-permute-done | bytes 397344 | tf_op jit(solution)/shard_map/ppermute | solution.py:185
  322.9 9.4 %weights_two.1 = (bf16[2,4,32,3584]{3,2,1,0:T(8,128)(2,1)}, bf16[2,4,32,3584]{3,2,1,0:T(8,128)(2,1)}, bf16[8,64,1024]{2,1,0:T(8,128)(2,1)}, bf16[8,64,1024]{2,1,0:T(8,128)(2,1)}) custom-call(s32[1]{0:T(128)} %bitcast.39.y_ref, s32[1]{0:T(128)} %bitcast.40.x_ref, bf16[256,3072]{1,0:T(8,128)(2,1)} %get-tuple-element.227.keep_ref, ...), custom_call_target="tpu_custom_call" | custom-call | flops 2952790016 | bytes 18350088 | tf_op jit(solution)/shard_map/weights_two/pallas_call | solution.py:1020
  333.7 8.8 %scan_back.1 = (f32[256,1536]{1,0:T(8,128)}, bf16[256,256]{1,0:T(8,128)(2,1)}) custom-call(f32[256,1536]{1,0:T(8,128)} %get-tuple-element.247.dy_ref, f32[256,1536]{1,0:T(8,128)} %get-tuple-element.249.x_ref, f32[256,256]{1,0:T(8,128)} %get-tuple-element.250.bc_ref, f32[256,128]{1,0:T(8,128)} %get-tuple-element.251.step_ref, ...), custom_call_target="tpu_custom_call" | custom-call | flops 805306368 | bytes 5506048 | tf_op jit(solution)/shard_map/scan_back/pallas_call | solution.py:1020
  346.6 12.6 %mixer_back.1 = (f32[272,1792]{1,0:T(8,128)}, f32[256,128]{1,0:T(8,128)}, f32[8,1792]{1,0:T(8,128)}) custom-call(f32[256,1536]{1,0:T(8,128)} %get-tuple-element.247.dy_ref, f32[256,1536]{1,0:T(8,128)} %get-tuple-element.248.ycore_ref, f32[256,1536]{1,0:T(8,128)} %get-tuple-element.249.x_ref, f32[256,256]{1,0:T(8,128)} %get-tuple-element.250.bc_ref, ...), custom_call_target="tpu_custom_call" | custom-call | flops 402653184 | bytes 11835904 | tf_op jit(solution)/shard_map/mixer_back/pallas_call | solution.py:1020
  368.9 20.2 %collective-permute-done.24.ygot_ref = bf16[8,64,1024]{2,1,0:T(8,128)(2,1)S(1)} collective-permute-done((bf16[8,64,1024]{2,1,0:T(8,128)(2,1)}, bf16[8,64,1024]{2,1,0:T(8,128)(2,1)S(1)}, u32[]{:S(2)}, u32[]{:S(2)}) %collective-permute-start.24) | collective-permute-done | bytes 1048608 | tf_op jit(solution)/shard_map/ppermute | solution.py:95
  396.5 6.9 %back.1 = (f32[256,1024]{1,0:T(8,128)}, f32[16,1024]{1,0:T(8,128)}) custom-call(s32[1]{0:T(128)} %bitcast.core_ref, bf16[272,3200]{1,0:T(8,128)(2,1)} %get-tuple-element.285.gab_ref.own_ref, bf16[2,256,1152]{2,1,0:T(8,128)(2,1)} %bitcast.72, bf16[2,256,1152]{2,1,0:T(8,128)(2,1)} %bitcast.74, bf16[2,256,1536]{2,1,0:T(8,128)(2,1)} %pad_maximum_fusion.wb_own, ...), custom_call_target="tpu_custom_call" | custom-call | flops 1409286144 | bytes 11018244 | tf_op jit(solution)/shard_map/back/pallas_call | solution.py:1020
  412.7 8.5 %all-to-all-start.4 = ((bf16[4,256,512]{2,1,0:T(8,128)(2,1)}), bf16[4,256,512]{2,1,0:T(8,128)(2,1)S(1)}, u32[]{:S(2)}, u32[]{:S(2)}) async-start(bf16[4,256,512]{2,1,0:T(8,128)(2,1)} %fold_two.3), calls=%async_computation.4 | async-start | bytes 2097152 | tf_op jit(solution)/shard_map/all_to_all | solution.py:175
  423.4 12.0 %collective-permute-done.27.ygot_ref = bf16[4,64,1024]{2,1,0:T(8,128)(2,1)S(1)} collective-permute-done((bf16[4,64,1024]{2,1,0:T(8,128)(2,1)S(1)}, bf16[4,64,1024]{2,1,0:T(8,128)(2,1)S(1)}, u32[]{:S(2)}, u32[]{:S(2)}) %collective-permute-start.27) | collective-permute-done | bytes 524320 | tf_op jit(solution)/shard_map/ppermute | solution.py:95
  435.3 7.2 %collective-permute-done.26.xgot_ref = bf16[4,32,3584]{2,1,0:T(8,128)(2,1)S(1)} collective-permute-done((bf16[4,32,3584]{2,1,0:T(8,128)(2,1)S(1)}, bf16[4,32,3584]{2,1,0:T(8,128)(2,1)S(1)}, u32[]{:S(2)}, u32[]{:S(2)}) %collective-permute-start.26) | collective-permute-done | bytes 917536 | tf_op jit(solution)/shard_map/ppermute | solution.py:95
  455.0 11.9 %collective-permute-done.32.xgot_ref = bf16[2,4,32,1152]{3,2,1,0:T(8,128)(2,1)S(1)} collective-permute-done((bf16[2,4,32,1152]{3,2,1,0:T(8,128)(2,1)S(1)}, bf16[2,4,32,1152]{3,2,1,0:T(8,128)(2,1)S(1)}, u32[]{:S(2)}, u32[]{:S(2)}) %collective-permute-start.32) | collective-permute-done | bytes 589856 | tf_op jit(solution)/shard_map/ppermute | solution.py:95
  (297 shorter events, 199.9 us)
Async XLA Ops:
  7.3 168.2 %all-gather.3.cloned.1.call-start = ((), (), s32[]{:S(2)}) async-start(), calls=%async_computation.6 | async-start | bytes 10584064 | tf_op jit(solution)/shard_map/all_gather | solution.py:1092
  16.2 21.5 %collective-permute-start.1 = (f32[512]{0:T(512)S(1)}, f32[512]{0:T(512)S(1)}, u32[]{:S(2)}, u32[]{:S(2)}) collective-permute-start(f32[512]{0:T(512)S(1)} %pad_convert_fusion.1), channel_id=1, source_target_pairs={{0,6},{1,7},{2,4},{3,5},{4,2},{5,3},{6,0},{7,1},{8,14},{9,15},{10,... | collective-permute-start | bytes 6152 | tf_op jit(solution)/shard_map/ppermute | solution.py:95
  22.9 35.6 %all-to-all-start = ((bf16[4,32,2688]{2,1,0:T(8,128)(2,1)}), bf16[4,32,2688]{2,1,0:T(8,128)(2,1)S(1)}, u32[]{:S(2)}, u32[]{:S(2)}) async-start(bf16[4,32,2688]{2,1,0:T(8,128)(2,1)} %broadcast_in_dim.65), calls=%async_computation | async-start | bytes 1376256 | tf_op jit(solution)/shard_map/all_to_all | solution.py:175
  28.8 72.3 %collective-permute-start = (bf16[16,1024]{1,0:T(8,128)(2,1)S(1)}, bf16[16,1024]{1,0:T(8,128)(2,1)S(1)}, u32[]{:S(2)}, u32[]{:S(2)}) collective-permute-start(bf16[16,1024]{1,0:T(8,128)(2,1)S(1)} %slice.208), channel_id=1, source_target_pairs={{0,1},{1,2},{2,3},{3,4},{4,5},{5,6},{6,7},{8,9},{9,10},{10,11},{11... | collective-permute-start | bytes 98312 | tf_op jit(solution)/shard_map/ppermute | solution.py:185
  37.7 24.4 %collective-permute-start.4 = (f32[4,512]{1,0:T(4,128)S(1)}, f32[4,512]{1,0:T(4,128)S(1)}, u32[]{:S(2)}, u32[]{:S(2)}) collective-permute-start(f32[4,512]{1,0:T(4,128)S(1)} %pad_maximum_fusion.14), channel_id=1, source_target_pairs={{0,1},{1,0},{2,3},{3,2},{4,5},{5,4},{6,7},{7,6},{8,9},{9,8},{10,11... | collective-permute-start | bytes 24584 | tf_op jit(solution)/shard_map/ppermute | solution.py:95
  73.2 24.3 %collective-permute-start.11 = (bf16[4,2,32,1536]{3,2,1,0:T(8,128)(2,1)S(1)}, bf16[4,2,32,1536]{3,2,1,0:T(8,128)(2,1)S(1)}, u32[]{:S(2)}, u32[]{:S(2)}) collective-permute-start(bf16[4,2,32,1536]{3,2,1,0:T(8,128)(2,1)S(1)} %pad_maximum_fusion.3), channel_id=1, source_target_pairs={{0,16},{1,17},{2,18},{3,19},{4,20},{5,21},{6,22},{7,23},{8,24},{9,... | collective-permute-start | bytes 2359304 | tf_op jit(solution)/shard_map/ppermute | solution.py:95
  175.5 51.8 %collective-permute-start.16 = (bf16[2,8,304,1024]{3,2,1,0:T(8,128)(2,1)}, bf16[2,8,304,1024]{3,2,1,0:T(8,128)(2,1)}, u32[]{:S(2)}, u32[]{:S(2)}) collective-permute-start(bf16[2,8,304,1024]{3,2,1,0:T(8,128)(2,1)} %bitcast.101), channel_id=1, source_target_pairs={{0,8},{1,9},{2,10},{3,11},{4,12},{5,13},{6,14},{7,15},{8,0},{9,1},... | collective-permute-start | bytes 29884424 | tf_op jit(solution)/shard_map/ppermute | solution.py:95
  176.6 39.5 %all-to-all-start.1 = ((bf16[8,256,256]{2,1,0:T(8,128)(2,1)}), bf16[8,256,256]{2,1,0:T(8,128)(2,1)S(1)}, u32[]{:S(2)}, u32[]{:S(2)}) async-start(bf16[8,256,256]{2,1,0:T(8,128)(2,1)} %broadcast_in_dim.70), calls=%async_computation.1 | async-start | bytes 2097152 | tf_op jit(solution)/shard_map/all_to_all | solution.py:175
  186.4 27.3 %collective-permute-start.15 = (bf16[1552,128]{1,0:T(8,128)(2,1)S(1)}, bf16[1552,128]{1,0:T(8,128)(2,1)}, u32[]{:S(2)}, u32[]{:S(2)}) collective-permute-start(bf16[1552,128]{1,0:T(8,128)(2,1)S(1)} %fusion.4), channel_id=1, source_target_pairs={{0,2},{1,3},{2,4},{3,5},{4,6},{5,7},{8,10},{9,11},{10,12},{11,13},... | collective-permute-start | bytes 1191944 | tf_op jit(solution)/shard_map/ppermute | solution.py:185
  257.1 39.1 %collective-permute-start.20 = (bf16[256,10752]{1,0:T(8,128)(2,1)}, bf16[256,10752]{1,0:T(8,128)(2,1)}, u32[]{:S(2)}, u32[]{:S(2)}) collective-permute-start(bf16[256,10752]{1,0:T(8,128)(2,1)} %get-tuple-element.228.own_ref), channel_id=1, source_target_pairs={{0,8},{1,9},{2,10},{3,11},{4,12},{5,13},{6,14},{7,15},{8,0},{9,1},... | collective-permute-start | bytes 16515080 | tf_op jit(solution)/shard_map/ppermute | solution.py:95
  258.4 34.2 %collective-permute-start.17 = (bf16[1552,128]{1,0:T(8,128)(2,1)S(1)}, bf16[1552,128]{1,0:T(8,128)(2,1)S(1)}, u32[]{:S(2)}, u32[]{:S(2)}) collective-permute-start(bf16[1552,128]{1,0:T(8,128)(2,1)S(1)} %pad_maximum_fusion.5), channel_id=1, source_target_pairs={{1,0},{2,1},{3,2},{4,3},{5,4},{6,5},{7,6},{9,8},{10,9},{11,10},{12... | collective-permute-start | bytes 1191944 | tf_op jit(solution)/shard_map/ppermute | solution.py:185
  259.7 32.9 %collective-permute-start.18 = (bf16[1552,128]{1,0:T(8,128)(2,1)S(1)}, bf16[1552,128]{1,0:T(8,128)(2,1)S(1)}, u32[]{:S(2)}, u32[]{:S(2)}) collective-permute-start(bf16[1552,128]{1,0:T(8,128)(2,1)S(1)} %pad_maximum_fusion.5), channel_id=1, source_target_pairs={{2,0},{3,1},{4,2},{5,3},{6,4},{7,5},{10,8},{11,9},{12,10},{13,11},... | collective-permute-start | bytes 1191944 | tf_op jit(solution)/shard_map/ppermute | solution.py:185
  278.0 81.2 %all-to-all-start.2 = ((bf16[8,256,256]{2,1,0:T(8,128)(2,1)}), bf16[8,256,256]{2,1,0:T(8,128)(2,1)}, u32[]{:S(2)}, u32[]{:S(2)}) async-start(bf16[8,256,256]{2,1,0:T(8,128)(2,1)} %get-tuple-element.212), calls=%async_computation.2 | async-start | bytes 2097152 | tf_op jit(solution)/shard_map/all_to_all | solution.py:175
  295.0 25.6 %collective-permute-start.19 = (bf16[1552,128]{1,0:T(8,128)(2,1)S(1)}, bf16[1552,128]{1,0:T(8,128)(2,1)}, u32[]{:S(2)}, u32[]{:S(2)}) collective-permute-start(bf16[1552,128]{1,0:T(8,128)(2,1)S(1)} %fusion.5), channel_id=1, source_target_pairs={{2,0},{3,1},{4,2},{5,3},{6,4},{7,5},{10,8},{11,9},{12,10},{13,11},... | collective-permute-start | bytes 1191944 | tf_op jit(solution)/shard_map/ppermute | solution.py:185
  304.3 38.2 %collective-permute-start.21 = (bf16[2,4,32,2048]{3,2,1,0:T(8,128)(2,1)}, bf16[2,4,32,2048]{3,2,1,0:T(8,128)(2,1)}, u32[]{:S(2)}, u32[]{:S(2)}) collective-permute-start(bf16[2,4,32,2048]{3,2,1,0:T(8,128)(2,1)} %get-tuple-element.223), channel_id=1, source_target_pairs={{0,1},{1,0},{2,3},{3,2},{4,5},{5,4},{6,7},{7,6},{8,9},{9,8},{10,11... | collective-permute-start | bytes 3145736 | tf_op jit(solution)/shard_map/ppermute | solution.py:95
  306.3 36.2 %collective-permute-start.22 = (bf16[8,64,1024]{2,1,0:T(8,128)(2,1)}, bf16[8,64,1024]{2,1,0:T(8,128)(2,1)}, u32[]{:S(2)}, u32[]{:S(2)}) collective-permute-start(bf16[8,64,1024]{2,1,0:T(8,128)(2,1)} %get-tuple-element.224), channel_id=1, source_target_pairs={{0,16},{1,17},{2,18},{3,19},{4,20},{5,21},{6,22},{7,23},{8,24},{9,... | collective-permute-start | bytes 3145736 | tf_op jit(solution)/shard_map/ppermute | solution.py:95
  332.3 56.9 %collective-permute-start.23 = (bf16[2,4,32,3584]{3,2,1,0:T(8,128)(2,1)}, bf16[2,4,32,3584]{3,2,1,0:T(8,128)(2,1)S(1)}, u32[]{:S(2)}, u32[]{:S(2)}) collective-permute-start(bf16[2,4,32,3584]{3,2,1,0:T(8,128)(2,1)} %get-tuple-element.230), channel_id=1, source_target_pairs={{0,1},{1,0},{2,3},{3,2},{4,5},{5,4},{6,7},{7,6},{8,9},{9,8},{10,11... | collective-permute-start | bytes 5505032 | tf_op jit(solution)/shard_map/ppermute | solution.py:95
  363.0 40.4 %collective-permute-start.30 = (bf16[272,3200]{1,0:T(8,128)(2,1)}, bf16[272,3200]{1,0:T(8,128)(2,1)}, u32[]{:S(2)}, u32[]{:S(2)}) collective-permute-start(bf16[272,3200]{1,0:T(8,128)(2,1)} %get-tuple-element.285.gab_ref.own_ref), channel_id=1, source_target_pairs={{0,8},{1,9},{2,10},{3,11},{4,12},{5,13},{6,14},{7,15},{8,0},{9,1},... | collective-permute-start | bytes 5222408 | tf_op jit(solution)/shard_map/ppermute | solution.py:95
  363.0 26.2 %collective-permute-start.24 = (bf16[8,64,1024]{2,1,0:T(8,128)(2,1)}, bf16[8,64,1024]{2,1,0:T(8,128)(2,1)S(1)}, u32[]{:S(2)}, u32[]{:S(2)}) collective-permute-start(bf16[8,64,1024]{2,1,0:T(8,128)(2,1)} %get-tuple-element.231), channel_id=1, source_target_pairs={{0,16},{1,17},{2,18},{3,19},{4,20},{5,21},{6,22},{7,23},{8,24},{9,... | collective-permute-start | bytes 3145736 | tf_op jit(solution)/shard_map/ppermute | solution.py:95
  364.7 45.0 %collective-permute-start.28 = (bf16[4,32,2048]{2,1,0:T(8,128)(2,1)}, bf16[4,32,2048]{2,1,0:T(8,128)(2,1)}, u32[]{:S(2)}, u32[]{:S(2)}) collective-permute-start(bf16[4,32,2048]{2,1,0:T(8,128)(2,1)} %get-tuple-element.245), channel_id=1, source_target_pairs={{0,16},{1,17},{2,18},{3,19},{4,20},{5,21},{6,22},{7,23},{8,24},{9,... | collective-permute-start | bytes 1572872 | tf_op jit(solution)/shard_map/ppermute | solution.py:95
  366.7 43.0 %collective-permute-start.29 = (bf16[4,64,1024]{2,1,0:T(8,128)(2,1)}, bf16[4,64,1024]{2,1,0:T(8,128)(2,1)}, u32[]{:S(2)}, u32[]{:S(2)}) collective-permute-start(bf16[4,64,1024]{2,1,0:T(8,128)(2,1)} %get-tuple-element.246), channel_id=1, source_target_pairs={{0,1},{1,0},{2,3},{3,2},{4,5},{5,4},{6,7},{7,6},{8,9},{9,8},{10,11... | collective-permute-start | bytes 1572872 | tf_op jit(solution)/shard_map/ppermute | solution.py:95
  412.7 34.3 %all-to-all-start.4 = ((bf16[4,256,512]{2,1,0:T(8,128)(2,1)}), bf16[4,256,512]{2,1,0:T(8,128)(2,1)S(1)}, u32[]{:S(2)}, u32[]{:S(2)}) async-start(bf16[4,256,512]{2,1,0:T(8,128)(2,1)} %fold_two.3), calls=%async_computation.4 | async-start | bytes 2097152 | tf_op jit(solution)/shard_map/all_to_all | solution.py:175
  448.0 37.0 %all-to-all-start.3 = ((bf16[4,352,512]{2,1,0:T(8,128)(2,1)}), bf16[4,352,512]{2,1,0:T(8,128)(2,1)S(1)}, u32[]{:S(2)}, u32[]{:S(2)}) async-start(bf16[4,352,512]{2,1,0:T(8,128)(2,1)} %fold_two.4), calls=%async_computation.3 | async-start | bytes 2883584 | tf_op jit(solution)/shard_map/all_to_all | solution.py:175
  485.0 22.4 %all-to-all-start.5 = ((bf16[4,224,384]{2,1,0:T(8,128)(2,1)}), bf16[4,224,384]{2,1,0:T(8,128)(2,1)}, u32[]{:S(2)}, u32[]{:S(2)}) async-start(bf16[4,224,384]{2,1,0:T(8,128)(2,1)} %fold_two.5), calls=%async_computation.5 | async-start | bytes 1376256 | tf_op jit(solution)/shard_map/all_to_all | solution.py:175
  (56 other events, 590.6 us)
Sparse Core Ops, SparseCore 0:
  15.9 159.4 all-gather.2

commit v3 on v2

--- a/solution.py
+++ b/solution.py
@@ -22,6 +22,7 @@
 EPS = 1e-6
 BASE = 10000.0
 NEG = -1e30
+SCALE = 6_600_000_000
 AXES = ("y", "core", "z", "x")
 SEQ = AXES[2:]
 
@@ -295,6 +296,31 @@
 def carry_of(cum, off):
     rows = cum.shape[0]
     return jnp.exp(cum[rows - 1 :, :]) * (off[rows - 1 :, :] >= rows).astype(f32)
+
+
+def pack_kernel(
+    gu_ref, inner_ref, ao_ref, so_ref, down_ref, kv_ref, q_ref, post_ref, front_ref
+):
+    part, width = gu_ref.shape[0], down_ref.shape[1]
+    a_rows = ao_ref.shape[0]
+    post_ref[:part, :] = inner_ref[:, :width]
+    post_ref[part : 2 * part, : DS - width] = inner_ref[:, width:DS]
+    for k in range(2):
+        rows = slice(part + k * a_rows, part + (k + 1) * a_rows)
+        post_ref[rows, DS - width :] = ao_ref[:, k * 512 : (k + 1) * 512]
+    at = 2 * part
+    post_ref[at : at + so_ref.shape[0], :] = so_ref[...]
+    at += so_ref.shape[0]
+    for k in range(gu_ref.shape[1] // width):
+        post_ref[at : at + part, :] = gu_ref[:, k * width : (k + 1) * width]
+        at += part
+    post_ref[at:, :] = down_ref[...]
+    front_ref[:, :256] = kv_ref[...]
+    front_ref[:, 256:768] = q_ref[...]
+    front_ref[:, 768:1024] = inner_ref[:, 2 * DS : DS + CONV_CH]
+    front_ref[:, 1024:A_COLS] = jnp.zeros((part, LANES), bf16)
+    front_ref[:, 1024 : 1024 + SSM_HEADS] = inner_ref[:, DS + CONV_CH :]
+    front_ref[:, A_COLS:] = inner_ref[:, DS : 2 * DS]
 
 
 def front_kernel(
@@ -474,7 +500,7 @@
 
 
 class PackedWeights:
-    def __init__(self, sources, held, sems, parts):
+    def __init__(self, source, core, held, sems, parts):
         self.held = held
         part, a_part, s_part, f_part = self.parts = parts
         self.so_at = 2 * part
@@ -487,7 +513,9 @@
             self.copies.append(
                 [
                     pltpu.make_async_copy(
-                        sources[i].at[:, :, rows], held.at[i, :, :, rows], sems.at[k, i]
+                        source.at[:, lax.rem(core + i, 2), :, rows],
+                        held.at[i, :, :, rows],
+                        sems.at[k, i],
                     )
                     for i in range(2)
                 ]
@@ -500,30 +528,28 @@
         for copy in self.copies[k]:
             copy.wait()
 
-    def block(self, i, y, start, size, cols):
-        got = self.held[i, y, :, start : start + size, cols]
-        return got.reshape(got.shape[0] * size, got.shape[2])
+    def block(self, i, y, start, size, col):
+        rows, cols = pl.ds(pl.multiple_of(start, 16), size), pl.ds(pl.multiple_of(col, 512), 512)
+        got = self.held[i, y, :, rows, cols]
+        return got.reshape(got.shape[0] * size, 512)
 
     def gate(self, i, y, j):
         part = self.parts[0]
-        return self.block(i, y, j // 2 * part, part, slice(j % 2 * 512, j % 2 * 512 + 512))
+        return self.block(i, y, j // 2 * part, part, j % 2 * 512)
 
     def ao(self, i, y, j):
         part, a_part = self.parts[:2]
-        return self.block(i, y, part + j * a_part, a_part, slice(512, 1024))
+        return self.block(i, y, part + j * a_part, a_part, 512)
 
     def so(self, i, y, j):
-        return self.block(i, y, self.so_at, self.parts[2], slice(j * 512, j * 512 + 512))
+        return self.block(i, y, self.so_at, self.parts[2], j * 512)
 
     def down(self, i, y, j):
-        return self.block(i, y, self.down_at, self.parts[3], slice(j * 512, j * 512 + 512))
+        return self.block(i, y, self.down_at, self.parts[3], j * 512)
 
     def gu(self, i, y, j):
         part = self.parts[0]
-        start = pl.multiple_of(self.gu_at + j // 2 * part, 16)
-        cols = pl.multiple_of(j % 2 * 512, 512)
-        got = self.held[i, y, :, pl.ds(start, part), pl.ds(cols, 512)]
-        return got.reshape(got.shape[0] * part, 512)
+        return self.block(i, y, self.gu_at + j // 2 * part, part, j % 2 * 512)
 
 
 class PlainWeights:
@@ -534,7 +560,7 @@
         pass
 
     def block(self, name, i, y, j):
-        return self.refs[2 * name + i][y, :, j * 512 : j * 512 + 512]
+        return self.refs[2 * name + i][y, :, pl.ds(pl.multiple_of(j * 512, 512), 512)]
 
     def gate(self, i, y, j):
         return self.block(0, i, y, j)
@@ -557,14 +583,13 @@
     entry_ref, skip_ref, normed_ref, gssm_ref, gffn_ref, *refs,
 ):
     if parts:
-        weights = PackedWeights(refs[:2], refs[-2], refs[-1], parts)
-        refs = refs[2:-2]
+        weights = PackedWeights(refs[0], core_ref[0], refs[-2], refs[-1], parts)
+        refs = refs[1:-2]
     else:
         weights, refs = PlainWeights(refs[:10]), refs[10:]
     pairs = [(i, y) for y in range(ys) for i in range(2)]
 
-    def through(ref, weight, j):
-        blocks = sides(ref, core, ys)
+    def through(blocks, weight, j):
         return sum(nn(blocks[y][i], weight(i, y, j)) for i, y in pairs)
 
     def back_through(ref, grad, weight, count):
@@ -578,7 +603,7 @@
 
     (
         out_ref, dmid_ref, datt_ref, dssd_ref, ycore_ref, dentry_ref, send_ref, keep_ref, dng_ref,
-        gi_ref, gd_ref, mid_ref, gu_ref, dn_ref, dmx_ref, fd_ref, n2_ref, hid_ref, mixed_ref, dh_ref,
+        gi_ref, gd_ref, mid_ref, gu_ref, dn_ref, dmx_ref, fd_ref, n2_ref, hid_ref, mixed_ref, dh_ref, fade_ref, ent_ref,
     ) = refs
     core = core_ref[0]
     rows, width = tok_ref.shape
@@ -588,59 +613,76 @@
     cot_at, dbr_at, dgate_at, sel_at = 2 * ff, 2 * ff + width, 2 * ff + 2 * width, 2 * ff + 2 * width + DS
     reads = bc_ref[:, STATE:].astype(bf16)
     spread = head_spread()
-    fade = nn_left(fade_of(cum_ref[...], off_ref[...]), spread, 2)
-    entered = nt(reads, entry_ref[...].astype(bf16))
-    square = 0.0
+    fade_ref[...] = nn_left(fade_of(cum_ref[...], off_ref[...]), spread, 2)
+    ent_ref[...] = nt(reads, entry_ref[...].astype(bf16))
+    none = jnp.zeros((rows, 1), f32)
+
+    def at(j, first=0):
+        return pl.ds(pl.multiple_of(first + j * 512, 512), 512)
+
     weights.wait(0)
-    for j in range(DS // 512):
-        cols = slice(j * 512, (j + 1) * 512)
-        gate = through(normed_ref, weights.gate, j).astype(bf16).astype(f32)
+    blocks = sides(normed_ref, core, ys)
+
+    def gates(j, square):
+        cols = at(j)
+        gate = through(blocks, weights.gate, j).astype(bf16).astype(f32)
         gi_ref[:, cols] = gate
-        ycore = yl_ref[:, cols] + fade[:, cols] * entered[:, cols]
+        ycore = yl_ref[:, cols] + fade_ref[:, cols] * ent_ref[:, cols]
         ycore_ref[:, cols] = ycore
         ssd = ycore + skip_ref[:, cols] * x_ref[:, cols]
         gated = ssd * gate * sigmoid(gate)
         gd_ref[:, cols] = gated
-        square = square + jnp.sum(gated * gated, axis=1, keepdims=True)
+        return square + jnp.sum(gated * gated, axis=1, keepdims=True)
+
+    square = lax.fori_loop(0, DS // 512, gates, none, unroll=True)
     rms_gate = lax.rsqrt(square / DS + EPS)
     mixed_ref[...] = (gd_ref[...] * rms_gate * gssm_ref[...]).astype(bf16)
-    square = 0.0
     weights.wait(1)
-    for j in range(width // 512):
-        cols = slice(j * 512, (j + 1) * 512)
-        branch = through(att_ref, weights.ao, j) + through(mixed_ref, weights.so, j)
-        middle = tok_ref[:, cols].astype(f32) + branch
-        mid_ref[:, cols] = middle
-        square = square + jnp.sum(middle * middle, axis=1, keepdims=True)
+    att_blocks, mix_blocks = sides(att_ref, core, ys), sides(mixed_ref, core, ys)
+
+    def branches(j, square):
+        branch = through(att_blocks, weights.ao, j) + through(mix_blocks, weights.so, j)
+        middle = tok_ref[:, at(j)].astype(f32) + branch
+        mid_ref[:, at(j)] = middle
+        return square + jnp.sum(middle * middle, axis=1, keepdims=True)
+
+    square = lax.fori_loop(0, width // 512, branches, none, unroll=True)
     rms = lax.rsqrt(square / width + EPS)
     n2_ref[...] = (mid_ref[...] * rms * gffn_ref[...]).astype(bf16)
     weights.wait(2)
-    blocks = sides(n2_ref, core, ys)
+    ups = sides(n2_ref, core, ys)
 
     def up(j, unused):
-        cols = pl.ds(pl.multiple_of(j * 512, 512), 512)
-        gu_ref[:, cols] = sum(nn(blocks[y][i], weights.gu(i, y, j)) for i, y in pairs)
+        gu_ref[:, at(j)] = through(ups, weights.gu, j)
         return unused
 
     lax.fori_loop(0, 2 * ff // 512, up, 0)
-    for j in range(ff // 512):
-        gate = gu_ref[:, j * 512 : (j + 1) * 512]
-        lift = gu_ref[:, ff + j * 512 : ff + (j + 1) * 512]
-        hid_ref[:, j * 512 : (j + 1) * 512] = (gate * sigmoid(gate) * lift).astype(bf16)
-    for j in range(width // 512):
-        cols = slice(j * 512, (j + 1) * 512)
-        out_ref[:, cols] = (mid_ref[:, cols] + through(hid_ref, weights.down, j)).astype(bf16)
+
+    def hide(j, unused):
+        gate = gu_ref[:, at(j)]
+        hid_ref[:, at(j)] = (gate * sigmoid(gate) * gu_ref[:, at(j, ff)]).astype(bf16)
+        return unused
+
+    lax.fori_loop(0, ff // 512, hide, 0)
+    hids = sides(hid_ref, core, ys)
+
+    def finals(j, unused):
+        out_ref[:, at(j)] = (mid_ref[:, at(j)] + through(hids, weights.down, j)).astype(bf16)
+        return unused
+
+    lax.fori_loop(0, width // 512, finals, 0, unroll=True)
     cot = cot_ref[...]
     back_through(dh_ref, cot, weights.down, 2)
-    for j in range(ff // 512):
-        cols = slice(j * 512, (j + 1) * 512)
-        gate = gu_ref[:, cols]
-        lift = gu_ref[:, ff + j * 512 : ff + (j + 1) * 512]
+
+    def unhide(j, unused):
+        gate, lift, dhid = gu_ref[:, at(j)], gu_ref[:, at(j, ff)], dh_ref[:, at(j)]
         sg = sigmoid(gate)
-        dhid = dh_ref[:, cols]
         dgate = dhid * lift * (sg * (1.0 + gate * (1.0 - sg)))
-        send_ref[:, cols] = dgate.astype(bf16)
-        send_ref[:, ff + j * 512 : ff + (j + 1) * 512] = (dhid * gate * sg).astype(bf16)
+        send_ref[:, at(j)] = dgate.astype(bf16)
+        send_ref[:, at(j, ff)] = (dhid * gate * sg).astype(bf16)
+        return unused
+
+    lax.fori_loop(0, ff // 512, unhide, 0)
     send_ref[:, cot_at:dbr_at] = cot
     wide = width // ys // 2
 
@@ -661,15 +703,15 @@
     send_ref[:, dbr_at:dgate_at] = dbr
     back_through(datt_ref, dbr, weights.ao, 2)
     back_through(dmx_ref, dbr, weights.so, 2)
-    mean = 0.0
-    for j in range(DS // 512):
-        cols = slice(j * 512, (j + 1) * 512)
-        unit = gd_ref[:, cols] * rms_gate
-        dmx = dmx_ref[:, cols]
-        mean = mean + jnp.sum(dmx * gssm_ref[:, cols] * unit, axis=1, keepdims=True)
-    mean = mean / DS
-    for j in range(DS // 512):
-        cols = slice(j * 512, (j + 1) * 512)
+
+    def means(j, mean):
+        unit = gd_ref[:, at(j)] * rms_gate
+        return mean + jnp.sum(dmx_ref[:, at(j)] * gssm_ref[:, at(j)] * unit, axis=1, keepdims=True)
+
+    mean = lax.fori_loop(0, DS // 512, means, none) / DS
+
+    def ungate(j, unused):
+        cols = at(j)
         unit = gd_ref[:, cols] * rms_gate
         dgated = rms_gate * (dmx_ref[:, cols] * gssm_ref[:, cols] - unit * mean)
         gate = gi_ref[:, cols]
@@ -678,19 +720,22 @@
         dssd = dgated * gate * sg
         dssd_ref[:, cols] = dssd
         dgate = (dgated * ssd * (sg * (1.0 + gate * (1.0 - sg)))).astype(bf16)
-        send_ref[:, dgate_at + j * 512 : dgate_at + (j + 1) * 512] = dgate
-        fd_ref[:, cols] = (dssd * fade[:, cols]).astype(bf16)
+        send_ref[:, at(j, dgate_at)] = dgate
+        fd_ref[:, cols] = (dssd * fade_ref[:, cols]).astype(bf16)
+        return unused
+
+    lax.fori_loop(0, DS // 512, ungate, 0)
     back_through(dng_ref, send_ref[:, dgate_at:sel_at], weights.gate, 3)
     dentry_ref[...] = tn(fd_ref[...], reads)
-    at = 0
+    to = 0
     for ref in (n2_ref, hid_ref, att_ref, mixed_ref, normed_ref):
         count = ys
         wide = ref.shape[1] // count
         for y in range(count):
             own, oth = halves(ref[:, y * wide : (y + 1) * wide], core)
-            keep_ref[:, at : at + wide // 2] = own
-            send_ref[:, sel_at + at : sel_at + at + wide // 2] = oth
-            at += wide // 2
+            keep_ref[:, to : to + wide // 2] = own
+            send_ref[:, sel_at + to : sel_at + to + wide // 2] = oth
+            to += wide // 2
 
 
 def products_kernel(plan, extra, keep_ref, own_ref, act_ref, *refs):
@@ -723,24 +768,29 @@
             left = keep_ref[:, pl.ds(pl.multiple_of(a_at + y * size, LANES), size)]
             right = act_ref[:, pl.ds(pl.multiple_of(act_at + y * size, LANES), size)]
             keep, send = (xkeep_ref, xsend_ref) if kind == "x" else (ykeep_ref, ysend_ref)
-            for j in range(0, wide, 512):
-                stop = min(j + 512, wide)
-                total = tn(left, own_ref[:, g_at + j : g_at + stop])
-                total = total + tn(right, got_ref[:, g_at + j : g_at + stop])
+            block = 512 if wide % 512 == 0 else 384
+
+            def columns(j, unused):
+                at = pl.ds(pl.multiple_of(g_at + j * block, LANES), block)
+                total = tn(left, own_ref[:, at]) + tn(right, got_ref[:, at])
                 if kind == "x":
                     zs, each = keep.shape[1], keep.shape[2]
-                    if extra and stop == wide:
-                        total = total + extra_ref[k]
-                    cols = slice(place + j, place + stop)
-                    total = total.reshape(zs, 2, each, stop - j)
+                    if extra:
+                        total = total + extra_ref[k] * (j == wide // block - 1).astype(f32)
+                    cols = pl.ds(pl.multiple_of(place + j * block, LANES), block)
+                    total = total.reshape(zs, 2, each, block)
                     low, high = total[:, 0], total[:, 1]
                     keep[k, :, :, cols] = jnp.where(my_x == 0, low, high).astype(bf16)
                     send[k, :, :, cols] = jnp.where(my_x == 0, high, low).astype(bf16)
                 else:
                     count = keep.shape[0]
                     each = size // count
-                    total = total.reshape(count, each, stop - j).astype(bf16)
-                    (send if k else keep)[:, place : place + each, j:stop] = total
+                    cols = pl.ds(pl.multiple_of(j * block, LANES), block)
+                    total = total.reshape(count, each, block).astype(bf16)
+                    (send if k else keep)[:, place : place + each, cols] = total
+                return unused
+
+            lax.fori_loop(0, wide // block, columns, 0, unroll=True)
 
 
 def fold_one_kernel(
@@ -785,6 +835,67 @@
         for z in range(1, got_ref.shape[0]):
             total = total + got_ref[z, rows, :].astype(f32)
         out[:, col : col + width] = total
+
+
+def row_sums(value):
+    ones = jnp.ones((8, value.shape[1]), bf16)
+    return sum(nt(ones, part) for part in terms(value, 3))[:1]
+
+
+def summed(got_ref, rows):
+    total = got_ref[0, rows, :].astype(f32)
+    for z in range(1, got_ref.shape[0]):
+        total = total + got_ref[z, rows, :].astype(f32)
+    return total
+
+
+def finish_post_kernel(
+    got_ref, one_ref, guw_ref, sow_ref, gffn_ref, gssm_ref,
+    gu_ref, gate_ref, ao_ref, so_ref, dffn_ref, dssm_ref,
+):
+    part, ups = one_ref.shape
+    wide = got_ref.shape[2]
+    gu_ref[:, :ups] = one_ref[...]
+    at = 0
+    for out, start in ((gu_ref, ups), (gate_ref, 0)):
+        for col in range(start, out.shape[1], wide):
+            out[:, col : col + wide] = summed(got_ref, slice(at, at + part))
+            at += part
+    for col in range(0, ao_ref.shape[1], wide):
+        for out in (ao_ref, so_ref):
+            out[:, col : col + wide] = summed(got_ref, slice(at, at + out.shape[0]))
+            at += out.shape[0]
+    dffn_ref[...] = row_sums(guw_ref[...].astype(f32) * gu_ref[...]) / gffn_ref[...]
+    dssm_ref[...] = row_sums(sow_ref[...].astype(f32) * so_ref[...]) / gssm_ref[...]
+
+
+def finish_front_kernel(
+    got_ref, gate_ref, kvw_ref, qw_ref, iw_ref, gain_ref,
+    kv_ref, q_ref, inner_ref, conv_ref, bias_ref, log_ref, step_ref, skip_ref, dgain_ref,
+):
+    part, wide = kv_ref.shape[0], got_ref.shape[2]
+    count = A_COLS // wide
+    blocks = [summed(got_ref, slice(k * part, (k + 1) * part)) for k in range(count)]
+    first = jnp.concatenate(blocks, axis=1)
+    kv_ref[...] = first[:, :256]
+    q_ref[...] = first[:, 256:768]
+    inner_ref[:, :DS] = gate_ref[...]
+    for k in range(DS // wide):
+        rows = slice((count + k) * part, (count + k + 1) * part)
+        inner_ref[:, DS + k * wide : DS + (k + 1) * wide] = summed(got_ref, rows)
+    last = first[:, 1024:]
+    inner_ref[:, 2 * DS : 2 * DS + 2 * STATE] = first[:, 768:1024]
+    inner_ref[:, DS + CONV_CH :] = last[:, :SSM_HEADS]
+    turned_last = last.T
+    own = bias_ref.shape[1]
+    conv_ref[...] = turned_last[SSM_HEADS : SSM_HEADS + own, :CONV]
+    bias_ref[...] = last[CONV : CONV + 1, SSM_HEADS : SSM_HEADS + own]
+    for k, out in enumerate((log_ref, step_ref, skip_ref)):
+        out[...] = last[CONV + 1 + k : CONV + 2 + k, SSM_HEADS : 2 * SSM_HEADS]
+    total = row_sums(kvw_ref[...].astype(f32) * kv_ref[...])
+    total = total + row_sums(qw_ref[...].astype(f32) * q_ref[...])
+    total = total + row_sums(iw_ref[...].astype(f32) * inner_ref[...])
+    dgain_ref[...] = total / gain_ref[...]
 
 
 class PairReduction:
@@ -1010,7 +1121,7 @@
         out[...] = total / gains[k][...].astype(f32)
 
 
-def run(kernel, name, outs, args, scalars=0, scratch=(), flops=0, left=0, sems=()):
+def run(kernel, name, outs, args, scalars=0, scratch=(), us=3, left=0, sems=()):
     moved = sum(a.size * a.dtype.itemsize for a in args)
     shapes = [jax.ShapeDtypeStruct(shape, kind) for shape, kind in outs]
     moved += sum(s.size * s.dtype.itemsize for s in shapes)
@@ -1027,7 +1138,7 @@
         + [pltpu.SemaphoreType.DMA(shape) for shape in sems],
         compiler_params=pltpu.CompilerParams(vmem_limit_bytes=62 * 2**20),
         cost_estimate=pl.CostEstimate(
-            flops=flops, bytes_accessed=moved, transcendentals=0
+            flops=us * SCALE, bytes_accessed=moved, transcendentals=0
         ),
     )(*args)
 
@@ -1057,40 +1168,45 @@
     counts = [mixer_gain.size, conv_weight.size, conv_bias.size, ssm_gain.size, ffn_gain.size]
     slots = -(-small.size // LANES) * LANES
     small = gather_small(jnp.pad(small, (0, slots - small.size)))
-    inner_tail = inner_weight[:, DS + CONV_CH :]
-    front_a = jnp.concatenate(
-        [
-            keyval_weight,
-            query_weight,
-            inner_weight[:, 2 * DS : DS + CONV_CH],
-            jnp.pad(inner_tail, ((0, 0), (0, LANES - SSM_HEADS))),
-        ],
-        1,
-    )
-    front = shared(jnp.concatenate([front_a, inner_weight[:, DS : 2 * DS]], 1), "z")
-    wa_own, wa_oth = gather_pair(front[:, :, :A_COLS], "y")
-    wb_own, wb_oth = gather_pair(front[:, :, A_COLS:], "x")
     others = lax.axis_size(SEQ)
     aligned = ys == 2 and others == 8 and all(r % 16 == 0 for r in (part, a_rows, s_rows, f_rows))
     core_unit = extents()["core"][0]
-    packed = jnp.concatenate(
-        [
-            inner_weight[:, :width],
-            jnp.concatenate(
-                [
-                    inner_weight[:, width:DS],
-                    jnp.concatenate([attn_out_weight[:, :512], attn_out_weight[:, 512:]], 0),
-                ],
-                1,
+    pack_rows = 6 * part + s_rows + f_rows
+    if aligned:
+        packed, front = run(
+            pack_kernel,
+            "pack",
+            [((pack_rows, width), bf16), ((part, A_COLS + DS), bf16)],
+            (
+                gate_up_weight, inner_weight, attn_out_weight, ssm_out_weight, down_weight,
+                keyval_weight, query_weight,
             ),
-            ssm_out_weight,
-        ]
-        + [gate_up_weight[:, k * width : (k + 1) * width] for k in range(2 * ff // width)]
-        + [down_weight],
-        0,
-    )
-    packed = lax.all_gather(packed, ("y", "z", "x"), axis=0)
-    packed = packed.reshape(ys, others, *packed.shape[1:])
+        )
+    else:
+        tail = jnp.pad(inner_weight[:, DS + CONV_CH :], ((0, 0), (0, LANES - SSM_HEADS)))
+        front = jnp.concatenate(
+            [
+                keyval_weight, query_weight, inner_weight[:, 2 * DS : DS + CONV_CH], tail,
+                inner_weight[:, DS : 2 * DS],
+            ],
+            1,
+        )
+        ao = jnp.concatenate([attn_out_weight[:, :512], attn_out_weight[:, 512:]], 0)
+        packed = jnp.concatenate(
+            [
+                inner_weight[:, :width],
+                jnp.concatenate([inner_weight[:, width:DS], ao], 1),
+                ssm_out_weight,
+            ]
+            + [gate_up_weight[:, k * width : (k + 1) * width] for k in range(2 * ff // width)]
+            + [down_weight],
+            0,
+        )
+    front = shared(front, "z")
+    wa_own, wa_oth = gather_pair(front[:, :, :A_COLS], "y")
+    wb_own, wb_oth = gather_pair(front[:, :, A_COLS:], "x")
+    packed = lax.all_gather(packed, AXES, axis=0)
+    packed = packed.reshape(ys, 2, others, *packed.shape[1:])
     starts = [sum(counts[:i]) for i in range(len(counts))]
     gain_one, w_conv, b_conv, gain_ssm, gain_two = (
         small[:, s : s + c].reshape(-1) for s, c in zip(starts, counts)
@@ -1141,33 +1257,51 @@
         ),
         scalars=1,
         scratch=[((rows + RIM, width), bf16), ((rows, DS), bf16)],
-        flops=2 * rows * width * (A_COLS + DS),
+        us=8,
     )
     carrying = Carrying(state, carry, back, 1)
     sent_state = carrying.send()
     rank = seq_rank.reshape(1).astype(jnp.int32)
-    kv_all = shared(kv, SEQ)
+    kv_slots = jnp.broadcast_to(kv[None], (seq_count, *kv.shape))
+    kv_all = dealt(kv_slots, SEQ)
     window = (back + 1) * rows
     y_local = run(
         scan_kernel, "scan", [((rows, DS), f32)],
-        after((x, bc, step, cum, cumt, off), sent_state),
-        scratch=[((rows, DS), bf16), ((rows, DS), f32)], flops=2 * SSM_HEADS * rows * rows * 128,
+        after((x, bc, step, cum, cumt, off), sent_state, kv_slots),
+        scratch=[((rows, DS), bf16), ((rows, DS), f32)], us=8,
     )[0]
-    order = y_local
-    entry = None
+    entry = carrying.receive(y_local)
+    if entry is None:
+        sent_state = carrying.send()
+    attended, lse = run(
+        functools.partial(attend_kernel, back + 1),
+        "attend",
+        [((rows, heads_width), bf16), ((LANES, rows), f32)],
+        after((rank, q8, kv_all, off), sent_state),
+        scalars=1,
+        scratch=[
+            ((window, LANES), bf16),
+            ((window, LANES), bf16),
+            ((rows, window), f32),
+            ((HEADS, rows, LANES), f32),
+        ],
+        us=10,
+    )
     while entry is None:
-        entry = carrying.receive(order)
+        entry = carrying.receive(attended)
         if entry is None:
-            sent_state = carrying.send()
-    packed = after(packed, order, sent_state)
-    packed = (packed, swap(packed, core_unit))
+            carrying.send()
+    packed = after(packed, entry)
     post_scratch, post_sems = [], []
     if aligned:
-        parts, post_weights = (part, a_rows, s_rows, f_rows), packed
-        post_scratch, post_sems = [((2, *packed[0].shape), bf16)], [(3, 2)]
+        parts, post_weights = (part, a_rows, s_rows, f_rows), (packed,)
+        post_scratch, post_sems = [((2, ys, others, *packed.shape[3:]), bf16)], [(3, 2)]
     else:
         parts = ()
         gu_at = 2 * part + s_rows
+        packed = [
+            lax.dynamic_index_in_dim(packed, place_on("core") ^ i, 1, False) for i in range(2)
+        ]
 
         def taken(full, start, size, low, high):
             return full[:, :, start : start + size, low:high].reshape(ys, -1, high - low)
@@ -1183,20 +1317,6 @@
             *joined_columns([(gu_at + k * part, part, 0, width) for k in range(2 * ff // width)]),
         )
 
-    attended, lse = run(
-        functools.partial(attend_kernel, back + 1),
-        "attend",
-        [((rows, heads_width), bf16), ((LANES, rows), f32)],
-        after((rank, q8, kv_all, off), packed[0]),
-        scalars=1,
-        scratch=[
-            ((window, LANES), bf16),
-            ((window, LANES), bf16),
-            ((rows, window), f32),
-            ((HEADS, rows, LANES), f32),
-        ],
-        flops=4 * HEADS * rows * window * LANES,
-    )
     half = (2 * width + ff + heads_width + DS) // 2
     sent = 2 * ff + 2 * width + DS
     output, dmid, datt, dssd, ycore, dentry, send, keep, dng = run(
@@ -1218,7 +1338,7 @@
             gain_ssm, gain_two, *post_weights,
         ),
         scalars=1,
-        left=2 if aligned else 0,
+        left=1 if aligned else 0,
         sems=post_sems,
         scratch=[
             ((rows, DS), f32),
@@ -1232,9 +1352,11 @@
             ((rows, ff), bf16),
             ((rows, DS), bf16),
             ((rows, ff), f32),
+            ((rows, DS), f32),
+            ((rows, DS), f32),
         ]
         + post_scratch,
-        flops=4 * rows * width * (3 * ff + DS + DS + heads_width),
+        us=30,
     )
     got = swap(send, core_unit)
     carrying = Carrying(dentry, carry, back, -1)
@@ -1248,7 +1370,6 @@
     places = tuple(place_on(g).reshape(1).astype(jnp.int32) for g in ("y", "x"))
 
     def weight_sums(name, x_parts, y_parts, keep, own, got, extra=()):
-        flops = sum(4 * rows * p[2] * p[4] * ys for p in x_parts + y_parts)
         plan, at, tall = [], 0, y_parts[0][4]
         for p in x_parts:
             plan.append(("x", at, *p))
@@ -1265,7 +1386,7 @@
                 [(xs, bf16), (xs, bf16), ((others, at, tall), bf16), ((others, at, tall), bf16)],
                 (*places, keep, own, got, *extra),
                 scalars=2,
-                flops=flops,
+                us=9,
             )
             return PairReduction(made, 512 if wide % 512 == 0 else 384)
         parts = x_parts + y_parts
@@ -1276,34 +1397,31 @@
             name,
             [((ys, p[2], p[4]), bf16) for p in parts],
             (keep, own, got, *extra),
-            flops=flops,
+            us=9,
         )
         heads = made[: len(x_parts)]
         tails = [m.reshape(ys, others, -1, tall) for m in made[len(x_parts) :]]
         rows_of = (x_parts[0][2] // others, at)
         return PlainReduction((jnp.concatenate(heads, 2), jnp.concatenate(tails, 2)), rows_of)
 
-    dq, dkv = run(
-        functools.partial(attend_back_kernel, back + 1),
-        "attend_back",
-        [((rows, heads_width), bf16), ((seq_count, rows, 256), bf16)],
-        after((rank, q8, kv_all, off_row, lse, datt, cos, sin), sent_state),
-        scalars=1,
+    dxw, dscores = run(
+        scan_back_kernel,
+        "scan_back",
+        [((rows, DS), f32), ((rows, rows), bf16)],
+        after((dssd, x, bc, step, cum, cumt, off_row), sent_state),
         scratch=[
-            ((window, LANES), bf16),
-            ((window, LANES), bf16),
-            ((window, rows), f32),
-            ((HEADS, rows, LANES), bf16),
-            ((HEADS, rows, LANES), f32),
-            ((window, 256), f32),
+            ((rows, DS), bf16),
+            ((rows, DS), f32),
+            ((rows, DS), bf16),
+            ((rows, rows), f32),
         ],
-        flops=10 * HEADS * rows * window * LANES,
+        us=9,
     )
-    dkv_got = dealt(dkv, SEQ)
-    downstream = carrying.receive(dq)
+
+    downstream = carrying.receive(dxw)
     if downstream is None:
         sent_state = carrying.send()
-    keep, send, got = after((keep, send, got), dq, sent_state)
+    keep, send, got = after((keep, send, got), dxw, sent_state)
     red_one = weight_sums(
         "weights_one",
         [(n2_at, sent + n2_at, sizes[0], 0, ff)],
@@ -1312,11 +1430,7 @@
         send,
         got,
     )
-    while downstream is None:
-        downstream = carrying.receive(red_one.sent)
-        if downstream is None:
-            carrying.send()
-    keep, send, got = after((keep, send, got), red_one.sent, downstream)
+    keep, send, got = after((keep, send, got), red_one.sent)
     red_two = weight_sums(
         "weights_two",
         [
@@ -1331,21 +1445,28 @@
         send,
         got,
     )
-    dxw, dscores = run(
-        scan_back_kernel,
-        "scan_back",
-        [((rows, DS), f32), ((rows, rows), bf16)],
-        after((dssd, x, bc, step, cum, cumt, off_row), red_two.sent),
+    dq, dkv = run(
+        functools.partial(attend_back_kernel, back + 1),
+        "attend_back",
+        [((rows, heads_width), bf16), ((seq_count, rows, 256), bf16)],
+        after((rank, q8, kv_all, off_row, lse, datt, cos, sin), red_two.sent),
+        scalars=1,
         scratch=[
-            ((rows, DS), bf16),
-            ((rows, DS), f32),
-            ((rows, DS), bf16),
-            ((rows, rows), f32),
+            ((window, LANES), bf16),
+            ((window, LANES), bf16),
+            ((window, rows), f32),
+            ((HEADS, rows, LANES), bf16),
+            ((HEADS, rows, LANES), f32),
+            ((window, 256), f32),
         ],
-        flops=4 * SSM_HEADS * rows * rows * 128,
+        us=14,
     )
-
-    red_one.fold_one(dxw)
+    dkv_got = dealt(dkv, SEQ)
+    while downstream is None:
+        downstream = carrying.receive(dq)
+        if downstream is None:
+            carrying.send()
+    red_one.fold_one(dq, downstream)
     dext, dz, small = run(
         mixer_back_kernel,
         "mixer_back",
@@ -1362,7 +1483,7 @@
             red_one.sent,
         ),
         scratch=[((rows, CONV_CH), f32)],
-        flops=8 * rows * DS * 128,
+        us=13,
     )
     count = lax.axis_size(AXES)
     small_got = swap(small, core_unit)
@@ -1376,25 +1497,32 @@
     gab_got = swap(gab, core_unit)
     red_two.fold_one(gab)
     small = small + after(small_got, gab)
-    per_device = jnp.concatenate(
-        [
-            small[: CONV + 1].reshape(CONV + 1, count, -1).transpose(1, 0, 2).reshape(count, -1),
-            jnp.broadcast_to(
-                small[CONV + 1, : 3 * LANES].reshape(3, LANES)[:, :SSM_HEADS].reshape(1, -1),
-                (count, 3 * SSM_HEADS),
-            ),
-        ],
-        1,
+    free = LANES - SSM_HEADS
+    convs = small[: CONV + 1].reshape(CONV + 1, count, -1).transpose(1, 0, 2)
+    head_sums = small[CONV + 1, : 3 * LANES].reshape(3, LANES)[:, :SSM_HEADS]
+    if aligned:
+        head_sums = jnp.broadcast_to(head_sums[None], (count, 3, SSM_HEADS))
+        per_device = jnp.concatenate(
+            [
+                jnp.pad(convs, ((0, 0), (0, 0), (0, free - convs.shape[2]))),
+                jnp.pad(head_sums, ((0, 0), (0, 0), (0, free - SSM_HEADS))),
+            ],
+            1,
+        )
+        slots = CONV + 4
+    else:
+        head_sums = jnp.broadcast_to(head_sums.reshape(1, -1), (count, 3 * SSM_HEADS))
+        per_device = jnp.concatenate([convs.reshape(count, -1), head_sums], 1)
+        slots = per_device.shape[1]
+        per_device = jnp.pad(per_device, ((0, 0), (0, part * free - slots)))
+        per_device = per_device.reshape(count, part, free)
+    per_device = lax.dynamic_index_in_dim(
+        per_device.reshape(ys, 2, others, -1, free), place_on("core"), 1, False
     )
-    slots = per_device.shape[1]
-    free = LANES - SSM_HEADS
-    per_device = lax.dynamic_index_in_dim(
-        per_device.reshape(ys, 2, others, slots), place_on("core"), 1, False
-    )
-    extra = jnp.pad(per_device, ((0, 0), (0, 0), (0, part * free - slots)))
-    extra = extra.reshape(ys, others * part, free)
-    aside = 512 if A_COLS % 512 == 0 else A_COLS % 512
-    extra = jnp.pad(extra, ((0, 0), (0, 0), (aside - free, 0)))
+    aside = 384 if aligned else A_COLS % 512
+    extra = jnp.pad(
+        per_device, ((0, 0), (0, 0), (0, part - per_device.shape[2]), (aside - free, 0))
+    ).reshape(ys, others * part, aside)
     grad_tokens, grad_rim = run(
         back_kernel,
         "back",
@@ -1405,10 +1533,10 @@
         ),
         scalars=1,
         scratch=[((rows + RIM, width), f32)],
-        flops=2 * rows * width * (A_COLS + DS),
+        us=7,
     )
-    rim_got = shifted(grad_rim, -1)
-    norm_keep, gab, gab_got, extra = after((norm_keep, gab, gab_got, extra), grad_tokens)
+    red_one.fold_two(grad_tokens)
+    norm_keep, gab, gab_got, extra = after((norm_keep, gab, gab_got, extra), red_one.sent)
     red_three = weight_sums(
         "front_weights",
         [(0, A_COLS + DS, sizes[4], 0, A_COLS)],
@@ -1418,45 +1546,88 @@
         gab_got,
         (extra,),
     )
-    red_one.fold_two(red_three.sent)
-    red_two.fold_two(red_one.sent)
-    red_three.fold_one(red_two.sent)
-    r_one, r_down = red_one.fold_three(red_three.sent)
-    red_three.fold_two(r_one)
-    r_two, r_out = red_two.fold_three(red_three.sent)
-    rim_got = after(rim_got, r_two)
-    grad_tokens = grad_tokens.at[rows - RIM :].add(rim_got)
-    r_e, r_f = red_three.fold_three(grad_tokens)
-    r_gu = jnp.concatenate([r_one, r_two[:, :ff]], 1)
-    small = r_e[:, A_COLS - free :].reshape(-1)[:slots]
-    conv = small[: (CONV + 1) * conv_bias.size].reshape(CONV + 1, -1)
-    heads = small[(CONV + 1) * conv_bias.size :].reshape(3, SSM_HEADS)
-    g_inner = jnp.concatenate([r_two[:, ff:], r_f, r_e[:, 768 : 1024 + SSM_HEADS]], 1)
-    g_mixer, g_ssm, g_ffn = run(
-        functools.partial(
-            gain_kernel, [(0, 0, 1), (0, 2, 3), (0, 4, 5), (1, 6, 7), (2, 8, 9)], 3
-        ),
-        "gains",
-        [((part, 1), f32), ((s_rows, 1), f32), ((part, 1), f32)],
-        (
-            mixer_gain[:, None], ssm_gain[:, None], ffn_gain[:, None],
-            keyval_weight, r_e[:, :256], query_weight, r_e[:, 256:768], inner_weight, g_inner,
-            ssm_out_weight, r_out[a_rows:], gate_up_weight, r_gu,
-        ),
-    )
+    red_two.fold_two(red_three.sent)
+    r_one, r_down = red_one.fold_three(red_two.sent)
+    red_three.fold_one(r_one)
+    rim_got = shifted(after(grad_rim, red_three.sent), -1)
+    red_three.fold_two(red_three.sent)
+    if aligned:
+        r_gu, r_gate, r_ao, r_so, g_ffn, g_ssm = run(
+            finish_post_kernel,
+            "finish_post",
+            [
+                ((part, 2 * ff), f32),
+                ((part, DS), f32),
+                ((a_rows, width), f32),
+                ((s_rows, width), f32),
+                ((1, part), f32),
+                ((1, s_rows), f32),
+            ],
+            (
+                after(red_two.gots, red_three.sent), r_one, gate_up_weight, ssm_out_weight,
+                ffn_gain.astype(f32)[None, :], ssm_gain.astype(f32)[None, :],
+            ),
+        )
+        rim_got = after(rim_got, r_gu)
+        grad_tokens = grad_tokens.at[rows - RIM :].add(rim_got)
+        r_kv, r_q, g_inner, g_conv, g_bias, g_log, g_step, g_skip, g_mixer = run(
+            finish_front_kernel,
+            "finish_front",
+            [
+                ((part, 256), f32),
+                ((part, heads_width), f32),
+                ((part, inner_weight.shape[1]), f32),
+                (conv_weight.shape, f32),
+                ((1, conv_bias.size), f32),
+                ((1, SSM_HEADS), f32),
+                ((1, SSM_HEADS), f32),
+                ((1, SSM_HEADS), f32),
+                ((1, part), f32),
+            ],
+            (
+                after(red_three.gots, grad_tokens), r_gate, keyval_weight, query_weight,
+                inner_weight, mixer_gain.astype(f32)[None, :],
+            ),
+        )
+        g_bias, g_mixer, g_ssm, g_ffn = (v[0] for v in (g_bias, g_mixer, g_ssm, g_ffn))
+        heads = [v[0] for v in (g_log, g_step, g_skip)]
+    else:
+        r_two, r_out = red_two.fold_three(red_three.sent)
+        rim_got = after(rim_got, r_two)
+        grad_tokens = grad_tokens.at[rows - RIM :].add(rim_got)
+        r_e, r_f = red_three.fold_three(grad_tokens)
+        r_gu = jnp.concatenate([r_one, r_two[:, :ff]], 1)
+        small = r_e[:, A_COLS - free :].reshape(-1)[:slots]
+        conv = small[: (CONV + 1) * conv_bias.size].reshape(CONV + 1, -1)
+        g_conv, g_bias = conv[:CONV].T, conv[CONV]
+        heads = small[(CONV + 1) * conv_bias.size :].reshape(3, SSM_HEADS)
+        g_inner = jnp.concatenate([r_two[:, ff:], r_f, r_e[:, 768 : 1024 + SSM_HEADS]], 1)
+        r_kv, r_q, r_ao, r_so = r_e[:, :256], r_e[:, 256:768], r_out[:a_rows], r_out[a_rows:]
+        pairs = [(0, 0, 1), (0, 2, 3), (0, 4, 5), (1, 6, 7), (2, 8, 9)]
+        gains = run(
+            functools.partial(gain_kernel, pairs, 3),
+            "gains",
+            [((part, 1), f32), ((s_rows, 1), f32), ((part, 1), f32)],
+            (
+                mixer_gain[:, None], ssm_gain[:, None], ffn_gain[:, None],
+                keyval_weight, r_kv, query_weight, r_q, inner_weight, g_inner,
+                ssm_out_weight, r_so, gate_up_weight, r_gu,
+            ),
+        )
+        g_mixer, g_ssm, g_ffn = (v[:, 0] for v in gains)
     return (
         output,
         grad_tokens,
-        g_mixer[:, 0],
-        r_e[:, 256:768],
-        r_e[:, :256],
+        g_mixer,
+        r_q,
+        r_kv,
         g_inner,
-        conv[:CONV].T,
-        conv[CONV],
-        g_ssm[:, 0],
-        r_out[:a_rows],
-        r_out[a_rows:],
-        g_ffn[:, 0],
+        g_conv,
+        g_bias,
+        g_ssm,
+        r_ao,
+        r_so,
+        g_ffn,
         r_gu,
         r_down,
         heads[0],

time: 541 us -> 489 us (0.904)
  waiting for transfers between devices: 185 us -> 152 us
  local copies, waits for them, and re-layouts: 53.2 us -> 26 us
  starting transfers between devices: 93.6 us -> 107 us
  other arithmetic: 24.9 us -> 18.7 us
    all_to_all x6, waiting for transfers between devices: 24.3 us -> 89.6 us  [dealt(): return lax.all_to_all(array, axes, 0, 0, tiled=True)]
    ppermute x28 -> x27, waiting for transfers between devices: 92.7 us -> 41.5 us  [swap(): return lax.ppermute(array, AXES, [(i, i ^ mask) for i in range(count)])]
    all_gather x1, waiting for transfers between devices: 26.1 us -> 0.01 us  [local(): packed = lax.all_gather(packed, AXES, axis=0)]
    ppermute x8, waiting for transfers between devices: 42.1 us -> 20.9 us  [shifted(): return lax.ppermute(array, SEQ, pairs)]
    slice x17 -> x1, local copies, waits for them, and re-layouts: 12.8 us -> 0.02 us  [local(): head_sums = small[CONV + 1, :3 * LANES].reshape(3, LANES)[:, :SSM_HEADS]]
    unnamed x84 -> x74, local copies, waits for them, and re-layouts: 14.7 us -> 4.64 us
    ppermute x8, starting transfers between devices: 17.9 us -> 27.9 us  [shifted(): return lax.ppermute(array, SEQ, pairs)]
    ppermute x28 -> x27, starting transfers between devices: 28.6 us -> 32.3 us  [swap(): return lax.ppermute(array, AXES, [(i, i ^ mask) for i in range(count)])]
  transfers between devices with their start and end apart: 43 -> 42, of which waited for: 20 -> 17; matrix products, arithmetic and copies ran while one was open for 9% -> 8% of each run, Pallas kernels for 22% -> 26%
where the time goes in v3:
time: 489 us; the launch traced here: 480 us
  Pallas kernels  159 us (33%)
  waiting for transfers between devices  152 us (31%)
  starting transfers between devices  107 us (22%)
  local copies, waits for them, and re-layouts  26 us (5%)
  other arithmetic  18.7 us (4%)
  between operations  18 us (4%)
    pallas_call x22, Pallas kernels, run(): pl.pallas_call(kernel, name=name, out_shape=shapes, in_specs=specs, out_s...  159 us
    all_to_all x6, waiting for transfers between devices, dealt(): return lax.all_to_all(array, axes, 0, 0, tiled=True)  89.6 us
    all_to_all x6, starting transfers between devices, dealt(): return lax.all_to_all(array, axes, 0, 0, tiled=True)  46.7 us
    ppermute x27, waiting for transfers between devices, swap(): return lax.ppermute(array, AXES, [(i, i ^ mask) for i in range(count)])  41.5 us
    ppermute x27, starting transfers between devices, swap(): return lax.ppermute(array, AXES, [(i, i ^ mask) for i in range(count)])  32.3 us
    ppermute x8, starting transfers between devices, shifted(): return lax.ppermute(array, SEQ, pairs)  27.9 us
    ppermute x8, waiting for transfers between devices, shifted(): return lax.ppermute(array, SEQ, pairs)  20.9 us
  transfers between devices with their start and end apart: 42, of which 17 were waited for; matrix products, arithmetic and copies ran while one was open for 8% of the time, Pallas kernels for 26%

profile of v3, /device:TPU:0, one launch (start us, length us, event | category | flops | bytes accessed | tf_op | source)
XLA Modules:
  0.0 480.2 jit_solution(1306370297890957375)
XLA Ops:
  33.9 20.7 %all-to-all-done = bf16[4,32,2688]{2,1,0:T(8,128)(2,1)S(1)} async-done(((bf16[4,32,2688]{2,1,0:T(8,128)(2,1)}), bf16[4,32,2688]{2,1,0:T(8,128)(2,1)S(1)}, u32[]{:S(2)}, u32[]{:S(2)}) %all-to-all-start) | async-done | bytes 688160 | tf_op jit(solution)/shard_map/all_to_all | solution.py:176
  60.7 11.5 %collective-permute-done.10 = bf16[4,32,1536]{2,1,0:T(8,128)(2,1)S(1)} collective-permute-done((bf16[4,32,1536]{2,1,0:T(8,128)(2,1)S(1)}, bf16[4,32,1536]{2,1,0:T(8,128)(2,1)S(1)}, u32[]{:S(2)}, u32[]{:S(2)}) %collective-permute-start.10) | collective-permute-done | bytes 393248 | tf_op jit(solution)/shard_map/ppermute | solution.py:96
  76.5 15.7 %collective-permute-done.11 = bf16[4,2,32,1536]{3,2,1,0:T(8,128)(2,1)S(1)} collective-permute-done((bf16[4,2,32,1536]{3,2,1,0:T(8,128)(2,1)S(1)}, bf16[4,2,32,1536]{3,2,1,0:T(8,128)(2,1)S(1)}, u32[]{:S(2)}, u32[]{:S(2)}) %collective-permute-start.11) | collective-permute-done | bytes 786464 | tf_op jit(solution)/shard_map/ppermute | solution.py:96
  111.8 8.3 %front.1 = (bf16[8,256,128]{2,1,0:T(8,128)(2,1)}, bf16[256,256]{1,0:T(8,128)(2,1)}, bf16[256,1024]{1,0:T(8,128)(2,1)}, bf16[16,1024]{1,0:T(8,128)(2,1)}, bf16[27...) custom-call(s32[1]{0:T(128)} %bitcast.core_ref, ...), custom_call_target="tpu_custom_call" | custom-call | flops 52800000000 | bytes 11728388 | tf_op jit(solution)/shard_map/front/pallas_call | solution.py:1131
  132.0 7.7 %scan.1.yl_ref = f32[256,1536]{1,0:T(8,128)} custom-call(f32[256,1536]{1,0:T(8,128)} %get-tuple-element.262.x_ref, f32[256,256]{1,0:T(8,128)} %get-tuple-element.263.bc_ref, f32[256,128]{1,0:T(8,128)} %get-tuple-element.264.step_ref, f32[256,128]{1,0:T(8,128)} %get-tuple-element.265.cum_ref, f32[128,256]{1,0:T(8,128)} %get-tuple-element.224.cumt_ref, ...), custom_call_target="tpu_custom_call" | custom-call | flops 52800000000 | bytes 3802112 | tf_op jit(solution)/shard_map/scan/pallas_call | solution.py:1131
  141.4 8.8 %collective-permute-done.13 = bf16[1552,128]{1,0:T(8,128)(2,1)S(1)} collective-permute-done((bf16[1552,128]{1,0:T(8,128)(2,1)S(1)}, bf16[1552,128]{1,0:T(8,128)(2,1)S(1)}, u32[]{:S(2)}, u32[]{:S(2)}) %collective-permute-start.13) | collective-permute-done | bytes 397344 | tf_op jit(solution)/shard_map/ppermute | solution.py:186
  151.0 14.4 %collective-permute-start.15 = (bf16[1552,128]{1,0:T(8,128)(2,1)S(1)}, bf16[1552,128]{1,0:T(8,128)(2,1)}, u32[]{:S(2)}, u32[]{:S(2)}) collective-permute-start(bf16[1552,128]{1,0:T(8,128)(2,1)S(1)} %fusion.4), channel_id=1, source_target_pairs={{0,2},{1,3},{2,4},{3,5},{4,6},{5,7},{8,10},{9,11},{10,12},{11,13},... | collective-permute-start | bytes 1191944 | tf_op jit(solution)/shard_map/ppermute | solution.py:186
  165.4 17.5 %all-to-all-done.1.kv_ref = bf16[8,256,256]{2,1,0:T(8,128)(2,1)} async-done(((bf16[8,256,256]{2,1,0:T(8,128)(2,1)}), bf16[8,256,256]{2,1,0:T(8,128)(2,1)}, u32[]{:S(2)}, u32[]{:S(2)}) %all-to-all-start.1) | async-done | bytes 1048608 | tf_op jit(solution)/shard_map/all_to_all | solution.py:176
  183.0 10.3 %attend.1 = (bf16[256,512]{1,0:T(8,128)(2,1)}, f32[128,256]{1,0:T(8,128)}) custom-call(s32[1]{0:T(128)} %bitcast.1.rank_ref, bf16[8,256,128]{2,1,0:T(8,128)(2,1)} %get-tuple-element.240.q8_ref, bf16[8,256,256]{2,1,0:T(8,128)(2,1)} %all-to-all-done.1.kv_ref, s32[256,1]{1,0:T(8,128)} %select_subtract_fusion.off_ref), custom_call_target="tpu_custom_call" | custom-call | flops 65999998976 | bytes 1967108 | tf_op jit(solution)/shard_map/attend/pallas_call | solution.py:1131
  195.6 31.3 %post.1 = (bf16[256,1024]{1,0:T(8,128)(2,1)}, f32[256,1024]{1,0:T(8,128)}, bf16[256,512]{1,0:T(8,128)(2,1)}, f32[256,1536]{1,0:T(8,128)}, f32[256,1536]{1,0:T(8,...) custom-call(s32[1]{0:T(128)} %bitcast.core_ref, ...), custom_call_target="tpu_custom_call" | custom-call | flops 198000001024 | bytes 39994372 | tf_op jit(solution)/shard_map/post/pallas_call | solution.py:1131
  231.0 8.8 %scan_back.1 = (f32[256,1536]{1,0:T(8,128)}, bf16[256,256]{1,0:T(8,128)(2,1)}) custom-call(f32[256,1536]{1,0:T(8,128)} %get-tuple-element.260.dy_ref, f32[256,1536]{1,0:T(8,128)} %get-tuple-element.262.x_ref, f32[256,256]{1,0:T(8,128)} %get-tuple-element.263.bc_ref, f32[256,128]{1,0:T(8,128)} %get-tuple-element.264.step_ref, ...), custom_call_target="tpu_custom_call" | custom-call | flops 59399999488 | bytes 5506048 | tf_op jit(solution)/shard_map/scan_back/pallas_call | solution.py:1131
  239.8 8.6 %collective-permute-done.18 = bf16[1552,128]{1,0:T(8,128)(2,1)S(1)} collective-permute-done((bf16[1552,128]{1,0:T(8,128)(2,1)S(1)}, bf16[1552,128]{1,0:T(8,128)(2,1)S(1)}, u32[]{:S(2)}, u32[]{:S(2)}) %collective-permute-start.18) | collective-permute-done | bytes 397344 | tf_op jit(solution)/shard_map/ppermute | solution.py:186
  253.7 8.0 %weights_one.1 = (bf16[2,4,32,2048]{3,2,1,0:T(8,128)(2,1)}, bf16[2,4,32,2048]{3,2,1,0:T(8,128)(2,1)}, bf16[8,64,1024]{2,1,0:T(8,128)(2,1)}, bf16[8,64,1024]{2,1,0:T(8,128)(2,1)}) custom-call(s32[1]{0:T(128)} %bitcast.37.y_ref, s32[1]{0:T(128)} %bitcast.38.x_ref, bf16[256,3072]{1,0:T(8,128)(2,1)} %get-tuple-element.234.keep_ref, ...), custom_call_target="tpu_custom_call" | custom-call | flops 59399999488 | bytes 16777224 | tf_op jit(solution)/shard_map/weights_one/pallas_call | solution.py:1131
  261.7 8.1 %collective-permute-start.20 = (bf16[2,4,32,2048]{3,2,1,0:T(8,128)(2,1)}, bf16[2,4,32,2048]{3,2,1,0:T(8,128)(2,1)}, u32[]{:S(2)}, u32[]{:S(2)}) collective-permute-start(bf16[2,4,32,2048]{3,2,1,0:T(8,128)(2,1)} %get-tuple-element.232), channel_id=1, source_target_pairs={{0,1},{1,0},{2,3},{3,2},{4,5},{5,4},{6,7},{7,6},{8,9},{9,8},{10,11... | collective-permute-start | bytes 3145736 | tf_op jit(solution)/shard_map/ppermute | solution.py:96
  271.2 9.3 %weights_two.1 = (bf16[2,4,32,3584]{3,2,1,0:T(8,128)(2,1)}, bf16[2,4,32,3584]{3,2,1,0:T(8,128)(2,1)}, bf16[8,64,1024]{2,1,0:T(8,128)(2,1)}, bf16[8,64,1024]{2,1,0:T(8,128)(2,1)}) custom-call(s32[1]{0:T(128)} %bitcast.37.y_ref, s32[1]{0:T(128)} %bitcast.38.x_ref, bf16[256,3072]{1,0:T(8,128)(2,1)} %get-tuple-element.234.keep_ref, ...), custom_call_target="tpu_custom_call" | custom-call | flops 59399999488 | bytes 18350088 | tf_op jit(solution)/shard_map/weights_two/pallas_call | solution.py:1131
  282.7 14.3 %attend_back.1 = (bf16[256,512]{1,0:T(8,128)(2,1)}, bf16[8,256,256]{2,1,0:T(8,128)(2,1)}) custom-call(s32[1]{0:T(128)} %bitcast.1.rank_ref, bf16[8,256,128]{2,1,0:T(8,128)(2,1)} %get-tuple-element.240.q8_ref, bf16[8,256,256]{2,1,0:T(8,128)(2,1)} %all-to-all-done.1.kv_ref, s32[1,256]{1,0:T(1,128)} %fusion.14.off_ref, f32[128,256]{1,0:T(8,128)} %get-tuple-element.243.lse_ref, ...), custom_call_target="tpu_custom_call" | custom-call | flops 92400001024 | bytes 3539972 | tf_op jit(solution)/shard_map/attend_back/pallas_call | solution.py:1131
  297.1 15.8 %all-to-all-start.2 = ((bf16[8,256,256]{2,1,0:T(8,128)(2,1)}), bf16[8,256,256]{2,1,0:T(8,128)(2,1)S(1)}, u32[]{:S(2)}, u32[]{:S(2)}) async-start(bf16[8,256,256]{2,1,0:T(8,128)(2,1)} %get-tuple-element.248), calls=%async_computation.2 | async-start | bytes 2097152 | tf_op jit(solution)/shard_map/all_to_all | solution.py:176
  322.5 12.6 %mixer_back.1 = (f32[272,1792]{1,0:T(8,128)}, f32[256,128]{1,0:T(8,128)}, f32[8,1792]{1,0:T(8,128)}) custom-call(f32[256,1536]{1,0:T(8,128)} %get-tuple-element.260.dy_ref, f32[256,1536]{1,0:T(8,128)} %get-tuple-element.261.ycore_ref, f32[256,1536]{1,0:T(8,128)} %get-tuple-element.262.x_ref, f32[256,256]{1,0:T(8,128)} %get-tuple-element.263.bc_ref, ...), custom_call_target="tpu_custom_call" | custom-call | flops 85800001536 | bytes 11835904 | tf_op jit(solution)/shard_map/mixer_back/pallas_call | solution.py:1131
  335.1 9.6 %all-to-all-done.2.dkv_ref = bf16[8,256,256]{2,1,0:T(8,128)(2,1)S(1)} async-done(((bf16[8,256,256]{2,1,0:T(8,128)(2,1)}), bf16[8,256,256]{2,1,0:T(8,128)(2,1)S(1)}, u32[]{:S(2)}, u32[]{:S(2)}) %all-to-all-start.2) | async-done | bytes 1048608 | tf_op jit(solution)/shard_map/all_to_all | solution.py:176
  356.6 7.0 %back.1 = (f32[256,1024]{1,0:T(8,128)}, f32[16,1024]{1,0:T(8,128)}) custom-call(s32[1]{0:T(128)} %bitcast.core_ref, bf16[272,3200]{1,0:T(8,128)(2,1)} %get-tuple-element.300.gab_ref.own_ref, bf16[2,256,1152]{2,1,0:T(8,128)(2,1)} %bitcast.91, bf16[2,256,1152]{2,1,0:T(8,128)(2,1)} %bitcast.93, bf16[2,256,1536]{2,1,0:T(8,128)(2,1)} %pad_maximum_fusion.wb_own, ...), custom_call_target="tpu_custom_call" | custom-call | flops 46200000512 | bytes 11018244 | tf_op jit(solution)/shard_map/back/pallas_call | solution.py:1131
  369.5 13.9 %all-to-all-start.3 = ((bf16[4,256,512]{2,1,0:T(8,128)(2,1)}), bf16[4,256,512]{2,1,0:T(8,128)(2,1)S(1)}, u32[]{:S(2)}, u32[]{:S(2)}) async-start(bf16[4,256,512]{2,1,0:T(8,128)(2,1)} %fold_two.3), calls=%async_computation.3 | async-start | bytes 2097152 | tf_op jit(solution)/shard_map/all_to_all | solution.py:176
  394.2 14.9 %all-to-all-done.3.got_ref = bf16[4,256,512]{2,1,0:T(8,128)(2,1)S(1)} async-done(((bf16[4,256,512]{2,1,0:T(8,128)(2,1)}), bf16[4,256,512]{2,1,0:T(8,128)(2,1)S(1)}, u32[]{:S(2)}, u32[]{:S(2)}) %all-to-all-start.3) | async-done | bytes 1048608 | tf_op jit(solution)/shard_map/all_to_all | solution.py:176
  433.9 14.2 %all-to-all-done.4.got_ref = bf16[4,352,512]{2,1,0:T(8,128)(2,1)S(1)} async-done(((bf16[4,352,512]{2,1,0:T(8,128)(2,1)}), bf16[4,352,512]{2,1,0:T(8,128)(2,1)S(1)}, u32[]{:S(2)}, u32[]{:S(2)}) %all-to-all-start.4) | async-done | bytes 1441824 | tf_op jit(solution)/shard_map/all_to_all | solution.py:176
  456.4 12.7 %all-to-all-done.5.got_ref = bf16[4,224,384]{2,1,0:T(8,128)(2,1)} async-done(((bf16[4,224,384]{2,1,0:T(8,128)(2,1)}), bf16[4,224,384]{2,1,0:T(8,128)(2,1)}, u32[]{:S(2)}, u32[]{:S(2)}) %all-to-all-start.5) | async-done | bytes 688160 | tf_op jit(solution)/shard_map/all_to_all | solution.py:176
  (256 shorter events, 158.2 us)
Async XLA Ops:
  7.3 188.3 %all-gather.3.cloned.1.call-start = ((), (), s32[]{:S(2)}) async-start(), calls=%async_computation.6 | async-start | bytes 20545536 | tf_op jit(solution)/shard_map/all_gather | solution.py:1208
  15.5 82.2 %collective-permute-start = (bf16[16,1024]{1,0:T(8,128)(2,1)S(1)}, bf16[16,1024]{1,0:T(8,128)(2,1)S(1)}, u32[]{:S(2)}, u32[]{:S(2)}) collective-permute-start(bf16[16,1024]{1,0:T(8,128)(2,1)S(1)} %slice.114), channel_id=1, source_target_pairs={{0,1},{1,2},{2,3},{3,4},{4,5},{5,6},{6,7},{8,9},{9,10},{10,11},{11... | collective-permute-start | bytes 98312 | tf_op jit(solution)/shard_map/ppermute | solution.py:186
  21.0 33.6 %all-to-all-start = ((bf16[4,32,2688]{2,1,0:T(8,128)(2,1)}), bf16[4,32,2688]{2,1,0:T(8,128)(2,1)S(1)}, u32[]{:S(2)}, u32[]{:S(2)}) async-start(bf16[4,32,2688]{2,1,0:T(8,128)(2,1)} %broadcast_in_dim.70), calls=%async_computation | async-start | bytes 1376256 | tf_op jit(solution)/shard_map/all_to_all | solution.py:176
  33.3 25.7 %collective-permute-start.4 = (f32[4,512]{1,0:T(4,128)S(1)}, f32[4,512]{1,0:T(4,128)S(1)}, u32[]{:S(2)}, u32[]{:S(2)}) collective-permute-start(f32[4,512]{1,0:T(4,128)S(1)} %pad_maximum_fusion.11), channel_id=1, source_target_pairs={{0,1},{1,0},{2,3},{3,2},{4,5},{5,4},{6,7},{7,6},{8,9},{9,8},{10,11... | collective-permute-start | bytes 24584 | tf_op jit(solution)/shard_map/ppermute | solution.py:96
  123.4 26.8 %collective-permute-start.13 = (bf16[1552,128]{1,0:T(8,128)(2,1)S(1)}, bf16[1552,128]{1,0:T(8,128)(2,1)S(1)}, u32[]{:S(2)}, u32[]{:S(2)}) collective-permute-start(bf16[1552,128]{1,0:T(8,128)(2,1)S(1)} %pad_maximum_fusion.6), channel_id=1, source_target_pairs={{0,1},{1,2},{2,3},{3,4},{4,5},{5,6},{6,7},{8,9},{9,10},{10,11},{11... | collective-permute-start | bytes 1191944 | tf_op jit(solution)/shard_map/ppermute | solution.py:186
  127.7 55.3 %all-to-all-start.1 = ((bf16[8,256,256]{2,1,0:T(8,128)(2,1)}), bf16[8,256,256]{2,1,0:T(8,128)(2,1)}, u32[]{:S(2)}, u32[]{:S(2)}) async-start(bf16[8,256,256]{2,1,0:T(8,128)(2,1)} %broadcast_in_dim.75), calls=%async_computation.1 | async-start | bytes 2097152 | tf_op jit(solution)/shard_map/all_to_all | solution.py:176
  151.0 42.2 %collective-permute-start.15 = (bf16[1552,128]{1,0:T(8,128)(2,1)S(1)}, bf16[1552,128]{1,0:T(8,128)(2,1)}, u32[]{:S(2)}, u32[]{:S(2)}) collective-permute-start(bf16[1552,128]{1,0:T(8,128)(2,1)S(1)} %fusion.4), channel_id=1, source_target_pairs={{0,2},{1,3},{2,4},{3,5},{4,6},{5,7},{8,10},{9,11},{10,12},{11,13},... | collective-permute-start | bytes 1191944 | tf_op jit(solution)/shard_map/ppermute | solution.py:186
  252.4 44.6 %collective-permute-start.19 = (bf16[1552,128]{1,0:T(8,128)(2,1)}, bf16[1552,128]{1,0:T(8,128)(2,1)}, u32[]{:S(2)}, u32[]{:S(2)}) collective-permute-start(bf16[1552,128]{1,0:T(8,128)(2,1)} %fusion.5), channel_id=1, source_target_pairs={{2,0},{3,1},{4,2},{5,3},{6,4},{7,5},{10,8},{11,9},{12,10},{13,11},... | collective-permute-start | bytes 1191944 | tf_op jit(solution)/shard_map/ppermute | solution.py:186
  261.7 53.5 %collective-permute-start.20 = (bf16[2,4,32,2048]{3,2,1,0:T(8,128)(2,1)}, bf16[2,4,32,2048]{3,2,1,0:T(8,128)(2,1)}, u32[]{:S(2)}, u32[]{:S(2)}) collective-permute-start(bf16[2,4,32,2048]{3,2,1,0:T(8,128)(2,1)} %get-tuple-element.232), channel_id=1, source_target_pairs={{0,1},{1,0},{2,3},{3,2},{4,5},{5,4},{6,7},{7,6},{8,9},{9,8},{10,11... | collective-permute-start | bytes 3145736 | tf_op jit(solution)/shard_map/ppermute | solution.py:96
  269.8 45.4 %collective-permute-start.21 = (bf16[8,64,1024]{2,1,0:T(8,128)(2,1)}, bf16[8,64,1024]{2,1,0:T(8,128)(2,1)}, u32[]{:S(2)}, u32[]{:S(2)}) collective-permute-start(bf16[8,64,1024]{2,1,0:T(8,128)(2,1)} %get-tuple-element.233), channel_id=1, source_target_pairs={{0,16},{1,17},{2,18},{3,19},{4,20},{5,21},{6,22},{7,23},{8,24},{9,... | collective-permute-start | bytes 3145736 | tf_op jit(solution)/shard_map/ppermute | solution.py:96
  280.4 69.0 %collective-permute-start.23 = (bf16[8,64,1024]{2,1,0:T(8,128)(2,1)}, bf16[8,64,1024]{2,1,0:T(8,128)(2,1)}, u32[]{:S(2)}, u32[]{:S(2)}) collective-permute-start(bf16[8,64,1024]{2,1,0:T(8,128)(2,1)} %get-tuple-element.238), channel_id=1, source_target_pairs={{0,16},{1,17},{2,18},{3,19},{4,20},{5,21},{6,22},{7,23},{8,24},{9,... | collective-permute-start | bytes 3145736 | tf_op jit(solution)/shard_map/ppermute | solution.py:96
  281.1 68.3 %collective-permute-start.22 = (bf16[2,4,32,3584]{3,2,1,0:T(8,128)(2,1)}, bf16[2,4,32,3584]{3,2,1,0:T(8,128)(2,1)}, u32[]{:S(2)}, u32[]{:S(2)}) collective-permute-start(bf16[2,4,32,3584]{3,2,1,0:T(8,128)(2,1)} %get-tuple-element.237), channel_id=1, source_target_pairs={{0,1},{1,0},{2,3},{3,2},{4,5},{5,4},{6,7},{7,6},{8,9},{9,8},{10,11... | collective-permute-start | bytes 5505032 | tf_op jit(solution)/shard_map/ppermute | solution.py:96
  297.1 47.6 %all-to-all-start.2 = ((bf16[8,256,256]{2,1,0:T(8,128)(2,1)}), bf16[8,256,256]{2,1,0:T(8,128)(2,1)S(1)}, u32[]{:S(2)}, u32[]{:S(2)}) async-start(bf16[8,256,256]{2,1,0:T(8,128)(2,1)} %get-tuple-element.248), calls=%async_computation.2 | async-start | bytes 2097152 | tf_op jit(solution)/shard_map/all_to_all | solution.py:176
  319.4 47.1 %collective-permute-start.26 = (bf16[4,32,2048]{2,1,0:T(8,128)(2,1)}, bf16[4,32,2048]{2,1,0:T(8,128)(2,1)}, u32[]{:S(2)}, u32[]{:S(2)}) collective-permute-start(bf16[4,32,2048]{2,1,0:T(8,128)(2,1)} %get-tuple-element.258), channel_id=1, source_target_pairs={{0,16},{1,17},{2,18},{3,19},{4,20},{5,21},{6,22},{7,23},{8,24},{9,... | collective-permute-start | bytes 1572872 | tf_op jit(solution)/shard_map/ppermute | solution.py:96
  320.5 46.0 %collective-permute-start.27 = (bf16[4,64,1024]{2,1,0:T(8,128)(2,1)}, bf16[4,64,1024]{2,1,0:T(8,128)(2,1)}, u32[]{:S(2)}, u32[]{:S(2)}) collective-permute-start(bf16[4,64,1024]{2,1,0:T(8,128)(2,1)} %get-tuple-element.259), channel_id=1, source_target_pairs={{0,1},{1,0},{2,3},{3,2},{4,5},{5,4},{6,7},{7,6},{8,9},{9,8},{10,11... | collective-permute-start | bytes 1572872 | tf_op jit(solution)/shard_map/ppermute | solution.py:96
  335.1 28.5 %collective-permute-start.25 = (f32[8,1792]{1,0:T(8,128)}, f32[8,1792]{1,0:T(8,128)S(1)}, u32[]{:S(2)}, u32[]{:S(2)}) collective-permute-start(f32[8,1792]{1,0:T(8,128)} %get-tuple-element.293), channel_id=1, source_target_pairs={{0,8},{1,9},{2,10},{3,11},{4,12},{5,13},{6,14},{7,15},{8,0},{9,1},... | collective-permute-start | bytes 172040 | tf_op jit(solution)/shard_map/ppermute | solution.py:96
  349.4 33.9 %collective-permute-start.24 = (bf16[272,3200]{1,0:T(8,128)(2,1)}, bf16[272,3200]{1,0:T(8,128)(2,1)}, u32[]{:S(2)}, u32[]{:S(2)}) collective-permute-start(bf16[272,3200]{1,0:T(8,128)(2,1)} %get-tuple-element.300.gab_ref.own_ref), channel_id=1, source_target_pairs={{0,8},{1,9},{2,10},{3,11},{4,12},{5,13},{6,14},{7,15},{8,0},{9,1},... | collective-permute-start | bytes 5222408 | tf_op jit(solution)/shard_map/ppermute | solution.py:96
  354.6 36.1 %collective-permute-start.31 = (bf16[4,64,1024]{2,1,0:T(8,128)(2,1)}, bf16[4,64,1024]{2,1,0:T(8,128)(2,1)}, u32[]{:S(2)}, u32[]{:S(2)}) collective-permute-start(bf16[4,64,1024]{2,1,0:T(8,128)(2,1)} %get-tuple-element.286), channel_id=1, source_target_pairs={{0,1},{1,0},{2,3},{3,2},{4,5},{5,4},{6,7},{7,6},{8,9},{9,8},{10,11... | collective-permute-start | bytes 1572872 | tf_op jit(solution)/shard_map/ppermute | solution.py:96
  363.6 27.1 %collective-permute-start.30 = (bf16[4,32,3584]{2,1,0:T(8,128)(2,1)S(1)}, bf16[4,32,3584]{2,1,0:T(8,128)(2,1)}, u32[]{:S(2)}, u32[]{:S(2)}) collective-permute-start(bf16[4,32,3584]{2,1,0:T(8,128)(2,1)S(1)} %copy-done.30), channel_id=1, source_target_pairs={{0,16},{1,17},{2,18},{3,19},{4,20},{5,21},{6,22},{7,23},{8,24},{9,... | collective-permute-start | bytes 2752520 | tf_op jit(solution)/shard_map/ppermute | solution.py:96
  369.5 39.7 %all-to-all-start.3 = ((bf16[4,256,512]{2,1,0:T(8,128)(2,1)}), bf16[4,256,512]{2,1,0:T(8,128)(2,1)S(1)}, u32[]{:S(2)}, u32[]{:S(2)}) async-start(bf16[4,256,512]{2,1,0:T(8,128)(2,1)} %fold_two.3), calls=%async_computation.3 | async-start | bytes 2097152 | tf_op jit(solution)/shard_map/all_to_all | solution.py:176
  389.8 26.0 %collective-permute-start.28 = (bf16[2,4,32,1152]{3,2,1,0:T(8,128)(2,1)}, bf16[2,4,32,1152]{3,2,1,0:T(8,128)(2,1)}, u32[]{:S(2)}, u32[]{:S(2)}) collective-permute-start(bf16[2,4,32,1152]{3,2,1,0:T(8,128)(2,1)} %get-tuple-element.304), channel_id=1, source_target_pairs={{0,1},{1,0},{2,3},{3,2},{4,5},{5,4},{6,7},{7,6},{8,9},{9,8},{10,11... | collective-permute-start | bytes 1769480 | tf_op jit(solution)/shard_map/ppermute | solution.py:96
  389.8 26.0 %collective-permute-start.29 = (bf16[8,32,1536]{2,1,0:T(8,128)(2,1)}, bf16[8,32,1536]{2,1,0:T(8,128)(2,1)}, u32[]{:S(2)}, u32[]{:S(2)}) collective-permute-start(bf16[8,32,1536]{2,1,0:T(8,128)(2,1)} %get-tuple-element.305), channel_id=1, source_target_pairs={{0,16},{1,17},{2,18},{3,19},{4,20},{5,21},{6,22},{7,23},{8,24},{9,... | collective-permute-start | bytes 2359304 | tf_op jit(solution)/shard_map/ppermute | solution.py:96
  410.2 37.9 %all-to-all-start.4 = ((bf16[4,352,512]{2,1,0:T(8,128)(2,1)}), bf16[4,352,512]{2,1,0:T(8,128)(2,1)S(1)}, u32[]{:S(2)}, u32[]{:S(2)}) async-start(bf16[4,352,512]{2,1,0:T(8,128)(2,1)} %fold_two.4), calls=%async_computation.4 | async-start | bytes 2883584 | tf_op jit(solution)/shard_map/all_to_all | solution.py:176
  421.3 33.6 %collective-permute-start.32 = (f32[16,1024]{1,0:T(8,128)S(1)}, f32[16,1024]{1,0:T(8,128)S(1)}, u32[]{:S(2)}, u32[]{:S(2)}) collective-permute-start(f32[16,1024]{1,0:T(8,128)S(1)} %copy-done.33), channel_id=1, source_target_pairs={{1,0},{2,1},{3,2},{4,3},{5,4},{6,5},{7,6},{9,8},{10,9},{11,10},{12... | collective-permute-start | bytes 196616 | tf_op jit(solution)/shard_map/ppermute | solution.py:186
  (53 other events, 632.2 us)
Sparse Core Ops, SparseCore 0:
  11.0 181.6 all-gather.2

commit v4 on v3

--- a/solution.py
+++ b/solution.py
@@ -746,11 +746,11 @@
         out = outs[which]
         for y in range(out.shape[0]):
             left = keep_ref[:, a_at + y * size : a_at + (y + 1) * size]
-            right = act_ref[:, act_at + y * size : act_at + (y + 1) * size]
+            right = act_ref[: left.shape[0], act_at + y * size : act_at + (y + 1) * size]
             for j in range(0, out.shape[-1], 512):
                 stop = min(j + 512, out.shape[-1])
-                total = tn(left, own_ref[:, g_at + j : g_at + stop])
-                total = total + tn(right, got_ref[:, g_at + j : g_at + stop])
+                total = tn(left, own_ref[: left.shape[0], g_at + j : g_at + stop])
+                total = total + tn(right, got_ref[: left.shape[0], g_at + j : g_at + stop])
                 if extra and which == 0 and stop == out.shape[-1]:
                     total = total + extra_ref[y]
                 out[y, :, j:stop] = total.astype(bf16)
@@ -761,18 +761,19 @@
     if extra:
         (extra_ref, *outs) = refs
     xkeep_ref, xsend_ref, ykeep_ref, ysend_ref = outs
+    rows = keep_ref.shape[0]
     my_y, my_x = y_ref[0], x_ref[0]
     for kind, place, a_at, act_at, size, g_at, wide in plan:
         for k in range(2):
             y = k if kind == "x" else lax.rem(my_y + k, 2)
             left = keep_ref[:, pl.ds(pl.multiple_of(a_at + y * size, LANES), size)]
-            right = act_ref[:, pl.ds(pl.multiple_of(act_at + y * size, LANES), size)]
+            right = act_ref[:rows, pl.ds(pl.multiple_of(act_at + y * size, LANES), size)]
             keep, send = (xkeep_ref, xsend_ref) if kind == "x" else (ykeep_ref, ysend_ref)
             block = 512 if wide % 512 == 0 else 384
 
             def columns(j, unused):
                 at = pl.ds(pl.multiple_of(g_at + j * block, LANES), block)
-                total = tn(left, own_ref[:, at]) + tn(right, got_ref[:, at])
+                total = tn(left, own_ref[:rows, at]) + tn(right, got_ref[:rows, at])
                 if kind == "x":
                     zs, each = keep.shape[1], keep.shape[2]
                     if extra:
@@ -817,24 +818,35 @@
             at += each
 
 
-def fold_two_kernel(xkeep_ref, xgot_ref, ykeep_ref, ygot_ref, out_ref):
-    width = out_ref.shape[2]
+def fold_two_kernel(z_ref, xkeep_ref, xgot_ref, ykeep_ref, ygot_ref, keep_out, send_out):
+    low = lax.rem(z_ref[0], 2)
+    width = keep_out.shape[2]
     keeps = laid((xkeep_ref, ykeep_ref), width)
     gots = laid((xgot_ref, ygot_ref), width)
     for (keep, at, col), (got, *unused) in zip(keeps, gots):
-        each = keep.shape[-2]
-        value = keep[:, :, col : col + width] + got[:, :, col : col + width].astype(f32)
-        out_ref[:, at : at + each, :] = value.astype(bf16)
-
-
-def fold_three_kernel(got_ref, *outs):
-    width = got_ref.shape[2]
-    for out, at, col in laid(outs, width):
+        rows, cols = slice(at, at + keep.shape[-2]), slice(col, col + width)
+        for high in range(keep_out.shape[0]):
+            for out, z in ((keep_out, 2 * high + low), (send_out, 2 * high + 1 - low)):
+                value = keep[z, :, cols] + got[z, :, cols].astype(f32)
+                out[high, rows, :] = value.astype(out.dtype)
+
+
+def fold_three_kernel(z_ref, keep_ref, got_ref, keep_out, send_out):
+    high = lax.div(z_ref[0], 2)
+    keep_out[...] = keep_ref[high] + got_ref[high].astype(f32)
+    other = 1 - high
+    send_out[...] = (keep_ref[other] + got_ref[other].astype(f32)).astype(bf16)
+
+
+def summed(refs, rows):
+    keep_ref, got_ref = refs
+    return keep_ref[rows, :] + got_ref[rows, :].astype(f32)
+
+
+def fold_four_kernel(keep_ref, got_ref, *outs):
+    for out, at, col in laid(outs, keep_ref.shape[1]):
         rows = slice(at, at + out.shape[0])
-        total = got_ref[0, rows, :].astype(f32)
-        for z in range(1, got_ref.shape[0]):
-            total = total + got_ref[z, rows, :].astype(f32)
-        out[:, col : col + width] = total
+        out[:, col : col + keep_ref.shape[1]] = summed((keep_ref, got_ref), rows)
 
 
 def row_sums(value):
@@ -842,47 +854,42 @@
     return sum(nt(ones, part) for part in terms(value, 3))[:1]
 
 
-def summed(got_ref, rows):
-    total = got_ref[0, rows, :].astype(f32)
-    for z in range(1, got_ref.shape[0]):
-        total = total + got_ref[z, rows, :].astype(f32)
-    return total
-
-
 def finish_post_kernel(
-    got_ref, one_ref, guw_ref, sow_ref, gffn_ref, gssm_ref,
+    keep_ref, sum_ref, one_ref, guw_ref, sow_ref, gffn_ref, gssm_ref,
     gu_ref, gate_ref, ao_ref, so_ref, dffn_ref, dssm_ref,
 ):
+    both = (keep_ref, sum_ref)
     part, ups = one_ref.shape
-    wide = got_ref.shape[2]
+    wide = keep_ref.shape[1]
     gu_ref[:, :ups] = one_ref[...]
     at = 0
     for out, start in ((gu_ref, ups), (gate_ref, 0)):
         for col in range(start, out.shape[1], wide):
-            out[:, col : col + wide] = summed(got_ref, slice(at, at + part))
+            out[:, col : col + wide] = summed(both, slice(at, at + part))
             at += part
     for col in range(0, ao_ref.shape[1], wide):
         for out in (ao_ref, so_ref):
-            out[:, col : col + wide] = summed(got_ref, slice(at, at + out.shape[0]))
+            out[:, col : col + wide] = summed(both, slice(at, at + out.shape[0]))
             at += out.shape[0]
     dffn_ref[...] = row_sums(guw_ref[...].astype(f32) * gu_ref[...]) / gffn_ref[...]
     dssm_ref[...] = row_sums(sow_ref[...].astype(f32) * so_ref[...]) / gssm_ref[...]
 
 
 def finish_front_kernel(
-    got_ref, gate_ref, kvw_ref, qw_ref, iw_ref, gain_ref,
+    keep_ref, sum_ref, gate_ref, kvw_ref, qw_ref, iw_ref, gain_ref,
     kv_ref, q_ref, inner_ref, conv_ref, bias_ref, log_ref, step_ref, skip_ref, dgain_ref,
 ):
-    part, wide = kv_ref.shape[0], got_ref.shape[2]
+    both = (keep_ref, sum_ref)
+    part, wide = kv_ref.shape[0], keep_ref.shape[1]
     count = A_COLS // wide
-    blocks = [summed(got_ref, slice(k * part, (k + 1) * part)) for k in range(count)]
+    blocks = [summed(both, slice(k * part, (k + 1) * part)) for k in range(count)]
     first = jnp.concatenate(blocks, axis=1)
     kv_ref[...] = first[:, :256]
     q_ref[...] = first[:, 256:768]
     inner_ref[:, :DS] = gate_ref[...]
     for k in range(DS // wide):
         rows = slice((count + k) * part, (count + k + 1) * part)
-        inner_ref[:, DS + k * wide : DS + (k + 1) * wide] = summed(got_ref, rows)
+        inner_ref[:, DS + k * wide : DS + (k + 1) * wide] = summed(both, rows)
     last = first[:, 1024:]
     inner_ref[:, 2 * DS : 2 * DS + 2 * STATE] = first[:, 768:1024]
     inner_ref[:, DS + CONV_CH :] = last[:, :SSM_HEADS]
@@ -900,7 +907,7 @@
 
 class PairReduction:
     def __init__(self, pieces, width):
-        self.places = tuple(place_on(g).reshape(1).astype(jnp.int32) for g in ("y", "x"))
+        self.places = tuple(place_on(g).reshape(1).astype(jnp.int32) for g in ("y", "x", "z"))
         self.xkeep, xsend, self.ykeep, ysend = pieces
         self.width = width
         self.send(xsend, ysend, "x", "y")
@@ -917,7 +924,7 @@
         x, y = x[1:], (y[0] // 2, *y[1:])
         self.xkeep, xsend, self.ykeep, ysend = run(
             fold_one_kernel, "fold_one", [(x, f32), (x, bf16), (y, f32), (y, bf16)],
-            (*self.places, self.xkeep, gots[0], self.ykeep, gots[1]),
+            (*self.places[:2], self.xkeep, gots[0], self.ykeep, gots[1]),
             scalars=2,
         )
         self.send(xsend, ysend, "y", "x")
@@ -926,19 +933,28 @@
         gots = after(self.gots, *others)
         self.shapes = [self.xkeep.shape[1:], self.ykeep.shape[1:]]
         rows = sum(r * c // self.width for r, c in self.shapes)
-        zs = self.xkeep.shape[0]
-        self.sent = run(
-            fold_two_kernel, "fold_two", [((zs, rows, self.width), bf16)],
-            (self.xkeep, gots[0], self.ykeep, gots[1]),
-        )[0]
-        self.gots = dealt(self.sent, "z")
+        half = (self.xkeep.shape[0] // 2, rows, self.width)
+        self.keep, self.sent = run(
+            fold_two_kernel, "fold_two", [(half, f32), (half, bf16)],
+            (self.places[2], self.xkeep, gots[0], self.ykeep, gots[1]),
+            scalars=1,
+        )
+        self.gots = swap(self.sent, extents()["z"][0])
 
     def fold_three(self, *others):
-        gots = after(self.gots, *others)
-        self.sent = run(
-            fold_three_kernel, "fold_three", [(shape, f32) for shape in self.shapes], (gots,),
+        whole = self.keep.shape[1:]
+        self.keep, self.sent = run(
+            fold_three_kernel, "fold_three", [(whole, f32), (whole, bf16)],
+            (self.places[2], self.keep, after(self.gots, *others)),
+            scalars=1,
         )
-        return self.sent
+        self.gots = swap(self.sent, 2 * extents()["z"][0])
+
+    def fold_four(self, *others):
+        return run(
+            fold_four_kernel, "fold_four", [(shape, f32) for shape in self.shapes],
+            (self.keep, after(self.gots, *others)),
+        )
 
 
 class PlainReduction:
@@ -954,8 +970,10 @@
     fold_two = fold_one
 
     def fold_three(self, *others):
-        self.sent = [part.receive(*others) for part in self.parts]
-        return self.sent
+        pass
+
+    def fold_four(self, *others):
+        return [part.receive(*others) for part in self.parts]
 
 
 def scan_back_kernel(
@@ -1061,25 +1079,28 @@
 
 def back_grads_kernel(
     ys, core_ref, dq_ref, dkv_ref, dext_ref, dz_ref, cos_ref, sin_ref, normed_ref, nrim_ref,
-    ga_ref, keep_ref,
+    small_ref, ga_ref, keep_ref,
 ):
     core = core_ref[0]
+    count, last = small_ref.shape[0], keep_ref.shape[0]
+    ga_ref[last:, :] = jnp.zeros((ga_ref.shape[0] - last, ga_ref.shape[1]), bf16)
+    ga_ref[last : last + count, :CONV_CH] = small_ref[...].astype(bf16)
     dkv = dkv_ref[0].astype(f32)
     for i in range(1, dkv_ref.shape[0]):
         dkv = dkv + dkv_ref[i].astype(f32)
     ga_ref[:RIM, :768] = jnp.zeros((RIM, 768), bf16)
     ga_ref[:RIM, 1024:A_COLS] = jnp.zeros((RIM, LANES), bf16)
-    ga_ref[RIM:, :LANES] = turned_back(dkv[:, :LANES], cos_ref[...], sin_ref[...]).astype(bf16)
-    ga_ref[RIM:, LANES:256] = dkv[:, LANES:].astype(bf16)
-    ga_ref[RIM:, 256:768] = dq_ref[...]
-    ga_ref[:, 768:1024] = dext_ref[:, DS:].astype(bf16)
-    ga_ref[RIM:, 1024:A_COLS] = dz_ref[...].astype(bf16)
-    ga_ref[:, A_COLS : A_COLS + DS] = dext_ref[:, :DS].astype(bf16)
+    ga_ref[RIM:last, :LANES] = turned_back(dkv[:, :LANES], cos_ref[...], sin_ref[...]).astype(bf16)
+    ga_ref[RIM:last, LANES:256] = dkv[:, LANES:].astype(bf16)
+    ga_ref[RIM:last, 256:768] = dq_ref[...]
+    ga_ref[:last, 768:1024] = dext_ref[:, DS:].astype(bf16)
+    ga_ref[RIM:last, 1024:A_COLS] = dz_ref[...].astype(bf16)
+    ga_ref[:last, A_COLS : A_COLS + DS] = dext_ref[:, :DS].astype(bf16)
     wide = normed_ref.shape[1] // ys
     at, to = 0, A_COLS + DS
     for y in range(ys):
         cols = slice(y * wide, (y + 1) * wide)
-        for ref, rows in ((nrim_ref, slice(0, RIM)), (normed_ref, slice(RIM, None))):
+        for ref, rows in ((nrim_ref, slice(0, RIM)), (normed_ref, slice(RIM, last))):
             own, oth = halves(ref[:, cols], core)
             keep_ref[rows, at : at + wide // 2] = own
             ga_ref[rows, to + at : to + at + wide // 2] = oth
@@ -1092,7 +1113,8 @@
 ):
     core = core_ref[0]
     for y in range(wa_own.shape[0]):
-        ga, gb = gab_ref[:, :A_COLS], gab_ref[:, A_COLS : A_COLS + DS]
+        last = tok_ref.shape[0]
+        ga, gb = gab_ref[:last, :A_COLS], gab_ref[:last, A_COLS : A_COLS + DS]
         own = nt(ga, wa_own[y]) + nt(gb, wb_own[y])
         oth = nt(ga, wa_oth[y]) + nt(gb, wb_oth[y])
         put(dn_ref, y, own, oth, core)
@@ -1430,7 +1452,24 @@
         send,
         got,
     )
-    keep, send, got = after((keep, send, got), red_one.sent)
+    dq, dkv = run(
+        functools.partial(attend_back_kernel, back + 1),
+        "attend_back",
+        [((rows, heads_width), bf16), ((seq_count, rows, 256), bf16)],
+        after((rank, q8, kv_all, off_row, lse, datt, cos, sin), red_one.sent),
+        scalars=1,
+        scratch=[
+            ((window, LANES), bf16),
+            ((window, LANES), bf16),
+            ((window, rows), f32),
+            ((HEADS, rows, LANES), bf16),
+            ((HEADS, rows, LANES), f32),
+            ((window, 256), f32),
+        ],
+        us=14,
+    )
+    dkv_got = dealt(dkv, SEQ)
+    keep, send, got = after((keep, send, got), red_one.sent, dq, dkv)
     red_two = weight_sums(
         "weights_two",
         [
@@ -1445,28 +1484,11 @@
         send,
         got,
     )
-    dq, dkv = run(
-        functools.partial(attend_back_kernel, back + 1),
-        "attend_back",
-        [((rows, heads_width), bf16), ((seq_count, rows, 256), bf16)],
-        after((rank, q8, kv_all, off_row, lse, datt, cos, sin), red_two.sent),
-        scalars=1,
-        scratch=[
-            ((window, LANES), bf16),
-            ((window, LANES), bf16),
-            ((window, rows), f32),
-            ((HEADS, rows, LANES), bf16),
-            ((HEADS, rows, LANES), f32),
-            ((window, 256), f32),
-        ],
-        us=14,
-    )
-    dkv_got = dealt(dkv, SEQ)
     while downstream is None:
-        downstream = carrying.receive(dq)
+        downstream = carrying.receive(red_two.sent)
         if downstream is None:
             carrying.send()
-    red_one.fold_one(dq, downstream)
+    red_one.fold_one(red_two.sent, downstream)
     dext, dz, small = run(
         mixer_back_kernel,
         "mixer_back",
@@ -1486,17 +1508,15 @@
         us=13,
     )
     count = lax.axis_size(AXES)
-    small_got = swap(small, core_unit)
     gab, norm_keep = run(
         functools.partial(back_grads_kernel, ys),
         "back_grads",
-        [((rows + RIM, A_COLS + DS + width // 2), bf16), ((rows + RIM, width // 2), bf16)],
-        (side, dq, dkv_got, dext, dz, cos, sin, normed, nrim),
+        [((rows + 2 * RIM, A_COLS + DS + width // 2), bf16), ((rows + RIM, width // 2), bf16)],
+        (side, dq, dkv_got, dext, dz, cos, sin, normed, nrim, small),
         scalars=1,
     )
     gab_got = swap(gab, core_unit)
-    red_two.fold_one(gab)
-    small = small + after(small_got, gab)
+    small = small + gab_got[rows + RIM : rows + RIM + small.shape[0], :CONV_CH].astype(f32)
     free = LANES - SSM_HEADS
     convs = small[: CONV + 1].reshape(CONV + 1, count, -1).transpose(1, 0, 2)
     head_sums = small[CONV + 1, : 3 * LANES].reshape(3, LANES)[:, :SSM_HEADS]
@@ -1528,15 +1548,14 @@
         "back",
         [((rows, width), f32), ((RIM, width), f32)],
         (
-            side, after(gab, red_two.sent), wa_own, wa_oth, wb_own, wb_oth, tokens_rim, dmid, dng,
+            side, gab, wa_own, wa_oth, wb_own, wb_oth, tokens_rim, dmid, dng,
             gain_one,
         ),
         scalars=1,
         scratch=[((rows + RIM, width), f32)],
         us=7,
     )
-    red_one.fold_two(grad_tokens)
-    norm_keep, gab, gab_got, extra = after((norm_keep, gab, gab_got, extra), red_one.sent)
+    norm_keep, gab, gab_got, extra = after((norm_keep, gab, gab_got, extra), grad_tokens)
     red_three = weight_sums(
         "front_weights",
         [(0, A_COLS + DS, sizes[4], 0, A_COLS)],
@@ -1546,11 +1565,16 @@
         gab_got,
         (extra,),
     )
-    red_two.fold_two(red_three.sent)
-    r_one, r_down = red_one.fold_three(red_two.sent)
-    red_three.fold_one(r_one)
-    rim_got = shifted(after(grad_rim, red_three.sent), -1)
-    red_three.fold_two(red_three.sent)
+    red_two.fold_one(red_three.sent)
+    red_one.fold_two(red_two.sent)
+    red_three.fold_one(red_one.sent)
+    red_one.fold_three(red_three.sent)
+    red_two.fold_two(red_one.sent)
+    red_three.fold_two(red_two.sent)
+    red_two.fold_three(red_three.sent)
+    rim_got = shifted(after(grad_rim, red_two.sent), -1)
+    r_one, r_down = red_one.fold_four(red_two.sent)
+    red_three.fold_three(r_one)
     if aligned:
         r_gu, r_gate, r_ao, r_so, g_ffn, g_ssm = run(
             finish_post_kernel,
@@ -1564,7 +1588,7 @@
                 ((1, s_rows), f32),
             ],
             (
-                after(red_two.gots, red_three.sent), r_one, gate_up_weight, ssm_out_weight,
+                red_two.keep, after(red_two.gots, red_three.sent), r_one, gate_up_weight, ssm_out_weight,
                 ffn_gain.astype(f32)[None, :], ssm_gain.astype(f32)[None, :],
             ),
         )
@@ -1585,17 +1609,17 @@
                 ((1, part), f32),
             ],
             (
-                after(red_three.gots, grad_tokens), r_gate, keyval_weight, query_weight,
+                red_three.keep, after(red_three.gots, grad_tokens), r_gate, keyval_weight, query_weight,
                 inner_weight, mixer_gain.astype(f32)[None, :],
             ),
         )
         g_bias, g_mixer, g_ssm, g_ffn = (v[0] for v in (g_bias, g_mixer, g_ssm, g_ffn))
         heads = [v[0] for v in (g_log, g_step, g_skip)]
     else:
-        r_two, r_out = red_two.fold_three(red_three.sent)
+        r_two, r_out = red_two.fold_four(red_three.sent)
         rim_got = after(rim_got, r_two)
         grad_tokens = grad_tokens.at[rows - RIM :].add(rim_got)
-        r_e, r_f = red_three.fold_three(grad_tokens)
+        r_e, r_f = red_three.fold_four(grad_tokens)
         r_gu = jnp.concatenate([r_one, r_two[:, :ff]], 1)
         small = r_e[:, A_COLS - free :].reshape(-1)[:slots]
         conv = small[: (CONV + 1) * conv_bias.size].reshape(CONV + 1, -1)

time: 489 us -> 468 us (0.957)
  waiting for transfers between devices: 152 us -> 128 us
  starting transfers between devices: 107 us -> 99.7 us
  Pallas kernels: 159 us -> 166 us
    all_to_all x6 -> x3, waiting for transfers between devices: 89.6 us -> 37.1 us  [dealt(): return lax.all_to_all(array, axes, 0, 0, tiled=True)]
    ppermute x27 -> x32, waiting for transfers between devices: 41.5 us -> 70.2 us  [swap(): return lax.ppermute(array, AXES, [(i, i ^ mask) for i in range(count)])]
    all_to_all x6 -> x3, starting transfers between devices: 46.7 us -> 23.3 us  [dealt(): return lax.all_to_all(array, axes, 0, 0, tiled=True)]
    ppermute x27 -> x32, starting transfers between devices: 32.3 us -> 48.4 us  [swap(): return lax.ppermute(array, AXES, [(i, i ^ mask) for i in range(count)])]
    pallas_call x22 -> x25, Pallas kernels: 159 us -> 166 us  [run(): pl.pallas_call(kernel, name=name, out_shape=shapes, in_specs=specs, out_s...]
  transfers between devices with their start and end apart: 42 -> 44, of which waited for: 17 -> 18; matrix products, arithmetic and copies ran while one was open for 8% -> 9% of each run, Pallas kernels for 26% -> 28%
where the time goes in v4:
time: 468 us; the launch traced here: 459 us
  Pallas kernels  166 us (35%)
  waiting for transfers between devices  128 us (27%)
  starting transfers between devices  99.7 us (21%)
  local copies, waits for them, and re-layouts  28.8 us (6%)
  other arithmetic  18.9 us (4%)
  between operations  17.9 us (4%)
    pallas_call x25, Pallas kernels, run(): pl.pallas_call(kernel, name=name, out_shape=shapes, in_specs=specs, out_s...  166 us
    ppermute x32, waiting for transfers between devices, swap(): return lax.ppermute(array, AXES, [(i, i ^ mask) for i in range(count)])  70.2 us
    ppermute x32, starting transfers between devices, swap(): return lax.ppermute(array, AXES, [(i, i ^ mask) for i in range(count)])  48.4 us
    all_to_all x3, waiting for transfers between devices, dealt(): return lax.all_to_all(array, axes, 0, 0, tiled=True)  37.1 us
    ppermute x8, starting transfers between devices, shifted(): return lax.ppermute(array, SEQ, pairs)  27.9 us
    all_to_all x3, starting transfers between devices, dealt(): return lax.all_to_all(array, axes, 0, 0, tiled=True)  23.3 us
    ppermute x8, waiting for transfers between devices, shifted(): return lax.ppermute(array, SEQ, pairs)  20.9 us
  transfers between devices with their start and end apart: 44, of which 18 were waited for; matrix products, arithmetic and copies ran while one was open for 9% of the time, Pallas kernels for 28%

profile of v4, /device:TPU:0, one launch (start us, length us, event | category | flops | bytes accessed | tf_op | source)
XLA Modules:
  0.0 459.5 jit_solution(1191346819306697600)
XLA Ops:
  35.0 19.6 %all-to-all-done = bf16[4,32,2688]{2,1,0:T(8,128)(2,1)S(1)} async-done(((bf16[4,32,2688]{2,1,0:T(8,128)(2,1)}), bf16[4,32,2688]{2,1,0:T(8,128)(2,1)S(1)}, u32[]{:S(2)}, u32[]{:S(2)}) %all-to-all-start) | async-done | bytes 688160 | tf_op jit(solution)/shard_map/all_to_all | solution.py:176
  60.7 11.5 %collective-permute-done.10 = bf16[4,32,1536]{2,1,0:T(8,128)(2,1)S(1)} collective-permute-done((bf16[4,32,1536]{2,1,0:T(8,128)(2,1)S(1)}, bf16[4,32,1536]{2,1,0:T(8,128)(2,1)S(1)}, u32[]{:S(2)}, u32[]{:S(2)}) %collective-permute-start.10) | collective-permute-done | bytes 393248 | tf_op jit(solution)/shard_map/ppermute | solution.py:96
  76.4 15.7 %collective-permute-done.11 = bf16[4,2,32,1536]{3,2,1,0:T(8,128)(2,1)S(1)} collective-permute-done((bf16[4,2,32,1536]{3,2,1,0:T(8,128)(2,1)S(1)}, bf16[4,2,32,1536]{3,2,1,0:T(8,128)(2,1)S(1)}, u32[]{:S(2)}, u32[]{:S(2)}) %collective-permute-start.11) | collective-permute-done | bytes 786464 | tf_op jit(solution)/shard_map/ppermute | solution.py:96
  111.8 8.3 %front.1 = (bf16[8,256,128]{2,1,0:T(8,128)(2,1)}, bf16[256,256]{1,0:T(8,128)(2,1)}, bf16[256,1024]{1,0:T(8,128)(2,1)}, bf16[16,1024]{1,0:T(8,128)(2,1)}, bf16[27...) custom-call(s32[1]{0:T(128)} %bitcast.core_ref, ...), custom_call_target="tpu_custom_call" | custom-call | flops 52800000000 | bytes 11728388 | tf_op jit(solution)/shard_map/front/pallas_call | solution.py:1153
  131.9 7.7 %scan.1.yl_ref = f32[256,1536]{1,0:T(8,128)} custom-call(f32[256,1536]{1,0:T(8,128)} %get-tuple-element.275.x_ref, f32[256,256]{1,0:T(8,128)} %get-tuple-element.276.bc_ref, f32[256,128]{1,0:T(8,128)} %get-tuple-element.277.step_ref, f32[256,128]{1,0:T(8,128)} %get-tuple-element.278.cum_ref, f32[128,256]{1,0:T(8,128)} %get-tuple-element.237.cumt_ref, ...), custom_call_target="tpu_custom_call" | custom-call | flops 52800000000 | bytes 3802112 | tf_op jit(solution)/shard_map/scan/pallas_call | solution.py:1153
  141.4 8.8 %collective-permute-done.13 = bf16[1552,128]{1,0:T(8,128)(2,1)S(1)} collective-permute-done((bf16[1552,128]{1,0:T(8,128)(2,1)S(1)}, bf16[1552,128]{1,0:T(8,128)(2,1)S(1)}, u32[]{:S(2)}, u32[]{:S(2)}) %collective-permute-start.13) | collective-permute-done | bytes 397344 | tf_op jit(solution)/shard_map/ppermute | solution.py:186
  151.0 14.5 %collective-permute-start.15 = (bf16[1552,128]{1,0:T(8,128)(2,1)S(1)}, bf16[1552,128]{1,0:T(8,128)(2,1)}, u32[]{:S(2)}, u32[]{:S(2)}) collective-permute-start(bf16[1552,128]{1,0:T(8,128)(2,1)S(1)} %fusion.4), channel_id=1, source_target_pairs={{0,2},{1,3},{2,4},{3,5},{4,6},{5,7},{8,10},{9,11},{10,12},{11,13},... | collective-permute-start | bytes 1191944 | tf_op jit(solution)/shard_map/ppermute | solution.py:186
  165.5 17.5 %all-to-all-done.1.kv_ref = bf16[8,256,256]{2,1,0:T(8,128)(2,1)} async-done(((bf16[8,256,256]{2,1,0:T(8,128)(2,1)}), bf16[8,256,256]{2,1,0:T(8,128)(2,1)}, u32[]{:S(2)}, u32[]{:S(2)}) %all-to-all-start.1) | async-done | bytes 1048608 | tf_op jit(solution)/shard_map/all_to_all | solution.py:176
  183.0 10.3 %attend.1 = (bf16[256,512]{1,0:T(8,128)(2,1)}, f32[128,256]{1,0:T(8,128)}) custom-call(s32[1]{0:T(128)} %bitcast.1.rank_ref, bf16[8,256,128]{2,1,0:T(8,128)(2,1)} %get-tuple-element.248.q8_ref, bf16[8,256,256]{2,1,0:T(8,128)(2,1)} %all-to-all-done.1.kv_ref, s32[256,1]{1,0:T(8,128)} %select_subtract_fusion.off_ref), custom_call_target="tpu_custom_call" | custom-call | flops 65999998976 | bytes 1967108 | tf_op jit(solution)/shard_map/attend/pallas_call | solution.py:1153
  195.6 31.3 %post.1 = (bf16[256,1024]{1,0:T(8,128)(2,1)}, f32[256,1024]{1,0:T(8,128)}, bf16[256,512]{1,0:T(8,128)(2,1)}, f32[256,1536]{1,0:T(8,128)}, f32[256,1536]{1,0:T(8,...) custom-call(s32[1]{0:T(128)} %bitcast.core_ref, ...), custom_call_target="tpu_custom_call" | custom-call | flops 198000001024 | bytes 39994372 | tf_op jit(solution)/shard_map/post/pallas_call | solution.py:1153
  231.0 8.8 %scan_back.1 = (f32[256,1536]{1,0:T(8,128)}, bf16[256,256]{1,0:T(8,128)(2,1)}) custom-call(f32[256,1536]{1,0:T(8,128)} %get-tuple-element.273.dy_ref, f32[256,1536]{1,0:T(8,128)} %get-tuple-element.275.x_ref, f32[256,256]{1,0:T(8,128)} %get-tuple-element.276.bc_ref, f32[256,128]{1,0:T(8,128)} %get-tuple-element.277.step_ref, ...), custom_call_target="tpu_custom_call" | custom-call | flops 59399999488 | bytes 5506048 | tf_op jit(solution)/shard_map/scan_back/pallas_call | solution.py:1153
  239.9 8.6 %collective-permute-done.18 = bf16[1552,128]{1,0:T(8,128)(2,1)S(1)} collective-permute-done((bf16[1552,128]{1,0:T(8,128)(2,1)S(1)}, bf16[1552,128]{1,0:T(8,128)(2,1)S(1)}, u32[]{:S(2)}, u32[]{:S(2)}) %collective-permute-start.18) | collective-permute-done | bytes 397344 | tf_op jit(solution)/shard_map/ppermute | solution.py:186
  253.7 8.0 %weights_one.1 = (bf16[2,4,32,2048]{3,2,1,0:T(8,128)(2,1)}, bf16[2,4,32,2048]{3,2,1,0:T(8,128)(2,1)}, bf16[8,64,1024]{2,1,0:T(8,128)(2,1)}, bf16[8,64,1024]{2,1,0:T(8,128)(2,1)}) custom-call(s32[1]{0:T(128)} %bitcast.37.y_ref, s32[1]{0:T(128)} %bitcast.38.x_ref, bf16[256,3072]{1,0:T(8,128)(2,1)} %get-tuple-element.259.keep_ref, ...), custom_call_target="tpu_custom_call" | custom-call | flops 59399999488 | bytes 16777224 | tf_op jit(solution)/shard_map/weights_one/pallas_call | solution.py:1153
  261.7 8.1 %collective-permute-start.20 = (bf16[2,4,32,2048]{3,2,1,0:T(8,128)(2,1)}, bf16[2,4,32,2048]{3,2,1,0:T(8,128)(2,1)}, u32[]{:S(2)}, u32[]{:S(2)}) collective-permute-start(bf16[2,4,32,2048]{3,2,1,0:T(8,128)(2,1)} %get-tuple-element.245), channel_id=1, source_target_pairs={{0,1},{1,0},{2,3},{3,2},{4,5},{5,4},{6,7},{7,6},{8,9},{9,8},{10,11... | collective-permute-start | bytes 3145736 | tf_op jit(solution)/shard_map/ppermute | solution.py:96
  272.6 14.3 %attend_back.1 = (bf16[256,512]{1,0:T(8,128)(2,1)}, bf16[8,256,256]{2,1,0:T(8,128)(2,1)}) custom-call(s32[1]{0:T(128)} %bitcast.1.rank_ref, bf16[8,256,128]{2,1,0:T(8,128)(2,1)} %get-tuple-element.248.q8_ref, bf16[8,256,256]{2,1,0:T(8,128)(2,1)} %all-to-all-done.1.kv_ref, s32[1,256]{1,0:T(1,128)} %fusion.14.off_ref, f32[128,256]{1,0:T(8,128)} %get-tuple-element.251.lse_ref, ...), custom_call_target="tpu_custom_call" | custom-call | flops 92400001024 | bytes 3539972 | tf_op jit(solution)/shard_map/attend_back/pallas_call | solution.py:1153
  287.0 14.1 %all-to-all-start.2 = ((bf16[8,256,256]{2,1,0:T(8,128)(2,1)}), bf16[8,256,256]{2,1,0:T(8,128)(2,1)}, u32[]{:S(2)}, u32[]{:S(2)}) async-start(bf16[8,256,256]{2,1,0:T(8,128)(2,1)} %get-tuple-element.256), calls=%async_computation.2 | async-start | bytes 2097152 | tf_op jit(solution)/shard_map/all_to_all | solution.py:176
  301.1 9.4 %weights_two.1 = (bf16[2,4,32,3584]{3,2,1,0:T(8,128)(2,1)}, bf16[2,4,32,3584]{3,2,1,0:T(8,128)(2,1)}, bf16[8,64,1024]{2,1,0:T(8,128)(2,1)}, bf16[8,64,1024]{2,1,0:T(8,128)(2,1)}) custom-call(s32[1]{0:T(128)} %bitcast.37.y_ref, s32[1]{0:T(128)} %bitcast.38.x_ref, bf16[256,3072]{1,0:T(8,128)(2,1)} %get-tuple-element.259.keep_ref, ...), custom_call_target="tpu_custom_call" | custom-call | flops 59399999488 | bytes 18350088 | tf_op jit(solution)/shard_map/weights_two/pallas_call | solution.py:1153
  321.1 12.6 %mixer_back.1 = (f32[272,1792]{1,0:T(8,128)}, f32[256,128]{1,0:T(8,128)}, f32[8,1792]{1,0:T(8,128)}) custom-call(f32[256,1536]{1,0:T(8,128)} %get-tuple-element.273.dy_ref, f32[256,1536]{1,0:T(8,128)} %get-tuple-element.274.ycore_ref, f32[256,1536]{1,0:T(8,128)} %get-tuple-element.275.x_ref, f32[256,256]{1,0:T(8,128)} %get-tuple-element.276.bc_ref, ...), custom_call_target="tpu_custom_call" | custom-call | flops 85800001536 | bytes 11835904 | tf_op jit(solution)/shard_map/mixer_back/pallas_call | solution.py:1153
  337.8 6.9 %back.1 = (f32[256,1024]{1,0:T(8,128)}, f32[16,1024]{1,0:T(8,128)}) custom-call(s32[1]{0:T(128)} %bitcast.core_ref, bf16[288,3200]{1,0:T(8,128)(2,1)} %get-tuple-element.302.gab_ref.own_ref, bf16[2,256,1152]{2,1,0:T(8,128)(2,1)} %bitcast.92, bf16[2,256,1152]{2,1,0:T(8,128)(2,1)} %bitcast.94, bf16[2,256,1536]{2,1,0:T(8,128)(2,1)} %pad_maximum_fusion.wb_own, ...), custom_call_target="tpu_custom_call" | custom-call | flops 46200000512 | bytes 11120644 | tf_op jit(solution)/shard_map/back/pallas_call | solution.py:1153
  346.1 6.5 %front_weights.1 = (bf16[2,4,32,1152]{3,2,1,0:T(8,128)(2,1)}, bf16[2,4,32,1152]{3,2,1,0:T(8,128)(2,1)}, bf16[8,32,1536]{2,1,0:T(8,128)(2,1)}, bf16[8,32,1536]{2,1,0:T(8,128)(2,1)}) custom-call(s32[1]{0:T(128)} %bitcast.37.y_ref, s32[1]{0:T(128)} %bitcast.38.x_ref, bf16[272,512]{1,0:T(8,128)(2,1)} %get-tuple-element.301.keep_ref, ...), custom_call_target="tpu_custom_call" | custom-call | flops 59399999488 | bytes 7503880 | tf_op jit(solution)/shard_map/front_weights/pallas_call | solution.py:1153
  356.1 5.1 %fold_one.4 = (f32[4,32,3584]{2,1,0:T(8,128)}, bf16[4,32,3584]{2,1,0:T(8,128)(2,1)}, f32[4,64,1024]{2,1,0:T(8,128)}, bf16[4,64,1024]{2,1,0:T(8,128)(2,1)}) custom-call(s32[1]{0:T(128)} %bitcast.37.y_ref, s32[1]{0:T(128)} %bitcast.38.x_ref, bf16[2,4,32,3584]{3,2,1,0:T(8,128)(2,1)} %get-tuple-element.299.xkeep_ref, ...), custom_call_target="tpu_custom_call" | custom-call | flops 19800000512 | bytes 10092552 | tf_op jit(solution)/shard_map/fold_one/pallas_call | solution.py:1153
  373.3 6.6 %collective-permute-done.30.xgot_ref = bf16[2,4,32,1152]{3,2,1,0:T(8,128)(2,1)} collective-permute-done((bf16[2,4,32,1152]{3,2,1,0:T(8,128)(2,1)}, bf16[2,4,32,1152]{3,2,1,0:T(8,128)(2,1)}, u32[]{:S(2)}, u32[]{:S(2)}) %collective-permute-start.30) | collective-permute-done | bytes 589856 | tf_op jit(solution)/shard_map/ppermute | solution.py:96
  405.4 13.5 %collective-permute-done.32.got_ref = bf16[2,352,512]{2,1,0:T(8,128)(2,1)S(1)} collective-permute-done((bf16[2,352,512]{2,1,0:T(8,128)(2,1)}, bf16[2,352,512]{2,1,0:T(8,128)(2,1)S(1)}, u32[]{:S(2)}, u32[]{:S(2)}) %collective-permute-start.32) | collective-permute-done | bytes 720928 | tf_op jit(solution)/shard_map/ppermute | solution.py:96
  434.3 8.9 %collective-permute-done.36.sum_ref = bf16[352,512]{1,0:T(8,128)(2,1)S(1)} collective-permute-done((bf16[352,512]{1,0:T(8,128)(2,1)}, bf16[352,512]{1,0:T(8,128)(2,1)S(1)}, u32[]{:S(2)}, u32[]{:S(2)}) %collective-permute-start.36) | collective-permute-done | bytes 360480 | tf_op jit(solution)/shard_map/ppermute | solution.py:96
  (267 shorter events, 165.0 us)
Async XLA Ops:
  7.3 188.4 %all-gather.3.cloned.1.call-start = ((), (), s32[]{:S(2)}) async-start(), calls=%async_computation.3 | async-start | bytes 20545536 | tf_op jit(solution)/shard_map/all_gather | solution.py:1230
  9.9 24.5 %collective-permute-start.3 = (f32[512]{0:T(512)S(1)}, f32[512]{0:T(512)S(1)}, u32[]{:S(2)}, u32[]{:S(2)}) collective-permute-start(f32[512]{0:T(512)S(1)} %pad_convert_fusion.1), channel_id=1, source_target_pairs={{0,2},{1,3},{2,0},{3,1},{4,6},{5,7},{6,4},{7,5},{8,10},{9,11},{10,... | collective-permute-start | bytes 6152 | tf_op jit(solution)/shard_map/ppermute | solution.py:96
  12.9 21.4 %collective-permute-start.2 = (f32[512]{0:T(512)S(1)}, f32[512]{0:T(512)S(1)}, u32[]{:S(2)}, u32[]{:S(2)}) collective-permute-start(f32[512]{0:T(512)S(1)} %pad_convert_fusion.1), channel_id=1, source_target_pairs={{0,4},{1,5},{2,6},{3,7},{4,0},{5,1},{6,2},{7,3},{8,12},{9,13},{10,... | collective-permute-start | bytes 6152 | tf_op jit(solution)/shard_map/ppermute | solution.py:96
  15.5 82.2 %collective-permute-start = (bf16[16,1024]{1,0:T(8,128)(2,1)S(1)}, bf16[16,1024]{1,0:T(8,128)(2,1)S(1)}, u32[]{:S(2)}, u32[]{:S(2)}) collective-permute-start(bf16[16,1024]{1,0:T(8,128)(2,1)S(1)} %slice.117), channel_id=1, source_target_pairs={{0,1},{1,2},{2,3},{3,4},{4,5},{5,6},{6,7},{8,9},{9,10},{10,11},{11... | collective-permute-start | bytes 98312 | tf_op jit(solution)/shard_map/ppermute | solution.py:186
  21.0 33.6 %all-to-all-start = ((bf16[4,32,2688]{2,1,0:T(8,128)(2,1)}), bf16[4,32,2688]{2,1,0:T(8,128)(2,1)S(1)}, u32[]{:S(2)}, u32[]{:S(2)}) async-start(bf16[4,32,2688]{2,1,0:T(8,128)(2,1)} %broadcast_in_dim.70), calls=%async_computation | async-start | bytes 1376256 | tf_op jit(solution)/shard_map/all_to_all | solution.py:176
  34.4 24.6 %collective-permute-start.4 = (f32[4,512]{1,0:T(4,128)S(1)}, f32[4,512]{1,0:T(4,128)S(1)}, u32[]{:S(2)}, u32[]{:S(2)}) collective-permute-start(f32[4,512]{1,0:T(4,128)S(1)} %pad_maximum_fusion.11), channel_id=1, source_target_pairs={{0,1},{1,0},{2,3},{3,2},{4,5},{5,4},{6,7},{7,6},{8,9},{9,8},{10,11... | collective-permute-start | bytes 24584 | tf_op jit(solution)/shard_map/ppermute | solution.py:96
  123.4 26.8 %collective-permute-start.13 = (bf16[1552,128]{1,0:T(8,128)(2,1)S(1)}, bf16[1552,128]{1,0:T(8,128)(2,1)S(1)}, u32[]{:S(2)}, u32[]{:S(2)}) collective-permute-start(bf16[1552,128]{1,0:T(8,128)(2,1)S(1)} %pad_maximum_fusion.6), channel_id=1, source_target_pairs={{0,1},{1,2},{2,3},{3,4},{4,5},{5,6},{6,7},{8,9},{9,10},{10,11},{11... | collective-permute-start | bytes 1191944 | tf_op jit(solution)/shard_map/ppermute | solution.py:186
  127.7 55.3 %all-to-all-start.1 = ((bf16[8,256,256]{2,1,0:T(8,128)(2,1)}), bf16[8,256,256]{2,1,0:T(8,128)(2,1)}, u32[]{:S(2)}, u32[]{:S(2)}) async-start(bf16[8,256,256]{2,1,0:T(8,128)(2,1)} %broadcast_in_dim.75), calls=%async_computation.1 | async-start | bytes 2097152 | tf_op jit(solution)/shard_map/all_to_all | solution.py:176
  151.0 42.2 %collective-permute-start.15 = (bf16[1552,128]{1,0:T(8,128)(2,1)S(1)}, bf16[1552,128]{1,0:T(8,128)(2,1)}, u32[]{:S(2)}, u32[]{:S(2)}) collective-permute-start(bf16[1552,128]{1,0:T(8,128)(2,1)S(1)} %fusion.4), channel_id=1, source_target_pairs={{0,2},{1,3},{2,4},{3,5},{4,6},{5,7},{8,10},{9,11},{10,12},{11,13},... | collective-permute-start | bytes 1191944 | tf_op jit(solution)/shard_map/ppermute | solution.py:186
  231.0 22.8 %collective-permute-start.16 = (bf16[256,10752]{1,0:T(8,128)(2,1)}, bf16[256,10752]{1,0:T(8,128)(2,1)}, u32[]{:S(2)}, u32[]{:S(2)}) collective-permute-start(bf16[256,10752]{1,0:T(8,128)(2,1)} %get-tuple-element.260.own_ref), channel_id=1, source_target_pairs={{0,8},{1,9},{2,10},{3,11},{4,12},{5,13},{6,14},{7,15},{8,0},{9,1},... | collective-permute-start | bytes 16515080 | tf_op jit(solution)/shard_map/ppermute | solution.py:96
  252.4 60.9 %collective-permute-start.19 = (bf16[1552,128]{1,0:T(8,128)(2,1)}, bf16[1552,128]{1,0:T(8,128)(2,1)}, u32[]{:S(2)}, u32[]{:S(2)}) collective-permute-start(bf16[1552,128]{1,0:T(8,128)(2,1)} %fusion.5), channel_id=1, source_target_pairs={{2,0},{3,1},{4,2},{5,3},{6,4},{7,5},{10,8},{11,9},{12,10},{13,11},... | collective-permute-start | bytes 1191944 | tf_op jit(solution)/shard_map/ppermute | solution.py:186
  261.7 54.0 %collective-permute-start.20 = (bf16[2,4,32,2048]{3,2,1,0:T(8,128)(2,1)}, bf16[2,4,32,2048]{3,2,1,0:T(8,128)(2,1)}, u32[]{:S(2)}, u32[]{:S(2)}) collective-permute-start(bf16[2,4,32,2048]{3,2,1,0:T(8,128)(2,1)} %get-tuple-element.245), channel_id=1, source_target_pairs={{0,1},{1,0},{2,3},{3,2},{4,5},{5,4},{6,7},{7,6},{8,9},{9,8},{10,11... | collective-permute-start | bytes 3145736 | tf_op jit(solution)/shard_map/ppermute | solution.py:96
  269.8 45.9 %collective-permute-start.21 = (bf16[8,64,1024]{2,1,0:T(8,128)(2,1)}, bf16[8,64,1024]{2,1,0:T(8,128)(2,1)}, u32[]{:S(2)}, u32[]{:S(2)}) collective-permute-start(bf16[8,64,1024]{2,1,0:T(8,128)(2,1)} %get-tuple-element.246), channel_id=1, source_target_pairs={{0,16},{1,17},{2,18},{3,19},{4,20},{5,21},{6,22},{7,23},{8,24},{9,... | collective-permute-start | bytes 3145736 | tf_op jit(solution)/shard_map/ppermute | solution.py:96
  287.0 46.7 %all-to-all-start.2 = ((bf16[8,256,256]{2,1,0:T(8,128)(2,1)}), bf16[8,256,256]{2,1,0:T(8,128)(2,1)}, u32[]{:S(2)}, u32[]{:S(2)}) async-start(bf16[8,256,256]{2,1,0:T(8,128)(2,1)} %get-tuple-element.256), calls=%async_computation.2 | async-start | bytes 2097152 | tf_op jit(solution)/shard_map/all_to_all | solution.py:176
  310.5 44.2 %collective-permute-start.23 = (bf16[8,64,1024]{2,1,0:T(8,128)(2,1)}, bf16[8,64,1024]{2,1,0:T(8,128)(2,1)}, u32[]{:S(2)}, u32[]{:S(2)}) collective-permute-start(bf16[8,64,1024]{2,1,0:T(8,128)(2,1)} %get-tuple-element.263), channel_id=1, source_target_pairs={{0,16},{1,17},{2,18},{3,19},{4,20},{5,21},{6,22},{7,23},{8,24},{9,... | collective-permute-start | bytes 3145736 | tf_op jit(solution)/shard_map/ppermute | solution.py:96
  311.3 44.7 %collective-permute-start.22 = (bf16[2,4,32,3584]{3,2,1,0:T(8,128)(2,1)}, bf16[2,4,32,3584]{3,2,1,0:T(8,128)(2,1)}, u32[]{:S(2)}, u32[]{:S(2)}) collective-permute-start(bf16[2,4,32,3584]{3,2,1,0:T(8,128)(2,1)} %get-tuple-element.262), channel_id=1, source_target_pairs={{0,1},{1,0},{2,3},{3,2},{4,5},{5,4},{6,7},{7,6},{8,9},{9,8},{10,11... | collective-permute-start | bytes 5505032 | tf_op jit(solution)/shard_map/ppermute | solution.py:96
  319.9 43.2 %collective-permute-start.27 = (bf16[4,32,2048]{2,1,0:T(8,128)(2,1)}, bf16[4,32,2048]{2,1,0:T(8,128)(2,1)}, u32[]{:S(2)}, u32[]{:S(2)}) collective-permute-start(bf16[4,32,2048]{2,1,0:T(8,128)(2,1)} %get-tuple-element.271), channel_id=1, source_target_pairs={{0,16},{1,17},{2,18},{3,19},{4,20},{5,21},{6,22},{7,23},{8,24},{9,... | collective-permute-start | bytes 1572872 | tf_op jit(solution)/shard_map/ppermute | solution.py:96
  321.1 46.2 %collective-permute-start.28 = (bf16[4,64,1024]{2,1,0:T(8,128)(2,1)}, bf16[4,64,1024]{2,1,0:T(8,128)(2,1)}, u32[]{:S(2)}, u32[]{:S(2)}) collective-permute-start(bf16[4,64,1024]{2,1,0:T(8,128)(2,1)} %get-tuple-element.272), channel_id=1, source_target_pairs={{0,1},{1,0},{2,3},{3,2},{4,5},{5,4},{6,7},{7,6},{8,9},{9,8},{10,11... | collective-permute-start | bytes 1572872 | tf_op jit(solution)/shard_map/ppermute | solution.py:96
  352.6 27.3 %collective-permute-start.30 = (bf16[2,4,32,1152]{3,2,1,0:T(8,128)(2,1)}, bf16[2,4,32,1152]{3,2,1,0:T(8,128)(2,1)}, u32[]{:S(2)}, u32[]{:S(2)}) collective-permute-start(bf16[2,4,32,1152]{3,2,1,0:T(8,128)(2,1)} %get-tuple-element.305), channel_id=1, source_target_pairs={{0,1},{1,0},{2,3},{3,2},{4,5},{5,4},{6,7},{7,6},{8,9},{9,8},{10,11... | collective-permute-start | bytes 1769480 | tf_op jit(solution)/shard_map/ppermute | solution.py:96
  354.6 25.3 %collective-permute-start.31 = (bf16[8,32,1536]{2,1,0:T(8,128)(2,1)}, bf16[8,32,1536]{2,1,0:T(8,128)(2,1)S(1)}, u32[]{:S(2)}, u32[]{:S(2)}) collective-permute-start(bf16[8,32,1536]{2,1,0:T(8,128)(2,1)} %get-tuple-element.306), channel_id=1, source_target_pairs={{0,16},{1,17},{2,18},{3,19},{4,20},{5,21},{6,22},{7,23},{8,24},{9,... | collective-permute-start | bytes 2359304 | tf_op jit(solution)/shard_map/ppermute | solution.py:96
  361.2 30.7 %collective-permute-start.26 = (bf16[4,64,1024]{2,1,0:T(8,128)(2,1)}, bf16[4,64,1024]{2,1,0:T(8,128)(2,1)}, u32[]{:S(2)}, u32[]{:S(2)}) collective-permute-start(bf16[4,64,1024]{2,1,0:T(8,128)(2,1)} %get-tuple-element.312), channel_id=1, source_target_pairs={{0,1},{1,0},{2,3},{3,2},{4,5},{5,4},{6,7},{7,6},{8,9},{9,8},{10,11... | collective-permute-start | bytes 1572872 | tf_op jit(solution)/shard_map/ppermute | solution.py:96
  363.1 31.7 %collective-permute-start.25 = (bf16[4,32,3584]{2,1,0:T(8,128)(2,1)}, bf16[4,32,3584]{2,1,0:T(8,128)(2,1)S(1)}, u32[]{:S(2)}, u32[]{:S(2)}) collective-permute-start(bf16[4,32,3584]{2,1,0:T(8,128)(2,1)} %get-tuple-element.311), channel_id=1, source_target_pairs={{0,16},{1,17},{2,18},{3,19},{4,20},{5,21},{6,22},{7,23},{8,24},{9,... | collective-permute-start | bytes 2752520 | tf_op jit(solution)/shard_map/ppermute | solution.py:96
  389.5 35.2 %collective-permute-start.38 = (bf16[256,512]{1,0:T(8,128)(2,1)}, bf16[256,512]{1,0:T(8,128)(2,1)S(1)}, u32[]{:S(2)}, u32[]{:S(2)}) collective-permute-start(bf16[256,512]{1,0:T(8,128)(2,1)} %get-tuple-element.326), channel_id=1, source_target_pairs={{0,4},{1,5},{2,6},{3,7},{4,0},{5,1},{6,2},{7,3},{8,12},{9,13},{10,... | collective-permute-start | bytes 786440 | tf_op jit(solution)/shard_map/ppermute | solution.py:96
  404.5 24.1 %collective-permute-start.37 = (bf16[2,224,384]{2,1,0:T(8,128)(2,1)}, bf16[2,224,384]{2,1,0:T(8,128)(2,1)S(1)}, u32[]{:S(2)}, u32[]{:S(2)}) collective-permute-start(bf16[2,224,384]{2,1,0:T(8,128)(2,1)} %get-tuple-element.336), channel_id=1, source_target_pairs={{0,2},{1,3},{2,0},{3,1},{4,6},{5,7},{6,4},{7,5},{8,10},{9,11},{10,... | collective-permute-start | bytes 1032200 | tf_op jit(solution)/shard_map/ppermute | solution.py:96
  (57 other events, 635.2 us)
Sparse Core Ops, SparseCore 0:
  11.0 181.6 all-gather.2
